TPU v7x, 512 devices: a whole 4x8x8 slice. The times are simulated.
512 devices in a mesh: dp: 2 (over y_lo), ctx: 32 (over y_hi, x, core), tensor: 8 (over z).
Axes of the slice: x: 4, y: 8 (y_hi: 4, y_lo: 2; y = y_hi * 2 + y_lo), z: 8, core: 2. Of those that a mesh axis runs over, the one named last changes fastest.
Arguments:
- queries: bfloat16 [8192, 8192], P(('dp', 'ctx'), 'tensor'), parts along dimension 0, may hold values from -6 to 6
- keys: bfloat16 [8192, 1024], P(('dp', 'ctx'), 'tensor'), parts along dimension 0, may hold values from -6 to 6
- values: bfloat16 [8192, 1024], P(('dp', 'ctx'), 'tensor'), parts along dimension 0, may hold values from -6 to 6
- attn_out: bfloat16 [8192, 8192], P(('dp', 'ctx'), 'tensor'), parts along dimension 0, may hold values from -6 to 6
- grad_out: bfloat16 [8192, 8192], P(('dp', 'ctx'), 'tensor'), parts along dimension 0, may hold values from -6 to 6
- log_norm: float32 [64, 8192], P('tensor', ('dp', 'ctx')), parts along dimension 1, may hold values from 3 to 6
- doc_lengths: int32 [32], P('dp'), parts along dimension 0, may hold values from 1 to 1024, 4096 in all
- block_order: int32 [128], P('dp'), parts along dimension 0, may hold values from 0 to 63, each once
Outputs:
- grad_queries: bfloat16 [8192, 8192], P(('dp', 'ctx'), 'tensor'), parts along dimension 0
- key_gradient_rows: bfloat16 [8192, 1024], P(('dp', 'ctx'), 'tensor'), parts along dimension 0
- value_gradient_rows: bfloat16 [8192, 1024], P(('dp', 'ctx'), 'tensor'), parts along dimension 0
There are 2 independent parts, one for each index of `dp`. A program takes and returns all parts, laid end to end along the dimension named above; each array names one. Nothing has to cross between parts.
Inputs may be any that keep to these rules, and one draw needn't show every extreme that they name: `doc_lengths`: document lengths in sequence order; they sum to 4096 and the largest is exactly 1024. `block_order`: each of the 64 blocks of 64 positions appears once.
All inputs are finite; a program needn't handle non-finite values.
Results may differ from a plain program's by a relative error of at most 0.0049.
Values may be sent and summed in bfloat16 or wider, within the bound.
No kernel may reach another device: no remote copies, remote signals or barrier semaphores. Data moves between devices by JAX's collectives and lax.ppermute only.
A program may use at most 64 MiB of HBM per device.

v0:
```python
import math

import jax
import jax.numpy as jnp
from jax import lax
from jax.sharding import PartitionSpec as P

QUERY_HEADS = 64
KEY_VALUE_HEADS = 8
HEAD_SIZE = 128


def from_behind(block, axis, distance):
    devices = range(lax.axis_size(axis))
    route = [((i - distance) % len(devices), i) for i in devices]
    return lax.ppermute(block, axis, route)


def on_device(queries, keys, values, attn_out, grad_out, log_norm, doc_lengths, block_order):
    row_count, row_width = queries.shape
    kv_width = keys.shape[1]
    local_kv = kv_width // HEAD_SIZE
    query_group_width = QUERY_HEADS // KEY_VALUE_HEADS
    cycle_size = lax.axis_size("ctx")
    my_index = lax.axis_index("ctx")
    half_rows = row_count // 2
    doc_ends = jnp.cumsum(doc_lengths)
    local_rows = jnp.arange(row_count, dtype=jnp.int32)
    score_scale = 1.0 / math.sqrt(HEAD_SIZE)

    def positions(source):
        pair_blocks = lax.dynamic_slice_in_dim(block_order, source * 2, 2)
        starts = jnp.repeat(pair_blocks, half_rows, total_repeat_length=row_count) * half_rows
        position = starts + local_rows % half_rows
        doc_ids = jnp.sum((position[:, None] >= doc_ends[None, :]).astype(jnp.int32), axis=1)
        return (position, doc_ids)

    query_pos, query_doc = positions(my_index)
    query_heads = queries.reshape(row_count, local_kv, query_group_width, HEAD_SIZE)
    grad_heads = grad_out.reshape(row_count, local_kv, query_group_width, HEAD_SIZE)
    out_heads = attn_out.reshape(row_count, local_kv, query_group_width, HEAD_SIZE)
    out_dot = jnp.einsum(
        "rkgd,rkgd->kgr", grad_heads, out_heads, preferred_element_type=jnp.float32
    )
    log_norms = log_norm.reshape(local_kv, query_group_width, row_count)

    def full_terms(key_value, allowed):
        key_block = key_value[0].reshape(row_count, local_kv, HEAD_SIZE)
        value_block = key_value[1].reshape(row_count, local_kv, HEAD_SIZE)
        scores = (
            jnp.einsum("rkgd,ckd->kgrc", query_heads, key_block, preferred_element_type=jnp.float32)
            * score_scale
        )
        weights = jnp.where(allowed[None, None], jnp.exp(scores - log_norms[..., None]), 0.0)
        grad_weights = jnp.einsum(
            "rkgd,ckd->kgrc", grad_heads, value_block, preferred_element_type=jnp.float32
        )
        grad_scores = (weights * (grad_weights - out_dot[..., None]) * score_scale).astype(
            jnp.bfloat16
        )
        weights_bf = weights.astype(jnp.bfloat16)
        grad_query = jnp.einsum(
            "kgrc,ckd->rkgd", grad_scores, key_block, preferred_element_type=jnp.float32
        )
        grad_key = jnp.einsum(
            "kgrc,rkgd->ckd", grad_scores, query_heads, preferred_element_type=jnp.float32
        )
        grad_value = jnp.einsum(
            "kgrc,rkgd->ckd", weights_bf, grad_heads, preferred_element_type=jnp.float32
        )
        grad_pair = jnp.stack(
            [grad_key.reshape(row_count, kv_width), grad_value.reshape(row_count, kv_width)]
        )
        return (grad_query.reshape(row_count, row_width), grad_pair)

    def contribute(key_value, source):
        key_pos, key_doc = positions(source)
        allowed = (query_doc[:, None] == key_doc[None, :]) & (
            key_pos[None, :] <= query_pos[:, None]
        )
        return full_terms(key_value, allowed)

    initial = jnp.zeros((cycle_size, 2, row_count, kv_width), jnp.float32)

    def absorb(stored, partial_value, source):
        return lax.dynamic_update_index_in_dim(stored, partial_value, source, 0)

    def one_turn(step_index, loop_state):
        key_value, stored, grad_q = loop_state
        source = (my_index - step_index) % cycle_size
        part_q, partial_value = contribute(key_value, source)
        stored = absorb(stored, partial_value, source)
        key_value = from_behind(key_value, "ctx", 1)
        return (key_value, stored, grad_q + part_q)

    start_state = (
        jnp.stack([keys, values]),
        initial,
        jnp.zeros((row_count, row_width), jnp.float32),
    )
    key_value, stored, grad_q = lax.fori_loop(0, cycle_size - 1, one_turn, start_state)
    last_source = (my_index + 1) % cycle_size
    part_q, partial_value = contribute(key_value, last_source)
    stored = absorb(stored, partial_value, last_source)
    grad_q = grad_q + part_q
    received = lax.all_to_all(stored, "ctx", split_axis=0, concat_axis=0, tiled=True)
    summed = jnp.sum(received, axis=0)
    return (
        grad_q.astype(jnp.bfloat16),
        summed[0].astype(jnp.bfloat16),
        summed[1].astype(jnp.bfloat16),
    )


def solution(mesh):
    placed = (
        P(("dp", "ctx"), "tensor"),
        P(("dp", "ctx"), "tensor"),
        P(("dp", "ctx"), "tensor"),
        P(("dp", "ctx"), "tensor"),
        P(("dp", "ctx"), "tensor"),
        P("tensor", ("dp", "ctx")),
        P("dp"),
        P("dp"),
    )
    return jax.shard_map(
        on_device,
        mesh=mesh,
        in_specs=placed,
        out_specs=(
            P(("dp", "ctx"), "tensor"),
            P(("dp", "ctx"), "tensor"),
            P(("dp", "ctx"), "tensor"),
        ),
        check_vma=False,
    )
```

profile of v0, /device:TPU:1, one launch (start us, length us, event | category | flops | bytes accessed | tf_op | source)
XLA Modules:
  0.0 428.5 jit_solution(1497706124961121457)
XLA Ops:
  8.7 3.2 fusion.57
  12.1 2.5 broadcast_in_dim.107
  14.6 304.6 %while.25 = (s32[]{:T(128)}, bf16[2,128,128]{2,1,0:T(8,128)(2,1)S(1)}, f32[32,2,128,128]{3,2,1,0:T(8,128)}, f32[128,1024]{0,1:T(8,128)S(1)}, s32[128]{0:T(128)S(...) while((s32[]{:T(128)}, ...), condition=%wide.region_4.7_spmd.clone, body=%wide.region_2.0_spmd.clone.sunk | while | flops 169171984 | bytes 6434976 | solution.py:101
  14.6 4.6 %collective-permute-start = (bf16[2,128,128]{2,1,0:T(8,128)(2,1)S(1)}, bf16[2,128,128]{2,1,0:T(8,128)(2,1)S(1)}, u32[]{:S(2)}, u32[]{:S(2)}) collective-permute-start(bf16[2,128,128]{2,1,0:T(8,128)(2,1)S(1)} %copy.92), channel_id=1, source_target_pairs={{248,0},{0,8},{8,16},{16,24},{24,32},{32,40},{40,48},{48,56},{56,6... | collective-permute-start | bytes 196616 | tf_op jit(solution)/shard_map/while/body/eval_jaxpr/ppermute | solution.py:16
  24.3 1.9 collective-permute-start
  30.5 3.6 collective-permute-done
  34.1 1.9 collective-permute-start
  40.3 3.6 collective-permute-done
  43.9 1.9 collective-permute-start
  50.1 3.6 collective-permute-done
  53.7 1.9 collective-permute-start
  59.9 3.6 collective-permute-done
  63.5 1.9 collective-permute-start
  69.7 4.3 %collective-permute-done = bf16[2,128,128]{2,1,0:T(8,128)(2,1)S(1)} collective-permute-done((bf16[2,128,128]{2,1,0:T(8,128)(2,1)S(1)}, bf16[2,128,128]{2,1,0:T(8,128)(2,1)S(1)}, u32[]{:S(2)}, u32[]{:S(2)}) %collective-permute-start) | collective-permute-done | bytes 65568 | tf_op jit(solution)/shard_map/while/body/eval_jaxpr/ppermute | solution.py:16
  74.0 1.9 collective-permute-start
  80.2 3.6 collective-permute-done
  83.8 1.9 collective-permute-start
  90.0 3.6 collective-permute-done
  93.6 1.9 collective-permute-start
  99.8 3.6 collective-permute-done
  103.4 1.9 collective-permute-start
  109.6 3.6 collective-permute-done
  113.2 1.9 collective-permute-start
  119.4 3.6 collective-permute-done
  123.0 1.9 collective-permute-start
  129.2 3.6 collective-permute-done
  132.8 1.9 collective-permute-start
  139.0 3.9 collective-permute-done
  142.9 1.9 collective-permute-start
  149.1 3.6 collective-permute-done
  152.7 1.9 collective-permute-start
  158.9 3.6 collective-permute-done
  162.5 1.9 collective-permute-start
  168.7 3.6 collective-permute-done
  172.3 1.9 collective-permute-start
  178.5 3.6 collective-permute-done
  182.1 1.9 collective-permute-start
  188.2 3.6 collective-permute-done
  191.9 1.9 collective-permute-start
  198.1 3.6 collective-permute-done
  201.7 1.9 collective-permute-start
  207.9 3.6 collective-permute-done
  211.5 1.9 collective-permute-start
  217.7 3.6 collective-permute-done
  221.3 1.9 collective-permute-start
  227.4 3.6 collective-permute-done
  231.1 1.9 collective-permute-start
  237.2 3.6 collective-permute-done
  240.9 1.9 collective-permute-start
  247.1 3.6 collective-permute-done
  250.7 1.9 collective-permute-start
  256.8 3.6 collective-permute-done
  260.5 1.9 collective-permute-start
  266.6 3.6 collective-permute-done
  270.2 1.9 collective-permute-start
  276.4 3.6 collective-permute-done
  280.0 1.9 collective-permute-start
  286.2 3.6 collective-permute-done
  296.0 3.6 collective-permute-done
  305.8 3.6 collective-permute-done
  315.6 3.6 collective-permute-done
  320.9 11.6 %all-to-all-start = ((f32[32,2,128,128]{3,2,1,0:T(8,128)}), f32[32,2,128,128]{3,2,1,0:T(8,128)}, u32[]{:S(2)}, u32[]{:S(2)}) async-start(f32[32,2,128,128]{3,2,1,0:T(8,128)} %fusion.48), calls=%async_computation | async-start | bytes 8388608 | tf_op jit(solution)/shard_map/all_to_all | solution.py:106
  333.9 91.6 %all-to-all-done = f32[32,2,128,128]{3,2,1,0:T(8,128)} async-done(((f32[32,2,128,128]{3,2,1,0:T(8,128)}), f32[32,2,128,128]{3,2,1,0:T(8,128)}, u32[]{:S(2)}, u32[]{:S(2)}) %all-to-all-start) | async-done | bytes 4194336 | tf_op jit(solution)/shard_map/all_to_all | solution.py:106
  425.5 2.4 reduce_sum.47
  (444 shorter events, 147.9 us)
Async XLA Ops:
  0.6 14.0 %copy-start.3 = (pred[128]{0:T(512)(128)(4,1)S(1)}, pred[128]{0:T(512)(128)(4,1)}, u32[]{:S(2)}) copy-start(pred[128]{0:T(512)(128)(4,1)} %constant.365) | copy-start | bytes 388
  0.6 13.9 %copy-start.4 = (s32[64]{0:T(128)S(1)}, s32[64]{0:T(128)}, u32[]{:S(2)}) copy-start(s32[64]{0:T(128)} %param.27) | copy-start | bytes 772
  0.7 13.9 %copy-start.2 = (f32[8,128]{1,0:T(8,128)S(1)}, f32[8,128]{1,0:T(8,128)}, u32[]{:S(2)}) copy-start(f32[8,128]{1,0:T(8,128)} %param.25) | copy-start | bytes 12292
  14.6 304.6 %copy-start.1 = (bf16[128,1024]{1,0:T(8,128)(2,1)S(1)}, bf16[128,1024]{1,0:T(8,128)(2,1)}, u32[]{:S(2)}) copy-start(bf16[128,1024]{1,0:T(8,128)(2,1)} %param.20) | copy-start | bytes 786436
  14.6 304.9 %copy-start = (bf16[128,1024]{1,0:T(8,128)(2,1)S(1)}, bf16[128,1024]{1,0:T(8,128)(2,1)}, u32[]{:S(2)}) copy-start(bf16[128,1024]{1,0:T(8,128)(2,1)} %param.24) | copy-start | bytes 786436
  14.6 9.7 %collective-permute-start = (bf16[2,128,128]{2,1,0:T(8,128)(2,1)S(1)}, bf16[2,128,128]{2,1,0:T(8,128)(2,1)S(1)}, u32[]{:S(2)}, u32[]{:S(2)}) collective-permute-start(bf16[2,128,128]{2,1,0:T(8,128)(2,1)S(1)} %copy.92), channel_id=1, source_target_pairs={{248,0},{0,8},{8,16},{16,24},{24,32},{32,40},{40,48},{48,56},{56,6... | collective-permute-start | bytes 196616 | tf_op jit(solution)/shard_map/while/body/eval_jaxpr/ppermute | solution.py:16
  24.3 9.8 %collective-permute-start = (bf16[2,128,128]{2,1,0:T(8,128)(2,1)S(1)}, bf16[2,128,128]{2,1,0:T(8,128)(2,1)S(1)}, u32[]{:S(2)}, u32[]{:S(2)}) collective-permute-start(bf16[2,128,128]{2,1,0:T(8,128)(2,1)S(1)} %copy.92), channel_id=1, source_target_pairs={{248,0},{0,8},{8,16},{16,24},{24,32},{32,40},{40,48},{48,56},{56,6... | collective-permute-start | bytes 196616 | tf_op jit(solution)/shard_map/while/body/eval_jaxpr/ppermute | solution.py:16
  34.1 9.8 %collective-permute-start = (bf16[2,128,128]{2,1,0:T(8,128)(2,1)S(1)}, bf16[2,128,128]{2,1,0:T(8,128)(2,1)S(1)}, u32[]{:S(2)}, u32[]{:S(2)}) collective-permute-start(bf16[2,128,128]{2,1,0:T(8,128)(2,1)S(1)} %copy.92), channel_id=1, source_target_pairs={{248,0},{0,8},{8,16},{16,24},{24,32},{32,40},{40,48},{48,56},{56,6... | collective-permute-start | bytes 196616 | tf_op jit(solution)/shard_map/while/body/eval_jaxpr/ppermute | solution.py:16
  43.9 9.8 %collective-permute-start = (bf16[2,128,128]{2,1,0:T(8,128)(2,1)S(1)}, bf16[2,128,128]{2,1,0:T(8,128)(2,1)S(1)}, u32[]{:S(2)}, u32[]{:S(2)}) collective-permute-start(bf16[2,128,128]{2,1,0:T(8,128)(2,1)S(1)} %copy.92), channel_id=1, source_target_pairs={{248,0},{0,8},{8,16},{16,24},{24,32},{32,40},{40,48},{48,56},{56,6... | collective-permute-start | bytes 196616 | tf_op jit(solution)/shard_map/while/body/eval_jaxpr/ppermute | solution.py:16
  53.7 9.8 %collective-permute-start = (bf16[2,128,128]{2,1,0:T(8,128)(2,1)S(1)}, bf16[2,128,128]{2,1,0:T(8,128)(2,1)S(1)}, u32[]{:S(2)}, u32[]{:S(2)}) collective-permute-start(bf16[2,128,128]{2,1,0:T(8,128)(2,1)S(1)} %copy.92), channel_id=1, source_target_pairs={{248,0},{0,8},{8,16},{16,24},{24,32},{32,40},{40,48},{48,56},{56,6... | collective-permute-start | bytes 196616 | tf_op jit(solution)/shard_map/while/body/eval_jaxpr/ppermute | solution.py:16
  63.5 10.5 %collective-permute-start = (bf16[2,128,128]{2,1,0:T(8,128)(2,1)S(1)}, bf16[2,128,128]{2,1,0:T(8,128)(2,1)S(1)}, u32[]{:S(2)}, u32[]{:S(2)}) collective-permute-start(bf16[2,128,128]{2,1,0:T(8,128)(2,1)S(1)} %copy.92), channel_id=1, source_target_pairs={{248,0},{0,8},{8,16},{16,24},{24,32},{32,40},{40,48},{48,56},{56,6... | collective-permute-start | bytes 196616 | tf_op jit(solution)/shard_map/while/body/eval_jaxpr/ppermute | solution.py:16
  74.0 9.8 %collective-permute-start = (bf16[2,128,128]{2,1,0:T(8,128)(2,1)S(1)}, bf16[2,128,128]{2,1,0:T(8,128)(2,1)S(1)}, u32[]{:S(2)}, u32[]{:S(2)}) collective-permute-start(bf16[2,128,128]{2,1,0:T(8,128)(2,1)S(1)} %copy.92), channel_id=1, source_target_pairs={{248,0},{0,8},{8,16},{16,24},{24,32},{32,40},{40,48},{48,56},{56,6... | collective-permute-start | bytes 196616 | tf_op jit(solution)/shard_map/while/body/eval_jaxpr/ppermute | solution.py:16
  83.8 9.8 %collective-permute-start = (bf16[2,128,128]{2,1,0:T(8,128)(2,1)S(1)}, bf16[2,128,128]{2,1,0:T(8,128)(2,1)S(1)}, u32[]{:S(2)}, u32[]{:S(2)}) collective-permute-start(bf16[2,128,128]{2,1,0:T(8,128)(2,1)S(1)} %copy.92), channel_id=1, source_target_pairs={{248,0},{0,8},{8,16},{16,24},{24,32},{32,40},{40,48},{48,56},{56,6... | collective-permute-start | bytes 196616 | tf_op jit(solution)/shard_map/while/body/eval_jaxpr/ppermute | solution.py:16
  93.6 9.8 %collective-permute-start = (bf16[2,128,128]{2,1,0:T(8,128)(2,1)S(1)}, bf16[2,128,128]{2,1,0:T(8,128)(2,1)S(1)}, u32[]{:S(2)}, u32[]{:S(2)}) collective-permute-start(bf16[2,128,128]{2,1,0:T(8,128)(2,1)S(1)} %copy.92), channel_id=1, source_target_pairs={{248,0},{0,8},{8,16},{16,24},{24,32},{32,40},{40,48},{48,56},{56,6... | collective-permute-start | bytes 196616 | tf_op jit(solution)/shard_map/while/body/eval_jaxpr/ppermute | solution.py:16
  103.4 9.8 %collective-permute-start = (bf16[2,128,128]{2,1,0:T(8,128)(2,1)S(1)}, bf16[2,128,128]{2,1,0:T(8,128)(2,1)S(1)}, u32[]{:S(2)}, u32[]{:S(2)}) collective-permute-start(bf16[2,128,128]{2,1,0:T(8,128)(2,1)S(1)} %copy.92), channel_id=1, source_target_pairs={{248,0},{0,8},{8,16},{16,24},{24,32},{32,40},{40,48},{48,56},{56,6... | collective-permute-start | bytes 196616 | tf_op jit(solution)/shard_map/while/body/eval_jaxpr/ppermute | solution.py:16
  113.2 9.8 %collective-permute-start = (bf16[2,128,128]{2,1,0:T(8,128)(2,1)S(1)}, bf16[2,128,128]{2,1,0:T(8,128)(2,1)S(1)}, u32[]{:S(2)}, u32[]{:S(2)}) collective-permute-start(bf16[2,128,128]{2,1,0:T(8,128)(2,1)S(1)} %copy.92), channel_id=1, source_target_pairs={{248,0},{0,8},{8,16},{16,24},{24,32},{32,40},{40,48},{48,56},{56,6... | collective-permute-start | bytes 196616 | tf_op jit(solution)/shard_map/while/body/eval_jaxpr/ppermute | solution.py:16
  123.0 9.8 %collective-permute-start = (bf16[2,128,128]{2,1,0:T(8,128)(2,1)S(1)}, bf16[2,128,128]{2,1,0:T(8,128)(2,1)S(1)}, u32[]{:S(2)}, u32[]{:S(2)}) collective-permute-start(bf16[2,128,128]{2,1,0:T(8,128)(2,1)S(1)} %copy.92), channel_id=1, source_target_pairs={{248,0},{0,8},{8,16},{16,24},{24,32},{32,40},{40,48},{48,56},{56,6... | collective-permute-start | bytes 196616 | tf_op jit(solution)/shard_map/while/body/eval_jaxpr/ppermute | solution.py:16
  132.8 10.1 %collective-permute-start = (bf16[2,128,128]{2,1,0:T(8,128)(2,1)S(1)}, bf16[2,128,128]{2,1,0:T(8,128)(2,1)S(1)}, u32[]{:S(2)}, u32[]{:S(2)}) collective-permute-start(bf16[2,128,128]{2,1,0:T(8,128)(2,1)S(1)} %copy.92), channel_id=1, source_target_pairs={{248,0},{0,8},{8,16},{16,24},{24,32},{32,40},{40,48},{48,56},{56,6... | collective-permute-start | bytes 196616 | tf_op jit(solution)/shard_map/while/body/eval_jaxpr/ppermute | solution.py:16
  142.9 9.8 %collective-permute-start = (bf16[2,128,128]{2,1,0:T(8,128)(2,1)S(1)}, bf16[2,128,128]{2,1,0:T(8,128)(2,1)S(1)}, u32[]{:S(2)}, u32[]{:S(2)}) collective-permute-start(bf16[2,128,128]{2,1,0:T(8,128)(2,1)S(1)} %copy.92), channel_id=1, source_target_pairs={{248,0},{0,8},{8,16},{16,24},{24,32},{32,40},{40,48},{48,56},{56,6... | collective-permute-start | bytes 196616 | tf_op jit(solution)/shard_map/while/body/eval_jaxpr/ppermute | solution.py:16
  152.7 9.8 %collective-permute-start = (bf16[2,128,128]{2,1,0:T(8,128)(2,1)S(1)}, bf16[2,128,128]{2,1,0:T(8,128)(2,1)S(1)}, u32[]{:S(2)}, u32[]{:S(2)}) collective-permute-start(bf16[2,128,128]{2,1,0:T(8,128)(2,1)S(1)} %copy.92), channel_id=1, source_target_pairs={{248,0},{0,8},{8,16},{16,24},{24,32},{32,40},{40,48},{48,56},{56,6... | collective-permute-start | bytes 196616 | tf_op jit(solution)/shard_map/while/body/eval_jaxpr/ppermute | solution.py:16
  162.5 9.8 %collective-permute-start = (bf16[2,128,128]{2,1,0:T(8,128)(2,1)S(1)}, bf16[2,128,128]{2,1,0:T(8,128)(2,1)S(1)}, u32[]{:S(2)}, u32[]{:S(2)}) collective-permute-start(bf16[2,128,128]{2,1,0:T(8,128)(2,1)S(1)} %copy.92), channel_id=1, source_target_pairs={{248,0},{0,8},{8,16},{16,24},{24,32},{32,40},{40,48},{48,56},{56,6... | collective-permute-start | bytes 196616 | tf_op jit(solution)/shard_map/while/body/eval_jaxpr/ppermute | solution.py:16
  172.3 9.8 %collective-permute-start = (bf16[2,128,128]{2,1,0:T(8,128)(2,1)S(1)}, bf16[2,128,128]{2,1,0:T(8,128)(2,1)S(1)}, u32[]{:S(2)}, u32[]{:S(2)}) collective-permute-start(bf16[2,128,128]{2,1,0:T(8,128)(2,1)S(1)} %copy.92), channel_id=1, source_target_pairs={{248,0},{0,8},{8,16},{16,24},{24,32},{32,40},{40,48},{48,56},{56,6... | collective-permute-start | bytes 196616 | tf_op jit(solution)/shard_map/while/body/eval_jaxpr/ppermute | solution.py:16
  182.1 9.8 %collective-permute-start = (bf16[2,128,128]{2,1,0:T(8,128)(2,1)S(1)}, bf16[2,128,128]{2,1,0:T(8,128)(2,1)S(1)}, u32[]{:S(2)}, u32[]{:S(2)}) collective-permute-start(bf16[2,128,128]{2,1,0:T(8,128)(2,1)S(1)} %copy.92), channel_id=1, source_target_pairs={{248,0},{0,8},{8,16},{16,24},{24,32},{32,40},{40,48},{48,56},{56,6... | collective-permute-start | bytes 196616 | tf_op jit(solution)/shard_map/while/body/eval_jaxpr/ppermute | solution.py:16
  191.9 9.8 %collective-permute-start = (bf16[2,128,128]{2,1,0:T(8,128)(2,1)S(1)}, bf16[2,128,128]{2,1,0:T(8,128)(2,1)S(1)}, u32[]{:S(2)}, u32[]{:S(2)}) collective-permute-start(bf16[2,128,128]{2,1,0:T(8,128)(2,1)S(1)} %copy.92), channel_id=1, source_target_pairs={{248,0},{0,8},{8,16},{16,24},{24,32},{32,40},{40,48},{48,56},{56,6... | collective-permute-start | bytes 196616 | tf_op jit(solution)/shard_map/while/body/eval_jaxpr/ppermute | solution.py:16
  201.7 9.8 %collective-permute-start = (bf16[2,128,128]{2,1,0:T(8,128)(2,1)S(1)}, bf16[2,128,128]{2,1,0:T(8,128)(2,1)S(1)}, u32[]{:S(2)}, u32[]{:S(2)}) collective-permute-start(bf16[2,128,128]{2,1,0:T(8,128)(2,1)S(1)} %copy.92), channel_id=1, source_target_pairs={{248,0},{0,8},{8,16},{16,24},{24,32},{32,40},{40,48},{48,56},{56,6... | collective-permute-start | bytes 196616 | tf_op jit(solution)/shard_map/while/body/eval_jaxpr/ppermute | solution.py:16
  211.5 9.8 %collective-permute-start = (bf16[2,128,128]{2,1,0:T(8,128)(2,1)S(1)}, bf16[2,128,128]{2,1,0:T(8,128)(2,1)S(1)}, u32[]{:S(2)}, u32[]{:S(2)}) collective-permute-start(bf16[2,128,128]{2,1,0:T(8,128)(2,1)S(1)} %copy.92), channel_id=1, source_target_pairs={{248,0},{0,8},{8,16},{16,24},{24,32},{32,40},{40,48},{48,56},{56,6... | collective-permute-start | bytes 196616 | tf_op jit(solution)/shard_map/while/body/eval_jaxpr/ppermute | solution.py:16
  221.3 9.8 %collective-permute-start = (bf16[2,128,128]{2,1,0:T(8,128)(2,1)S(1)}, bf16[2,128,128]{2,1,0:T(8,128)(2,1)S(1)}, u32[]{:S(2)}, u32[]{:S(2)}) collective-permute-start(bf16[2,128,128]{2,1,0:T(8,128)(2,1)S(1)} %copy.92), channel_id=1, source_target_pairs={{248,0},{0,8},{8,16},{16,24},{24,32},{32,40},{40,48},{48,56},{56,6... | collective-permute-start | bytes 196616 | tf_op jit(solution)/shard_map/while/body/eval_jaxpr/ppermute | solution.py:16
  231.1 9.8 %collective-permute-start = (bf16[2,128,128]{2,1,0:T(8,128)(2,1)S(1)}, bf16[2,128,128]{2,1,0:T(8,128)(2,1)S(1)}, u32[]{:S(2)}, u32[]{:S(2)}) collective-permute-start(bf16[2,128,128]{2,1,0:T(8,128)(2,1)S(1)} %copy.92), channel_id=1, source_target_pairs={{248,0},{0,8},{8,16},{16,24},{24,32},{32,40},{40,48},{48,56},{56,6... | collective-permute-start | bytes 196616 | tf_op jit(solution)/shard_map/while/body/eval_jaxpr/ppermute | solution.py:16
  240.9 9.8 %collective-permute-start = (bf16[2,128,128]{2,1,0:T(8,128)(2,1)S(1)}, bf16[2,128,128]{2,1,0:T(8,128)(2,1)S(1)}, u32[]{:S(2)}, u32[]{:S(2)}) collective-permute-start(bf16[2,128,128]{2,1,0:T(8,128)(2,1)S(1)} %copy.92), channel_id=1, source_target_pairs={{248,0},{0,8},{8,16},{16,24},{24,32},{32,40},{40,48},{48,56},{56,6... | collective-permute-start | bytes 196616 | tf_op jit(solution)/shard_map/while/body/eval_jaxpr/ppermute | solution.py:16
  250.7 9.8 %collective-permute-start = (bf16[2,128,128]{2,1,0:T(8,128)(2,1)S(1)}, bf16[2,128,128]{2,1,0:T(8,128)(2,1)S(1)}, u32[]{:S(2)}, u32[]{:S(2)}) collective-permute-start(bf16[2,128,128]{2,1,0:T(8,128)(2,1)S(1)} %copy.92), channel_id=1, source_target_pairs={{248,0},{0,8},{8,16},{16,24},{24,32},{32,40},{40,48},{48,56},{56,6... | collective-permute-start | bytes 196616 | tf_op jit(solution)/shard_map/while/body/eval_jaxpr/ppermute | solution.py:16
  260.5 9.8 %collective-permute-start = (bf16[2,128,128]{2,1,0:T(8,128)(2,1)S(1)}, bf16[2,128,128]{2,1,0:T(8,128)(2,1)S(1)}, u32[]{:S(2)}, u32[]{:S(2)}) collective-permute-start(bf16[2,128,128]{2,1,0:T(8,128)(2,1)S(1)} %copy.92), channel_id=1, source_target_pairs={{248,0},{0,8},{8,16},{16,24},{24,32},{32,40},{40,48},{48,56},{56,6... | collective-permute-start | bytes 196616 | tf_op jit(solution)/shard_map/while/body/eval_jaxpr/ppermute | solution.py:16
  270.2 9.8 %collective-permute-start = (bf16[2,128,128]{2,1,0:T(8,128)(2,1)S(1)}, bf16[2,128,128]{2,1,0:T(8,128)(2,1)S(1)}, u32[]{:S(2)}, u32[]{:S(2)}) collective-permute-start(bf16[2,128,128]{2,1,0:T(8,128)(2,1)S(1)} %copy.92), channel_id=1, source_target_pairs={{248,0},{0,8},{8,16},{16,24},{24,32},{32,40},{40,48},{48,56},{56,6... | collective-permute-start | bytes 196616 | tf_op jit(solution)/shard_map/while/body/eval_jaxpr/ppermute | solution.py:16
  280.0 9.8 %collective-permute-start = (bf16[2,128,128]{2,1,0:T(8,128)(2,1)S(1)}, bf16[2,128,128]{2,1,0:T(8,128)(2,1)S(1)}, u32[]{:S(2)}, u32[]{:S(2)}) collective-permute-start(bf16[2,128,128]{2,1,0:T(8,128)(2,1)S(1)} %copy.92), channel_id=1, source_target_pairs={{248,0},{0,8},{8,16},{16,24},{24,32},{32,40},{40,48},{48,56},{56,6... | collective-permute-start | bytes 196616 | tf_op jit(solution)/shard_map/while/body/eval_jaxpr/ppermute | solution.py:16
  289.8 9.8 %collective-permute-start = (bf16[2,128,128]{2,1,0:T(8,128)(2,1)S(1)}, bf16[2,128,128]{2,1,0:T(8,128)(2,1)S(1)}, u32[]{:S(2)}, u32[]{:S(2)}) collective-permute-start(bf16[2,128,128]{2,1,0:T(8,128)(2,1)S(1)} %copy.92), channel_id=1, source_target_pairs={{248,0},{0,8},{8,16},{16,24},{24,32},{32,40},{40,48},{48,56},{56,6... | collective-permute-start | bytes 196616 | tf_op jit(solution)/shard_map/while/body/eval_jaxpr/ppermute | solution.py:16
  299.6 9.8 %collective-permute-start = (bf16[2,128,128]{2,1,0:T(8,128)(2,1)S(1)}, bf16[2,128,128]{2,1,0:T(8,128)(2,1)S(1)}, u32[]{:S(2)}, u32[]{:S(2)}) collective-permute-start(bf16[2,128,128]{2,1,0:T(8,128)(2,1)S(1)} %copy.92), channel_id=1, source_target_pairs={{248,0},{0,8},{8,16},{16,24},{24,32},{32,40},{40,48},{48,56},{56,6... | collective-permute-start | bytes 196616 | tf_op jit(solution)/shard_map/while/body/eval_jaxpr/ppermute | solution.py:16
  309.4 9.8 %collective-permute-start = (bf16[2,128,128]{2,1,0:T(8,128)(2,1)S(1)}, bf16[2,128,128]{2,1,0:T(8,128)(2,1)S(1)}, u32[]{:S(2)}, u32[]{:S(2)}) collective-permute-start(bf16[2,128,128]{2,1,0:T(8,128)(2,1)S(1)} %copy.92), channel_id=1, source_target_pairs={{248,0},{0,8},{8,16},{16,24},{24,32},{32,40},{40,48},{48,56},{56,6... | collective-permute-start | bytes 196616 | tf_op jit(solution)/shard_map/while/body/eval_jaxpr/ppermute | solution.py:16
  320.9 104.6 %all-to-all-start = ((f32[32,2,128,128]{3,2,1,0:T(8,128)}), f32[32,2,128,128]{3,2,1,0:T(8,128)}, u32[]{:S(2)}, u32[]{:S(2)}) async-start(f32[32,2,128,128]{3,2,1,0:T(8,128)} %fusion.48), calls=%async_computation | async-start | bytes 8388608 | tf_op jit(solution)/shard_map/all_to_all | solution.py:106
where the time goes:
time: 430 us; the launch traced here: 428 us
  waiting for transfers between devices  201 us (47%)
  other arithmetic  79.6 us (19%)
  starting transfers between devices  73.5 us (17%)
  matrix products  38.5 us (9%)
  local copies, waits for them, and re-layouts  31.3 us (7%)
    ppermute x31, waiting for transfers between devices, from_behind(): return lax.ppermute(block, axis, route)  110 us
    all_to_all x1, waiting for transfers between devices, on_device(): lax.all_to_all(stored, 'ctx', split_axis=0, concat_axis=0, tiled=True)  91.6 us
    ppermute x31, starting transfers between devices, from_behind(): return lax.ppermute(block, axis, route)  61.9 us
    add x32, other arithmetic, positions(): position = starts + local_rows % half_rows  44.7 us
    dynamic_update_slice x32, other arithmetic, absorb(): return lax.dynamic_update_index_in_dim(stored, partial_value, source, 0)  21.2 us
    gather x32, local copies, waits for them, and re-layouts, positions(): jnp.repeat(pair_blocks, half_rows, total_repeat_length=row_count)  19.1 us
    all_to_all x1, starting transfers between devices, on_device(): lax.all_to_all(stored, 'ctx', split_axis=0, concat_axis=0, tiled=True)  11.6 us
  transfers between devices with their start and end apart: 32, of which 32 were waited for; matrix products, arithmetic and copies ran while one was open for 31% of the time, Pallas kernels for 0%

commit v1 on v0

v1 whole, which is shorter than its diff:
```python
import math

import jax
import jax.numpy as jnp
from jax import lax
from jax.experimental import pallas as pl
from jax.experimental.pallas import tpu as pltpu
from jax.sharding import Mesh
from jax.sharding import PartitionSpec as P

HEADS = 8
HEAD = 128
BLOCK = 64
LANES = HEADS * BLOCK
SCALE = 1.0 / math.sqrt(HEAD)
LOG2E = math.log2(math.e)
CTX = ("yh", "x", "core")
CHIPS = ("yh", "x")
NT = (((1,), (1,)), ((), ()))
TN = (((0,), (0,)), ((), ()))


def attention_terms(
    from_ref, upto_ref, held_ref, place_ref,
    q_ref, q2_ref, do_ref, do2_ref, rows_f_ref, rows_i_ref, kv_ref,
    dq_ref, dq2_ref, dkv_ref, acc_ref, dqt_ref,
):
    acc_ref[...] = jnp.zeros_like(acc_ref)
    heads = range(HEADS)
    for b in range(4):
        rows = pl.ds((b % 2) * BLOCK, BLOCK)
        qs, dos, out = (q_ref, do_ref, dq_ref) if b < 2 else (q2_ref, do2_ref, dq2_ref)
        q = jnp.concatenate([qs[rows, h * HEAD : (h + 1) * HEAD] for h in heads], 0)
        do = jnp.concatenate([dos[rows, h * HEAD : (h + 1) * HEAD] for h in heads], 0)
        norm = rows_f_ref[2 * b : 2 * b + 1, :]
        dot = rows_f_ref[2 * b + 1 : 2 * b + 2, :]
        first = rows_i_ref[2 * b : 2 * b + 1, :]
        own = rows_i_ref[2 * b + 1 : 2 * b + 2, :]
        start, stop = from_ref[b], upto_ref[b]
        dqt_ref[...] = jnp.zeros_like(dqt_ref)

        def step(c, carry, q=q, do=do, norm=norm, dot=dot, first=first, own=own, start=start):
            j = start + 2 * c
            a0 = pl.multiple_of(place_ref[j], BLOCK)
            a1 = pl.multiple_of(place_ref[j + 1], BLOCK)
            k = jnp.concatenate([kv_ref[pl.ds(a0, BLOCK), :], kv_ref[pl.ds(a1, BLOCK), :]], 0)
            v = jnp.concatenate(
                [kv_ref[pl.ds(a0 + 128, BLOCK), :], kv_ref[pl.ds(a1 + 128, BLOCK), :]], 0
            )
            s = lax.dot_general(k, q, NT, preferred_element_type=jnp.float32)
            dp = lax.dot_general(v, do, NT, preferred_element_type=jnp.float32)
            lane = lax.broadcasted_iota(jnp.int32, (BLOCK, LANES), 0)
            pos = jnp.concatenate([lane + held_ref[j] * BLOCK, lane + held_ref[j + 1] * BLOCK], 0)
            ok = (pos >= first) & (pos <= own)
            w = jnp.where(ok, jnp.exp2(s * (SCALE * LOG2E) - norm), 0.0)
            ds = (w * (dp - dot) * SCALE).astype(jnp.bfloat16)
            wb = w.astype(jnp.bfloat16)
            dv = jnp.dot(wb, do, preferred_element_type=jnp.float32)
            dk = jnp.dot(ds, q, preferred_element_type=jnp.float32)
            dqt_ref[...] += lax.dot_general(k, ds, TN, preferred_element_type=jnp.float32)
            acc_ref[pl.ds(a0, BLOCK), :] += dk[:BLOCK]
            acc_ref[pl.ds(a1, BLOCK), :] += dk[BLOCK:]
            acc_ref[pl.ds(a0 + 128, BLOCK), :] += dv[:BLOCK]
            acc_ref[pl.ds(a1 + 128, BLOCK), :] += dv[BLOCK:]
            return carry

        lax.fori_loop(0, (stop - start + 1) // 2, step, 0)
        dq = dqt_ref[...].T.astype(out.dtype)
        for h in heads:
            out[rows, h * HEAD : (h + 1) * HEAD] = dq[h * BLOCK : (h + 1) * BLOCK]
    dkv_ref[...] = acc_ref[...].astype(jnp.bfloat16)


def lanes(x):
    return x.transpose(0, 2, 1).reshape(2, LANES)


def on_device(queries, keys, values, attn_out, grad_out, log_norm, doc_lengths, block_order):
    rows = queries.shape[0]
    nblk = block_order.shape[0]
    nheld = nblk // 2
    me, core = lax.axis_index(CTX), lax.axis_index("core")
    kv = jnp.concatenate([keys, values], 0)
    kv = lax.all_to_all(jnp.broadcast_to(kv, (16,) + kv.shape), CHIPS, 0, 0, tiled=True)

    swap = [(0, 1), (1, 0)]
    q2 = lax.ppermute(queries, "core", swap)
    do2 = lax.ppermute(grad_out, "core", swap)
    gh = grad_out.reshape(2, BLOCK, HEADS, HEAD).astype(jnp.float32)
    oh = attn_out.reshape(2, BLOCK, HEADS, HEAD).astype(jnp.float32)
    out_dot = lanes(jnp.sum(gh * oh, axis=3))
    norm = (log_norm * LOG2E).reshape(HEADS, 2, BLOCK).transpose(1, 0, 2).reshape(2, LANES)
    rows_f = jnp.stack([norm, out_dot], axis=1).reshape(4, LANES)
    rows_f = jnp.concatenate([rows_f, lax.ppermute(rows_f, "core", swap)], 0)

    docs = doc_lengths.shape[0]
    upto = jnp.arange(docs)[:, None] >= jnp.arange(docs)[None, :]
    ends = jnp.sum(jnp.where(upto, doc_lengths[None, :], 0), axis=1)
    blocks = jnp.arange(nblk, dtype=jnp.int32)
    held_here = (blocks // 2) % 2 == core
    place = (blocks // 4) * (2 * rows) + (blocks % 2) * BLOCK
    before = held_here[None, :] & (block_order[None, :] < block_order[:, None])
    rank = jnp.sum(before.astype(jnp.int32), axis=1)
    slots = jnp.arange(nheld + 8, dtype=jnp.int32)
    hit = held_here[None, :] & (rank[None, :] == slots[:, None])
    held = jnp.sum(jnp.where(hit, block_order[None, :], 0), axis=1)
    held = jnp.where(slots < nheld, held, nblk)
    place = jnp.sum(jnp.where(hit, place[None, :], 0), axis=1)
    mine = jnp.concatenate(
        [
            lax.dynamic_slice_in_dim(block_order, me * 2, 2),
            lax.dynamic_slice_in_dim(block_order, (me + 1 - 2 * core) * 2, 2),
        ]
    )
    pos = mine[:, None] * BLOCK + jnp.arange(BLOCK, dtype=jnp.int32)[None, :]
    first = jnp.max(jnp.where(ends[None, None, :] <= pos[:, :, None], ends[None, None, :], 0), axis=2)
    lo = first[:, 0] // BLOCK
    begin = jnp.sum((held[None, :] < lo[:, None]).astype(jnp.int32), axis=1)
    until = jnp.sum((held[None, :] <= mine[:, None]).astype(jnp.int32), axis=1)
    rows_i = jnp.tile(jnp.stack([first, pos], axis=1), (1, 1, HEADS)).reshape(8, LANES)

    vmem = pl.BlockSpec(memory_space=pltpu.VMEM)
    smem = pl.BlockSpec(memory_space=pltpu.SMEM)
    total = 2 * nheld * BLOCK
    dq, dq2, dkv = pl.pallas_call(
        attention_terms,
        out_shape=(
            jax.ShapeDtypeStruct(queries.shape, jnp.float32),
            jax.ShapeDtypeStruct(queries.shape, jnp.bfloat16),
            jax.ShapeDtypeStruct((total, HEAD), jnp.bfloat16),
        ),
        in_specs=[smem] * 4 + [vmem] * 7,
        out_specs=(vmem,) * 3,
        scratch_shapes=[
            pltpu.VMEM((total, HEAD), jnp.float32),
            pltpu.VMEM((HEAD, LANES), jnp.float32),
        ],
        compiler_params=pltpu.CompilerParams(vmem_limit_bytes=32 << 20),
        name="attention_terms",
    )(begin, until, held, place, queries, q2, grad_out, do2, rows_f, rows_i, kv.reshape(total, HEAD))

    got = lax.all_to_all(dkv.reshape(16, 2 * rows, HEAD), CHIPS, 0, 0, tiled=True)
    other = lax.ppermute(dq2, "core", swap)
    grad_q = (dq + other.astype(jnp.float32)).astype(jnp.bfloat16)
    both = jnp.sum(got.astype(jnp.float32), axis=0).astype(jnp.bfloat16)
    return grad_q, both[:rows], both[rows:]


def solution(mesh):
    parts = Mesh(mesh.devices.reshape(2, 4, 4, 2, 8), ("dp", "yh", "x", "core", "tensor"))
    seq = ("dp",) + CTX
    wide = P(seq, "tensor")
    return jax.shard_map(
        on_device,
        mesh=parts,
        in_specs=(wide,) * 5 + (P("tensor", seq), P("dp"), P("dp")),
        out_specs=(wide, wide, wide),
        check_vma=False,
    )
```

time: 430 us -> 88.5 us (0.21)
  the two profiles are of different devices: /device:TPU:1 before, /device:TPU:392 now
where the time goes in v1:
time: 88.5 us; the launch traced here: 88.1 us
  waiting for transfers between devices  45.3 us (51%)
  starting transfers between devices  27.7 us (31%)
  Pallas kernels  6.58 us (7%)
  other arithmetic  3.99 us (5%)
  local copies, waits for them, and re-layouts  3.64 us (4%)
    all_to_all x1, waiting for transfers between devices, on_device(): lax.all_to_all(dkv.reshape(16, 2 * rows, HEAD), CHIPS, 0, 0, tiled=True)  23.2 us
    all_to_all x1, waiting for transfers between devices, on_device(): lax.all_to_all(jnp.broadcast_to(kv, (16,) + kv.shape), CHIPS, 0, 0, tiled...  20.6 us
    all_to_all x1, starting transfers between devices, on_device(): lax.all_to_all(dkv.reshape(16, 2 * rows, HEAD), CHIPS, 0, 0, tiled=True)  10.6 us
    all_to_all x1, starting transfers between devices, on_device(): lax.all_to_all(jnp.broadcast_to(kv, (16,) + kv.shape), CHIPS, 0, 0, tiled...  8.9 us
    pallas_call x1, Pallas kernels, on_device(): pl.pallas_call(attention_terms, out_shape=(jax.ShapeDtypeStruct(queries.s...  6.58 us
    ppermute x1, starting transfers between devices, on_device(): do2 = lax.ppermute(grad_out, 'core', swap)  2.41 us
    ppermute x1, starting transfers between devices, on_device(): q2 = lax.ppermute(queries, 'core', swap)  1.92 us
    ppermute x1, starting transfers between devices, on_device(): other = lax.ppermute(dq2, 'core', swap)  1.92 us
  transfers between devices with their start and end apart: 6, of which 3 were waited for; matrix products, arithmetic and copies ran while one was open for 6% of the time, Pallas kernels for 0%

profile of v1, /device:TPU:392, one launch (start us, length us, event | category | flops | bytes accessed | tf_op | source)
XLA Modules:
  0.0 88.1 jit_solution(6516448096530487461)
XLA Ops:
  0.6 1.9 %collective-permute-start = (bf16[128,1024]{1,0:T(8,128)(2,1)}, bf16[128,1024]{1,0:T(8,128)(2,1)S(1)}, u32[]{:S(2)}, u32[]{:S(2)}) collective-permute-start(bf16[128,1024]{1,0:T(8,128)(2,1)} %q_ref.1), channel_id=1, source_target_pairs={{0,8},{8,0},{1,9},{9,1},{2,10},{10,2},{3,11},{11,3},{4,12},{12,4},... | collective-permute-start | bytes 786440 | tf_op jit(solution)/shard_map/ppermute | solution.py:87
  2.6 2.4 %collective-permute-start.1 = (bf16[128,1024]{1,0:T(8,128)(2,1)}, bf16[128,1024]{1,0:T(8,128)(2,1)S(1)}, u32[]{:S(2)}, u32[]{:S(2)}) collective-permute-start(bf16[128,1024]{1,0:T(8,128)(2,1)} %do_ref.1), channel_id=1, source_target_pairs={{0,8},{8,0},{1,9},{9,1},{2,10},{10,2},{3,11},{11,3},{4,12},{12,4},... | collective-permute-start | bytes 786440 | tf_op jit(solution)/shard_map/ppermute | solution.py:88
  5.0 0.7 broadcast_multiply_fusion
  5.7 0.1 reshape.149
  5.8 0.1 stack_reshape.6
  5.8 1.1 %multiply_bitcast_fusion = f32[16,8,8,128]{3,1,2,0:T(8,128)S(1)} fusion(bf16[128,1024]{1,0:T(8,128)(2,1)} %param.11, bf16[128,1024]{1,0:T(8,128)(2,1)} %do_ref.1), kind=kLoop, calls=%fused_computation.2 | loop fusion | flops 393216 | bytes 1048576
  6.9 0.1 copy.23
  7.0 0.2 bitcast_reduce_fusion
  7.2 0.0 copy-start.3
  7.3 0.1 copy.20
  7.3 0.0 copy-start.2
  7.3 0.1 stack_reshape.7
  7.4 1.9 %collective-permute-start.2 = (f32[4,512]{1,0:T(4,128)S(1)}, f32[4,512]{1,0:T(4,128)S(1)}, u32[]{:S(2)}, u32[]{:S(2)}) collective-permute-start(f32[4,512]{1,0:T(4,128)S(1)} %reshape.150), channel_id=1, source_target_pairs={{0,8},{8,0},{1,9},{9,1},{2,10},{10,2},{3,11},{11,3},{4,12},{12,4},... | collective-permute-start | bytes 24584 | tf_op jit(solution)/shard_map/ppermute | solution.py:94
  9.4 0.0 copy-done.3
  9.4 0.0 copy-done.2
  9.4 1.2 %broadcast_in_dim.74 = bf16[16,256,128]{2,1,0:T(8,128)(2,1)} broadcast(bf16[256,128]{1,0:T(8,128)(2,1)S(1)} %pad_maximum_fusion), dimensions={1,2} | broadcast | bytes 1114112 | tf_op jit(solution)/shard_map/broadcast_in_dim | solution.py:84
  10.6 0.0 copy-start
  10.6 0.0 copy-start.1
  10.6 8.9 %all-to-all-start = ((bf16[16,256,128]{2,1,0:T(8,128)(2,1)}), bf16[16,256,128]{2,1,0:T(8,128)(2,1)S(1)}, u32[]{:S(2)}, u32[]{:S(2)}) async-start(bf16[16,256,128]{2,1,0:T(8,128)(2,1)} %broadcast_in_dim.74), calls=%async_computation | async-start | bytes 2097152 | tf_op jit(solution)/shard_map/all_to_all | solution.py:84
  19.5 0.0 copy-start.4
  19.6 0.6 copy-done.4
  20.2 0.1 fusion.10
  20.3 0.0 copy-start.5
  20.3 0.1 broadcast_multiply_fusion.1
  20.4 0.6 copy-done.5
  20.9 0.1 select_reduce_fusion.3
  21.1 0.1 iota_add_fusion.1
  21.1 0.1 select_reduce_fusion
  21.2 0.1 fusion.2
  21.3 0.2 convert_reduce_fusion
  21.5 0.1 select_reduce_fusion.1
  21.7 0.1 iota_add_fusion
  21.7 0.2 convert_reduce_fusion.1
  22.0 0.1 tile.9.rows_i_ref
  22.0 0.0 collective-permute-done.2
  22.1 0.0 collective-permute-done.q2_ref
  22.1 0.0 collective-permute-done.1.do2_ref
  22.1 20.6 %all-to-all-done = bf16[16,256,128]{2,1,0:T(8,128)(2,1)S(1)} async-done(((bf16[16,256,128]{2,1,0:T(8,128)(2,1)}), bf16[16,256,128]{2,1,0:T(8,128)(2,1)S(1)}, u32[]{:S(2)}, u32[]{:S(2)}) %all-to-all-start) | async-done | bytes 1048608 | tf_op jit(solution)/shard_map/all_to_all | solution.py:84
  42.7 0.0 copy-done
  42.7 0.0 copy-done.1
  42.7 6.6 %attention_terms.1 = (f32[128,1024]{1,0:T(8,128)S(1)}, bf16[128,1024]{1,0:T(8,128)(2,1)S(1)}, bf16[4096,128]{1,0:T(8,128)(2,1)}) custom-call(s32[4]{0:T(128)S(1)} %get-tuple-element.12.from_ref, s32[4]{0:T(128)S(1)} %get-tuple-element.11.upto_ref, s32[40]{0:T(128)S(1)} %compare_select_fusion.2.held_ref, s32[40]{0:T(128)S(1)} %get-tuple-element.9.place_ref, ...), custom_call_target="tpu_custom_call" | custom-call | tf_op jit(solution)/shard_map/attention_terms/pallas_call | solution.py:125
  49.2 10.6 %all-to-all-start.1 = ((bf16[16,256,128]{2,1,0:T(8,128)(2,1)}), bf16[16,256,128]{2,1,0:T(8,128)(2,1)S(1)}, u32[]{:S(2)}, u32[]{:S(2)}) async-start(bf16[16,256,128]{2,1,0:T(8,128)(2,1)} %bitcast.4), calls=%async_computation.1 | async-start | bytes 2097152 | tf_op jit(solution)/shard_map/all_to_all | solution.py:142
  59.9 1.9 %collective-permute-start.3 = (bf16[128,1024]{1,0:T(8,128)(2,1)S(1)}, bf16[128,1024]{1,0:T(8,128)(2,1)S(1)}, u32[]{:S(2)}, u32[]{:S(2)}) collective-permute-start(bf16[128,1024]{1,0:T(8,128)(2,1)S(1)} %get-tuple-element.7), channel_id=1, source_target_pairs={{0,8},{8,0},{1,9},{9,1},{2,10},{10,2},{3,11},{11,3},{4,12},{12,4},... | collective-permute-start | bytes 786440 | tf_op jit(solution)/shard_map/ppermute | solution.py:143
  61.8 1.5 %collective-permute-done.3 = bf16[128,1024]{1,0:T(8,128)(2,1)S(1)} collective-permute-done((bf16[128,1024]{1,0:T(8,128)(2,1)S(1)}, bf16[128,1024]{1,0:T(8,128)(2,1)S(1)}, u32[]{:S(2)}, u32[]{:S(2)}) %collective-permute-start.3) | collective-permute-done | bytes 262176 | tf_op jit(solution)/shard_map/ppermute | solution.py:143
  63.3 0.8 add_convert_fusion
  64.1 23.2 %all-to-all-done.1 = bf16[16,256,128]{2,1,0:T(8,128)(2,1)S(1)} async-done(((bf16[16,256,128]{2,1,0:T(8,128)(2,1)}), bf16[16,256,128]{2,1,0:T(8,128)(2,1)S(1)}, u32[]{:S(2)}, u32[]{:S(2)}) %all-to-all-start.1) | async-done | bytes 1048608 | tf_op jit(solution)/shard_map/all_to_all | solution.py:142
  87.3 0.1 reduce_sum.82
  87.4 0.6 fusion.9
  (12 shorter events, 0.1 us)
Async XLA Ops:
  0.6 21.4 %collective-permute-start = (bf16[128,1024]{1,0:T(8,128)(2,1)}, bf16[128,1024]{1,0:T(8,128)(2,1)S(1)}, u32[]{:S(2)}, u32[]{:S(2)}) collective-permute-start(bf16[128,1024]{1,0:T(8,128)(2,1)} %q_ref.1), channel_id=1, source_target_pairs={{0,8},{8,0},{1,9},{9,1},{2,10},{10,2},{3,11},{11,3},{4,12},{12,4},... | collective-permute-start | bytes 786440 | tf_op jit(solution)/shard_map/ppermute | solution.py:87
  2.6 19.5 %collective-permute-start.1 = (bf16[128,1024]{1,0:T(8,128)(2,1)}, bf16[128,1024]{1,0:T(8,128)(2,1)S(1)}, u32[]{:S(2)}, u32[]{:S(2)}) collective-permute-start(bf16[128,1024]{1,0:T(8,128)(2,1)} %do_ref.1), channel_id=1, source_target_pairs={{0,8},{8,0},{1,9},{9,1},{2,10},{10,2},{3,11},{11,3},{4,12},{12,4},... | collective-permute-start | bytes 786440 | tf_op jit(solution)/shard_map/ppermute | solution.py:88
  7.2 2.1 %copy-start.3 = (bf16[128,128]{1,0:T(8,128)(2,1)S(1)}, bf16[128,128]{1,0:T(8,128)(2,1)}, u32[]{:S(2)}) copy-start(bf16[128,128]{1,0:T(8,128)(2,1)} %param.9) | copy-start | bytes 98308
  7.3 2.1 %copy-start.2 = (bf16[128,128]{1,0:T(8,128)(2,1)S(1)}, bf16[128,128]{1,0:T(8,128)(2,1)}, u32[]{:S(2)}) copy-start(bf16[128,128]{1,0:T(8,128)(2,1)} %param.10) | copy-start | bytes 98308
  7.4 14.6 %collective-permute-start.2 = (f32[4,512]{1,0:T(4,128)S(1)}, f32[4,512]{1,0:T(4,128)S(1)}, u32[]{:S(2)}, u32[]{:S(2)}) collective-permute-start(f32[4,512]{1,0:T(4,128)S(1)} %reshape.150), channel_id=1, source_target_pairs={{0,8},{8,0},{1,9},{9,1},{2,10},{10,2},{3,11},{11,3},{4,12},{12,4},... | collective-permute-start | bytes 24584 | tf_op jit(solution)/shard_map/ppermute | solution.py:94
  10.6 32.1 %copy-start = (bf16[128,1024]{1,0:T(8,128)(2,1)S(1)}, bf16[128,1024]{1,0:T(8,128)(2,1)}, u32[]{:S(2)}) copy-start(bf16[128,1024]{1,0:T(8,128)(2,1)} %do_ref.1) | copy-start | bytes 786436
  10.6 32.1 %copy-start.1 = (bf16[128,1024]{1,0:T(8,128)(2,1)S(1)}, bf16[128,1024]{1,0:T(8,128)(2,1)}, u32[]{:S(2)}) copy-start(bf16[128,1024]{1,0:T(8,128)(2,1)} %q_ref.1) | copy-start | bytes 786436
  10.6 32.0 %all-to-all-start = ((bf16[16,256,128]{2,1,0:T(8,128)(2,1)}), bf16[16,256,128]{2,1,0:T(8,128)(2,1)S(1)}, u32[]{:S(2)}, u32[]{:S(2)}) async-start(bf16[16,256,128]{2,1,0:T(8,128)(2,1)} %broadcast_in_dim.74), calls=%async_computation | async-start | bytes 2097152 | tf_op jit(solution)/shard_map/all_to_all | solution.py:84
  19.5 0.7 copy-start.4
  20.3 0.7 copy-start.5
  49.2 38.0 %all-to-all-start.1 = ((bf16[16,256,128]{2,1,0:T(8,128)(2,1)}), bf16[16,256,128]{2,1,0:T(8,128)(2,1)S(1)}, u32[]{:S(2)}, u32[]{:S(2)}) async-start(bf16[16,256,128]{2,1,0:T(8,128)(2,1)} %bitcast.4), calls=%async_computation.1 | async-start | bytes 2097152 | tf_op jit(solution)/shard_map/all_to_all | solution.py:142
  59.9 3.4 %collective-permute-start.3 = (bf16[128,1024]{1,0:T(8,128)(2,1)S(1)}, bf16[128,1024]{1,0:T(8,128)(2,1)S(1)}, u32[]{:S(2)}, u32[]{:S(2)}) collective-permute-start(bf16[128,1024]{1,0:T(8,128)(2,1)S(1)} %get-tuple-element.7), channel_id=1, source_target_pairs={{0,8},{8,0},{1,9},{9,1},{2,10},{10,2},{3,11},{11,3},{4,12},{12,4},... | collective-permute-start | bytes 786440 | tf_op jit(solution)/shard_map/ppermute | solution.py:143

commit v2 on v1

v2 whole, which is shorter than its diff:
```python
import math

import jax
import jax.numpy as jnp
from jax import lax
from jax.experimental import pallas as pl
from jax.experimental.pallas import tpu as pltpu
from jax.sharding import Mesh
from jax.sharding import PartitionSpec as P

HEADS = 8
HEAD = 128
BLOCK = 64
LANES = HEADS * BLOCK
SCALE = 1.0 / math.sqrt(HEAD)
LOG2E = math.log2(math.e)
CTX = ("yh", "xh", "xl", "core")
KEEPERS = ("yh", "xh")
NEXT = ("xh", "xl", "core")
NT = (((1,), (1,)), ((), ()))
TN = (((0,), (0,)), ((), ()))


def pack_rows(norm_ref, q_ref, do_ref, o_ref, out_ref):
    rows = q_ref.shape[0]
    out_ref[:rows] = q_ref[...]
    out_ref[rows : 2 * rows] = do_ref[...]
    ones = jnp.ones((8, HEAD), jnp.float32)
    dots = []
    for b in range(2):
        at = slice(b * BLOCK, (b + 1) * BLOCK)
        prod = jnp.concatenate(
            [
                do_ref[at, h * HEAD : (h + 1) * HEAD].astype(jnp.float32)
                * o_ref[at, h * HEAD : (h + 1) * HEAD].astype(jnp.float32)
                for h in range(HEADS)
            ],
            0,
        )
        dots.append(
            lax.dot_general(
                ones, prod, NT, precision=lax.Precision.HIGHEST, preferred_element_type=jnp.float32
            )[:1]
        )
    parts = []
    for x in (norm_ref[...], jnp.concatenate(dots, 1)):
        for _ in range(3):
            term = x.astype(jnp.bfloat16).astype(jnp.float32)
            parts.append(term)
            x = x - term
    parts.append(jnp.zeros((10, 2 * LANES), jnp.float32))
    out_ref[2 * rows :] = jnp.concatenate(parts, 0).astype(jnp.bfloat16)


def attention_terms(
    from_ref, upto_ref, held_ref, place_ref, rows_i_ref, p0_ref, p1_ref, p2_ref, p3_ref, kv_ref,
    dq0_ref, dq2_ref, sib_ref, dkv_ref, acc_ref, dqt_ref,
):
    acc_ref[...] = jnp.zeros_like(acc_ref)
    heads = range(HEADS)
    nrow = dq0_ref.shape[0]
    outs = (dq0_ref, sib_ref.at[:nrow], dq2_ref, sib_ref.at[nrow:])
    for g, (p_ref, out) in enumerate(zip((p0_ref, p1_ref, p2_ref, p3_ref), outs)):
        more = p_ref[2 * nrow :, :].astype(jnp.float32)
        norms = more[0:1] + more[1:2] + more[2:3]
        dots = more[3:4] + more[4:5] + more[5:6]
        for i in range(2):
            b = 2 * g + i
            at = slice(i * BLOCK, (i + 1) * BLOCK)
            at2 = slice(nrow + i * BLOCK, nrow + (i + 1) * BLOCK)
            q = jnp.concatenate([p_ref[at, h * HEAD : (h + 1) * HEAD] for h in heads], 0)
            do = jnp.concatenate([p_ref[at2, h * HEAD : (h + 1) * HEAD] for h in heads], 0)
            norm = norms[:, i * LANES : (i + 1) * LANES]
            dot = dots[:, i * LANES : (i + 1) * LANES]
            first = rows_i_ref[2 * b : 2 * b + 1, :]
            own = rows_i_ref[2 * b + 1 : 2 * b + 2, :]
            start, stop = from_ref[b], upto_ref[b]
            dqt_ref[...] = jnp.zeros_like(dqt_ref)

            def step(c, carry, q=q, do=do, norm=norm, dot=dot, first=first, own=own, start=start):
                j = start + 2 * c
                a0 = pl.multiple_of(place_ref[j], BLOCK)
                a1 = pl.multiple_of(place_ref[j + 1], BLOCK)
                k = jnp.concatenate([kv_ref[pl.ds(a0, BLOCK), :], kv_ref[pl.ds(a1, BLOCK), :]], 0)
                v = jnp.concatenate(
                    [kv_ref[pl.ds(a0 + 128, BLOCK), :], kv_ref[pl.ds(a1 + 128, BLOCK), :]], 0
                )
                s = lax.dot_general(k, q, NT, preferred_element_type=jnp.float32)
                dp = lax.dot_general(v, do, NT, preferred_element_type=jnp.float32)
                lane = lax.broadcasted_iota(jnp.int32, (BLOCK, LANES), 0)
                pos = jnp.concatenate(
                    [lane + held_ref[j] * BLOCK, lane + held_ref[j + 1] * BLOCK], 0
                )
                ok = (pos >= first) & (pos <= own)
                w = jnp.where(ok, jnp.exp2(s * (SCALE * LOG2E) - norm), 0.0)
                ds = (w * (dp - dot) * SCALE).astype(jnp.bfloat16)
                wb = w.astype(jnp.bfloat16)
                dv = jnp.dot(wb, do, preferred_element_type=jnp.float32)
                dk = jnp.dot(ds, q, preferred_element_type=jnp.float32)
                dqt_ref[...] += lax.dot_general(k, ds, TN, preferred_element_type=jnp.float32)
                acc_ref[pl.ds(a0, BLOCK), :] += dk[:BLOCK]
                acc_ref[pl.ds(a1, BLOCK), :] += dk[BLOCK:]
                acc_ref[pl.ds(a0 + 128, BLOCK), :] += dv[:BLOCK]
                acc_ref[pl.ds(a1 + 128, BLOCK), :] += dv[BLOCK:]
                return carry

            lax.fori_loop(0, (stop - start + 1) // 2, step, 0)
            dq = dqt_ref[...].T.astype(out.dtype)
            for h in heads:
                out[at, h * HEAD : (h + 1) * HEAD] = dq[h * BLOCK : (h + 1) * BLOCK]
    dkv_ref[...] = acc_ref[...].astype(jnp.bfloat16)


def on_device(queries, keys, values, attn_out, grad_out, log_norm, doc_lengths, block_order):
    rows = queries.shape[0]
    nblk = block_order.shape[0]
    nheld = nblk // 4
    yh, xh, xl, core = (lax.axis_index(a) for a in CTX)
    x = 2 * xh + xl
    vmem = pl.BlockSpec(memory_space=pltpu.VMEM)
    smem = pl.BlockSpec(memory_space=pltpu.SMEM)

    kv = jnp.concatenate([keys, values], 0)
    kv = lax.all_to_all(jnp.broadcast_to(kv, (8,) + kv.shape), KEEPERS, 0, 0, tiled=True)

    norm = (log_norm * LOG2E).reshape(HEADS, 2, BLOCK).transpose(1, 0, 2).reshape(1, 2 * LANES)
    p0 = pl.pallas_call(
        pack_rows,
        out_shape=jax.ShapeDtypeStruct((2 * rows + 16, queries.shape[1]), jnp.bfloat16),
        in_specs=[vmem] * 4,
        out_specs=vmem,
        compiler_params=pltpu.CompilerParams(vmem_limit_bytes=16 << 20),
        name="pack_rows",
    )(norm, queries, grad_out, attn_out)
    swap = [(0, 1), (1, 0)]
    there = [(2 * ((i + 1) % 4), 2 * i) for i in range(4)]
    there += [(2 * i + 1, 2 * ((i + 1) % 4) + 1) for i in range(4)]
    back = [(j, i) for i, j in there]
    p1 = lax.ppermute(p0, "core", swap)
    p2 = lax.ppermute(p0, NEXT, there)
    p3 = lax.ppermute(p2, "core", swap)

    docs = doc_lengths.shape[0]
    upto = jnp.arange(docs)[:, None] >= jnp.arange(docs)[None, :]
    ends = jnp.sum(jnp.where(upto, doc_lengths[None, :], 0), axis=1)
    blocks = jnp.arange(nblk, dtype=jnp.int32)
    held_here = ((blocks // 2) % 2 == core) & ((blocks // 4) % 2 == xl)
    place = (blocks // 8) * (2 * rows) + (blocks % 2) * BLOCK
    before = held_here[None, :] & (block_order[None, :] < block_order[:, None])
    rank = jnp.sum(before.astype(jnp.int32), axis=1)
    slots = jnp.arange(nheld + 8, dtype=jnp.int32)
    hit = held_here[None, :] & (rank[None, :] == slots[:, None])
    held = jnp.sum(jnp.where(hit, block_order[None, :], 0), axis=1)
    held = jnp.where(slots < nheld, held, nblk)
    place = jnp.sum(jnp.where(hit, place[None, :], 0), axis=1)
    turn = 1 - 2 * core
    owners = jnp.stack(
        [
            2 * x + core,
            2 * x + 1 - core,
            2 * ((x + turn) % 4) + core,
            2 * ((x - turn) % 4) + 1 - core,
        ]
    ) + 8 * yh
    stored = (2 * owners[:, None] + jnp.arange(2)[None, :]).reshape(8)
    mine = jnp.sum(jnp.where(stored[:, None] == blocks[None, :], block_order[None, :], 0), axis=1)
    pos = mine[:, None] * BLOCK + jnp.arange(BLOCK, dtype=jnp.int32)[None, :]
    first = jnp.max(jnp.where(ends[None, None, :] <= pos[:, :, None], ends[None, None, :], 0), axis=2)
    lo = first[:, 0] // BLOCK
    begin = jnp.sum((held[None, :] < lo[:, None]).astype(jnp.int32), axis=1)
    until = jnp.sum((held[None, :] <= mine[:, None]).astype(jnp.int32), axis=1)
    rows_i = jnp.tile(jnp.stack([first, pos], axis=1), (1, 1, HEADS)).reshape(16, LANES)

    total = 2 * nheld * BLOCK
    dq0, dq2, sib, dkv = pl.pallas_call(
        attention_terms,
        out_shape=(
            jax.ShapeDtypeStruct(queries.shape, jnp.float32),
            jax.ShapeDtypeStruct(queries.shape, jnp.float32),
            jax.ShapeDtypeStruct((2 * rows, queries.shape[1]), jnp.bfloat16),
            jax.ShapeDtypeStruct((total, HEAD), jnp.bfloat16),
        ),
        in_specs=[smem] * 4 + [vmem] * 6,
        out_specs=(vmem,) * 4,
        scratch_shapes=[
            pltpu.VMEM((total, HEAD), jnp.float32),
            pltpu.VMEM((HEAD, LANES), jnp.float32),
        ],
        compiler_params=pltpu.CompilerParams(vmem_limit_bytes=32 << 20),
        name="attention_terms",
    )(begin, until, held, place, rows_i, p0, p1, p2, p3, kv.reshape(total, HEAD))

    got = lax.all_to_all(dkv.reshape(8, 2 * rows, HEAD), KEEPERS, 0, 0, tiled=True)
    sib = lax.ppermute(sib, "core", swap).astype(jnp.float32)
    far = lax.ppermute((dq2 + sib[rows:]).astype(jnp.bfloat16), NEXT, back)
    grad_q = (dq0 + sib[:rows] + far.astype(jnp.float32)).astype(jnp.bfloat16)
    both = jnp.sum(got.astype(jnp.float32), axis=0).astype(jnp.bfloat16)
    return grad_q, both[:rows], both[rows:]


def solution(mesh):
    parts = Mesh(
        mesh.devices.reshape(2, 4, 2, 2, 2, 8), ("dp", "yh", "xh", "xl", "core", "tensor")
    )
    seq = ("dp",) + CTX
    wide = P(seq, "tensor")
    return jax.shard_map(
        on_device,
        mesh=parts,
        in_specs=(wide,) * 5 + (P("tensor", seq), P("dp"), P("dp")),
        out_specs=(wide, wide, wide),
        check_vma=False,
    )
```

time: 88.5 us -> 70.6 us (0.80)
  the two profiles are of different devices: /device:TPU:392 before, /device:TPU:384 now
where the time goes in v2:
time: 70.6 us; the launch traced here: 70 us
  starting transfers between devices  28.2 us (40%)
  waiting for transfers between devices  23.5 us (33%)
  local copies, waits for them, and re-layouts  8.36 us (12%)
  Pallas kernels  6.05 us (9%)
  other arithmetic  3.07 us (4%)
  between operations  0.81 us (1%)
    all_to_all x1, waiting for transfers between devices, on_device(): lax.all_to_all(jnp.broadcast_to(kv, (8,) + kv.shape), KEEPERS, 0, 0, tile...  12.2 us
    ppermute x1, waiting for transfers between devices, on_device(): far = lax.ppermute((dq2 + sib[rows:]).astype(jnp.bfloat16), NEXT, back)  11.2 us
    all_to_all x1, starting transfers between devices, on_device(): lax.all_to_all(jnp.broadcast_to(kv, (8,) + kv.shape), KEEPERS, 0, 0, tile...  7.54 us
    all_to_all x1, starting transfers between devices, on_device(): lax.all_to_all(dkv.reshape(8, 2 * rows, HEAD), KEEPERS, 0, 0, tiled=True)  7.43 us
    unnamed x20, local copies, waits for them, and re-layouts  6.53 us
    pallas_call x1, Pallas kernels, on_device(): pl.pallas_call(attention_terms, out_shape=(jax.ShapeDtypeStruct(queries.s...  5.5 us
    ppermute x1, starting transfers between devices, on_device(): p2 = lax.ppermute(p0, NEXT, there)  4.67 us
    ppermute x1, starting transfers between devices, on_device(): far = lax.ppermute((dq2 + sib[rows:]).astype(jnp.bfloat16), NEXT, back)  2.8 us
  transfers between devices with their start and end apart: 7, of which 2 were waited for; matrix products, arithmetic and copies ran while one was open for 5% of the time, Pallas kernels for 0%

profile of v2, /device:TPU:384, one launch (start us, length us, event | category | flops | bytes accessed | tf_op | source)
XLA Modules:
  0.0 70.0 jit_solution(6748333836072344887)
XLA Ops:
  0.6 0.7 broadcast_multiply_fusion
  1.3 0.1 reshape.202
  1.4 0.1 reshape.203.norm_ref
  1.5 0.0 copy-start.3
  1.5 0.9 %copy-done.3 = bf16[128,1024]{1,0:T(8,128)(2,1)S(1)} copy-done((bf16[128,1024]{1,0:T(8,128)(2,1)S(1)}, bf16[128,1024]{1,0:T(8,128)(2,1)}, u32[]{:S(2)}) %copy-start.3) | copy-done | bytes 262168
  2.4 0.0 copy-start.4
  2.4 0.9 %copy-done.4 = bf16[128,1024]{1,0:T(8,128)(2,1)S(1)} copy-done((bf16[128,1024]{1,0:T(8,128)(2,1)S(1)}, bf16[128,1024]{1,0:T(8,128)(2,1)}, u32[]{:S(2)}) %copy-start.4) | copy-done | bytes 262168
  3.4 0.0 copy-start.5
  3.4 0.9 %copy-done.5 = bf16[128,1024]{1,0:T(8,128)(2,1)S(1)} copy-done((bf16[128,1024]{1,0:T(8,128)(2,1)S(1)}, bf16[128,1024]{1,0:T(8,128)(2,1)}, u32[]{:S(2)}) %copy-start.5) | copy-done | bytes 262168
  4.3 0.0 copy-start.6
  4.3 0.0 copy-start.7
  4.3 0.6 pack_rows.1.p0_ref
  4.9 4.7 %collective-permute-start.1 = (bf16[272,1024]{1,0:T(8,128)(2,1)S(1)}, bf16[272,1024]{1,0:T(8,128)(2,1)S(1)}, u32[]{:S(2)}, u32[]{:S(2)}) collective-permute-start(bf16[272,1024]{1,0:T(8,128)(2,1)S(1)} %pack_rows.1.p0_ref), channel_id=1, source_target_pairs={{16,0},{32,16},{48,32},{0,48},{8,24},{24,40},{40,56},{56,8},{17,1}... | collective-permute-start | bytes 1671176 | tf_op jit(solution)/shard_map/ppermute | solution.py:140
  9.6 1.9 %collective-permute-start = (bf16[272,1024]{1,0:T(8,128)(2,1)S(1)}, bf16[272,1024]{1,0:T(8,128)(2,1)S(1)}, u32[]{:S(2)}, u32[]{:S(2)}) collective-permute-start(bf16[272,1024]{1,0:T(8,128)(2,1)S(1)} %pack_rows.1.p0_ref), channel_id=1, source_target_pairs={{0,8},{8,0},{1,9},{9,1},{2,10},{10,2},{3,11},{11,3},{4,12},{12,4},... | collective-permute-start | bytes 1671176 | tf_op jit(solution)/shard_map/ppermute | solution.py:139
  11.5 0.0 copy-done.6
  11.5 0.0 copy-done.7
  11.5 0.9 %broadcast_in_dim.92 = bf16[8,256,128]{2,1,0:T(8,128)(2,1)} broadcast(bf16[256,128]{1,0:T(8,128)(2,1)S(1)} %pad_maximum_fusion), dimensions={1,2} | broadcast | bytes 589824 | tf_op jit(solution)/shard_map/broadcast_in_dim | solution.py:124
  12.4 7.5 %all-to-all-start = ((bf16[8,256,128]{2,1,0:T(8,128)(2,1)}), bf16[8,256,128]{2,1,0:T(8,128)(2,1)S(1)}, u32[]{:S(2)}, u32[]{:S(2)}) async-start(bf16[8,256,128]{2,1,0:T(8,128)(2,1)} %broadcast_in_dim.92), calls=%async_computation | async-start | bytes 1048576 | tf_op jit(solution)/shard_map/all_to_all | solution.py:124
  19.9 0.1 fusion.13
  20.0 0.1 iota_add_fusion.2
  20.1 0.0 copy-start.8
  20.1 0.1 add.155
  20.2 0.6 copy-done.8
  20.8 0.2 select_reduce_fusion.4
  20.9 0.1 iota_add_fusion
  21.0 0.0 copy-start.9
  21.0 0.1 iota_add_fusion.1
  21.1 0.6 copy-done.9
  21.7 0.1 select_reduce_fusion.3
  21.8 0.1 select_reduce_fusion
  21.9 0.1 tile.9.rows_i_ref
  22.0 0.1 fusion.5
  22.1 0.2 convert_reduce_fusion
  22.3 0.0 collective-permute-done.1.p2_ref
  22.3 1.9 %collective-permute-start.2 = (bf16[272,1024]{1,0:T(8,128)(2,1)S(1)}, bf16[272,1024]{1,0:T(8,128)(2,1)S(1)}, u32[]{:S(2)}, u32[]{:S(2)}) collective-permute-start(bf16[272,1024]{1,0:T(8,128)(2,1)S(1)} %collective-permute-done.1.p2_ref), channel_id=1, source_target_pairs={{0,8},{8,0},{1,9},{9,1},{2,10},{10,2},{3,11},{11,3},{4,12},{12,4},... | collective-permute-start | bytes 1671176 | tf_op jit(solution)/shard_map/ppermute | solution.py:141
  24.3 0.1 select_reduce_fusion.1
  24.4 0.2 convert_reduce_fusion.1
  24.6 0.0 collective-permute-done.p1_ref
  24.6 12.2 %all-to-all-done = bf16[8,256,128]{2,1,0:T(8,128)(2,1)S(1)} async-done(((bf16[8,256,128]{2,1,0:T(8,128)(2,1)}), bf16[8,256,128]{2,1,0:T(8,128)(2,1)S(1)}, u32[]{:S(2)}, u32[]{:S(2)}) %all-to-all-start) | async-done | bytes 524320 | tf_op jit(solution)/shard_map/all_to_all | solution.py:124
  36.9 0.0 collective-permute-done.2.p3_ref
  36.9 5.5 %attention_terms.1 = (f32[128,1024]{1,0:T(8,128)S(1)}, f32[128,1024]{1,0:T(8,128)S(1)}, bf16[256,1024]{1,0:T(8,128)(2,1)}, bf16[2048,128]{1,0:T(8,128)(2,1)S(1)}) custom-call(s32[8]{0:T(128)S(1)} %get-tuple-element.14.from_ref, s32[8]{0:T(128)S(1)} %get-tuple-element.13.upto_ref, s32[24]{0:T(128)S(1)} %compare_select_fusion.4.held_ref, ...), custom_call_target="tpu_custom_call" | custom-call | tf_op jit(solution)/shard_map/attention_terms/pallas_call | solution.py:175
  42.4 0.0 copy-start
  42.4 0.8 %copy-done = bf16[2048,128]{1,0:T(8,128)(2,1)} copy-done((bf16[2048,128]{1,0:T(8,128)(2,1)}, bf16[2048,128]{1,0:T(8,128)(2,1)S(1)}, u32[]{:S(2)}) %copy-start) | copy-done | bytes 524312
  43.2 0.0 copy-start.1
  43.2 0.8 %copy-done.1 = f32[128,1024]{1,0:T(8,128)} copy-done((f32[128,1024]{1,0:T(8,128)}, f32[128,1024]{1,0:T(8,128)S(1)}, u32[]{:S(2)}) %copy-start.1) | copy-done | bytes 524312
  44.0 2.0 %collective-permute-start.3 = (bf16[256,1024]{1,0:T(8,128)(2,1)}, bf16[256,1024]{1,0:T(8,128)(2,1)S(1)}, u32[]{:S(2)}, u32[]{:S(2)}) collective-permute-start(bf16[256,1024]{1,0:T(8,128)(2,1)} %get-tuple-element.8), channel_id=1, source_target_pairs={{0,8},{8,0},{1,9},{9,1},{2,10},{10,2},{3,11},{11,3},{4,12},{12,4},... | collective-permute-start | bytes 1572872 | tf_op jit(solution)/shard_map/ppermute | solution.py:194
  45.9 7.4 %all-to-all-start.1 = ((bf16[8,256,128]{2,1,0:T(8,128)(2,1)}), bf16[8,256,128]{2,1,0:T(8,128)(2,1)S(1)}, u32[]{:S(2)}, u32[]{:S(2)}) async-start(bf16[8,256,128]{2,1,0:T(8,128)(2,1)} %bitcast.15), calls=%async_computation.1 | async-start | bytes 1048576 | tf_op jit(solution)/shard_map/all_to_all | solution.py:193
  53.4 0.0 copy-start.2
  53.4 0.0 collective-permute-done.3
  53.4 0.1 convert_element_type.26
  53.5 0.9 %copy-done.2 = f32[128,1024]{1,0:T(8,128)S(1)} copy-done((f32[128,1024]{1,0:T(8,128)S(1)}, f32[128,1024]{1,0:T(8,128)}, u32[]{:S(2)}) %copy-start.2) | copy-done | bytes 524312
  54.4 0.1 fusion
  54.5 2.8 %collective-permute-start.4 = (bf16[128,1024]{1,0:T(8,128)(2,1)S(1)}, bf16[128,1024]{1,0:T(8,128)(2,1)S(1)}, u32[]{:S(2)}, u32[]{:S(2)}) collective-permute-start(bf16[128,1024]{1,0:T(8,128)(2,1)S(1)} %fusion), channel_id=1, source_target_pairs={{0,16},{16,32},{32,48},{48,0},{24,8},{40,24},{56,40},{8,56},{1,17}... | collective-permute-start | bytes 786440 | tf_op jit(solution)/shard_map/ppermute | solution.py:195
  57.3 11.2 %collective-permute-done.4 = bf16[128,1024]{1,0:T(8,128)(2,1)S(1)} collective-permute-done((bf16[128,1024]{1,0:T(8,128)(2,1)S(1)}, bf16[128,1024]{1,0:T(8,128)(2,1)S(1)}, u32[]{:S(2)}, u32[]{:S(2)}) %collective-permute-start.4) | collective-permute-done | bytes 262176 | tf_op jit(solution)/shard_map/ppermute | solution.py:195
  68.5 0.8 %fusion.2 = bf16[128,1024]{1,0:T(8,128)(2,1)} fusion(f32[128,1024]{1,0:T(8,128)S(1)} %get-tuple-element.7, f32[256,1024]{1,0:T(8,128)S(1)} %convert_element_type.26, bf16[128,1024]{1,0:T(8,128)(2,1)S(1)} %collective-permute-done.4), kind=kLoop, calls=%fused_computation.4 | loop fusion | flops 524288 | bytes 1572864 | tf_op jit(solution)/shard_map/convert_element_type | solution.py:196
  69.3 0.0 all-to-all-done.1
  69.3 0.1 reduce_sum.82
  69.4 0.6 fusion.14
  (9 shorter events, 0.1 us)
Async XLA Ops:
  1.5 0.9 %copy-start.3 = (bf16[128,1024]{1,0:T(8,128)(2,1)S(1)}, bf16[128,1024]{1,0:T(8,128)(2,1)}, u32[]{:S(2)}) copy-start(bf16[128,1024]{1,0:T(8,128)(2,1)} %q_ref.1) | copy-start | bytes 786436
  2.4 0.9 %copy-start.4 = (bf16[128,1024]{1,0:T(8,128)(2,1)S(1)}, bf16[128,1024]{1,0:T(8,128)(2,1)}, u32[]{:S(2)}) copy-start(bf16[128,1024]{1,0:T(8,128)(2,1)} %do_ref.1) | copy-start | bytes 786436
  3.4 0.9 %copy-start.5 = (bf16[128,1024]{1,0:T(8,128)(2,1)S(1)}, bf16[128,1024]{1,0:T(8,128)(2,1)}, u32[]{:S(2)}) copy-start(bf16[128,1024]{1,0:T(8,128)(2,1)} %o_ref.1) | copy-start | bytes 786436
  4.3 7.2 %copy-start.6 = (bf16[128,128]{1,0:T(8,128)(2,1)S(1)}, bf16[128,128]{1,0:T(8,128)(2,1)}, u32[]{:S(2)}) copy-start(bf16[128,128]{1,0:T(8,128)(2,1)} %param.10) | copy-start | bytes 98308
  4.3 7.2 %copy-start.7 = (bf16[128,128]{1,0:T(8,128)(2,1)S(1)}, bf16[128,128]{1,0:T(8,128)(2,1)}, u32[]{:S(2)}) copy-start(bf16[128,128]{1,0:T(8,128)(2,1)} %param.9) | copy-start | bytes 98308
  4.9 17.4 %collective-permute-start.1 = (bf16[272,1024]{1,0:T(8,128)(2,1)S(1)}, bf16[272,1024]{1,0:T(8,128)(2,1)S(1)}, u32[]{:S(2)}, u32[]{:S(2)}) collective-permute-start(bf16[272,1024]{1,0:T(8,128)(2,1)S(1)} %pack_rows.1.p0_ref), channel_id=1, source_target_pairs={{16,0},{32,16},{48,32},{0,48},{8,24},{24,40},{40,56},{56,8},{17,1}... | collective-permute-start | bytes 1671176 | tf_op jit(solution)/shard_map/ppermute | solution.py:140
  9.6 15.0 %collective-permute-start = (bf16[272,1024]{1,0:T(8,128)(2,1)S(1)}, bf16[272,1024]{1,0:T(8,128)(2,1)S(1)}, u32[]{:S(2)}, u32[]{:S(2)}) collective-permute-start(bf16[272,1024]{1,0:T(8,128)(2,1)S(1)} %pack_rows.1.p0_ref), channel_id=1, source_target_pairs={{0,8},{8,0},{1,9},{9,1},{2,10},{10,2},{3,11},{11,3},{4,12},{12,4},... | collective-permute-start | bytes 1671176 | tf_op jit(solution)/shard_map/ppermute | solution.py:139
  12.4 24.5 %all-to-all-start = ((bf16[8,256,128]{2,1,0:T(8,128)(2,1)}), bf16[8,256,128]{2,1,0:T(8,128)(2,1)S(1)}, u32[]{:S(2)}, u32[]{:S(2)}) async-start(bf16[8,256,128]{2,1,0:T(8,128)(2,1)} %broadcast_in_dim.92), calls=%async_computation | async-start | bytes 1048576 | tf_op jit(solution)/shard_map/all_to_all | solution.py:124
  20.1 0.7 copy-start.8
  21.0 0.7 copy-start.9
  22.3 14.5 %collective-permute-start.2 = (bf16[272,1024]{1,0:T(8,128)(2,1)S(1)}, bf16[272,1024]{1,0:T(8,128)(2,1)S(1)}, u32[]{:S(2)}, u32[]{:S(2)}) collective-permute-start(bf16[272,1024]{1,0:T(8,128)(2,1)S(1)} %collective-permute-done.1.p2_ref), channel_id=1, source_target_pairs={{0,8},{8,0},{1,9},{9,1},{2,10},{10,2},{3,11},{11,3},{4,12},{12,4},... | collective-permute-start | bytes 1671176 | tf_op jit(solution)/shard_map/ppermute | solution.py:141
  42.4 0.8 %copy-start = (bf16[2048,128]{1,0:T(8,128)(2,1)}, bf16[2048,128]{1,0:T(8,128)(2,1)S(1)}, u32[]{:S(2)}) copy-start(bf16[2048,128]{1,0:T(8,128)(2,1)S(1)} %get-tuple-element.10) | copy-start | bytes 1572868
  43.2 0.8 %copy-start.1 = (f32[128,1024]{1,0:T(8,128)}, f32[128,1024]{1,0:T(8,128)S(1)}, u32[]{:S(2)}) copy-start(f32[128,1024]{1,0:T(8,128)S(1)} %get-tuple-element.9) | copy-start | bytes 1572868
  44.0 9.4 %collective-permute-start.3 = (bf16[256,1024]{1,0:T(8,128)(2,1)}, bf16[256,1024]{1,0:T(8,128)(2,1)S(1)}, u32[]{:S(2)}, u32[]{:S(2)}) collective-permute-start(bf16[256,1024]{1,0:T(8,128)(2,1)} %get-tuple-element.8), channel_id=1, source_target_pairs={{0,8},{8,0},{1,9},{9,1},{2,10},{10,2},{3,11},{11,3},{4,12},{12,4},... | collective-permute-start | bytes 1572872 | tf_op jit(solution)/shard_map/ppermute | solution.py:194
  45.9 23.3 %all-to-all-start.1 = ((bf16[8,256,128]{2,1,0:T(8,128)(2,1)}), bf16[8,256,128]{2,1,0:T(8,128)(2,1)S(1)}, u32[]{:S(2)}, u32[]{:S(2)}) async-start(bf16[8,256,128]{2,1,0:T(8,128)(2,1)} %bitcast.15), calls=%async_computation.1 | async-start | bytes 1048576 | tf_op jit(solution)/shard_map/all_to_all | solution.py:193
  53.4 1.0 %copy-start.2 = (f32[128,1024]{1,0:T(8,128)S(1)}, f32[128,1024]{1,0:T(8,128)}, u32[]{:S(2)}) copy-start(f32[128,1024]{1,0:T(8,128)} %copy-done.1) | copy-start | bytes 1572868
  54.5 14.0 %collective-permute-start.4 = (bf16[128,1024]{1,0:T(8,128)(2,1)S(1)}, bf16[128,1024]{1,0:T(8,128)(2,1)S(1)}, u32[]{:S(2)}, u32[]{:S(2)}) collective-permute-start(bf16[128,1024]{1,0:T(8,128)(2,1)S(1)} %fusion), channel_id=1, source_target_pairs={{0,16},{16,32},{32,48},{48,0},{24,8},{40,24},{56,40},{8,56},{1,17}... | collective-permute-start | bytes 786440 | tf_op jit(solution)/shard_map/ppermute | solution.py:195

commit v3 on v2

v3 whole, which is shorter than its diff:
```python
import math

import jax
import jax.numpy as jnp
from jax import lax
from jax.experimental import pallas as pl
from jax.experimental.pallas import tpu as pltpu
from jax.sharding import Mesh
from jax.sharding import PartitionSpec as P

HEADS = 8
HEAD = 128
BLOCK = 64
ROWS = 2 * BLOCK
WIDTH = HEADS * HEAD
LANES = HEADS * BLOCK
EXTRA = 16
PEERS = 8
SLOTS = 72
SCALE = 1.0 / math.sqrt(HEAD)
LOG2E = math.log2(math.e)
CTX = ("yh", "xh", "xl", "core")
KEEPERS = ("yh", "xh")
NEXT = ("xh", "xl", "core")
NT = (((1,), (1,)), ((), ()))
TN = (((0,), (0,)), ((), ()))
VMEM = pl.BlockSpec(memory_space=pltpu.VMEM)
SMEM = pl.BlockSpec(memory_space=pltpu.SMEM)
HBM = pl.BlockSpec(memory_space=pltpu.HBM)


def head(h):
    return slice(h * HEAD, (h + 1) * HEAD)


def in_hbm(x):
    return pltpu.with_memory_space_constraint(x, pltpu.HBM)


def call(kernel, out, ins, outs, *args, scratch=(), limit=16):
    return pl.pallas_call(
        kernel,
        out_shape=out,
        in_specs=ins,
        out_specs=outs,
        scratch_shapes=scratch,
        compiler_params=pltpu.CompilerParams(vmem_limit_bytes=limit << 20),
        name=kernel.__name__,
    )(*args)


def terms_of(x):
    parts = []
    for _ in range(3):
        term = x.astype(jnp.bfloat16).astype(jnp.float32)
        parts.append(term)
        x = x - term
    return parts


def pack(
    k_ref, v_ref, q_ref, do_ref, o_ref, norm_ref, kv_ref, out_ref, kv_buf, o_buf, sem, kv_sem
):
    reads = [
        pltpu.make_async_copy(k_ref, kv_buf.at[:ROWS], sem.at[0]),
        pltpu.make_async_copy(v_ref, kv_buf.at[ROWS:], sem.at[1]),
        pltpu.make_async_copy(do_ref, out_ref.at[ROWS : 2 * ROWS], sem.at[2]),
        pltpu.make_async_copy(o_ref, o_buf, sem.at[3]),
        pltpu.make_async_copy(q_ref, out_ref.at[:ROWS], sem.at[4]),
    ]
    for copy in reads:
        copy.start()
    reads[0].wait()
    reads[1].wait()
    writes = [pltpu.make_async_copy(kv_buf, kv_ref.at[i], kv_sem.at[i]) for i in range(PEERS)]
    for copy in writes:
        copy.start()
    reads[2].wait()
    reads[3].wait()
    ones = jnp.ones((8, HEAD), jnp.float32)
    dots = []
    for b in range(2):
        at = slice(b * BLOCK, (b + 1) * BLOCK)
        at2 = slice(ROWS + b * BLOCK, ROWS + (b + 1) * BLOCK)
        prod = jnp.concatenate(
            [
                out_ref[at2, head(h)].astype(jnp.float32) * o_buf[at, head(h)].astype(jnp.float32)
                for h in range(HEADS)
            ],
            0,
        )
        dots.append(
            lax.dot_general(
                ones, prod, NT, precision=lax.Precision.HIGHEST, preferred_element_type=jnp.float32
            )[:1]
        )
    norms = terms_of(norm_ref[...])
    norms = jnp.concatenate(norms + [jnp.zeros((8, WIDTH - 3 * HEAD), jnp.float32)], 1)
    dots = terms_of(jnp.concatenate(dots, 1))
    dots = dots + [jnp.zeros((5, WIDTH), jnp.float32)]
    out_ref[2 * ROWS :] = jnp.concatenate([norms] + dots, 0).astype(jnp.bfloat16)
    reads[4].wait()
    for copy in writes:
        copy.wait()


def stage(
    p0_ref, p1_ref, p2_ref, p3_ref, qs_ref, norm_ref, dot_ref, buf_ref, q_ref, do_ref, sem
):
    copies = [
        pltpu.make_async_copy(p_ref, buf_ref.at[g], sem.at[g])
        for g, p_ref in enumerate((p0_ref, p1_ref, p2_ref, p3_ref))
    ]
    for copy in copies:
        copy.start()
    for g, copy in enumerate(copies):
        copy.wait()
        p_ref = buf_ref.at[g]
        more = p_ref[2 * ROWS :, :].astype(jnp.float32)
        norm = (more[:8, head(0)] + more[:8, head(1)] + more[:8, head(2)]) * LOG2E
        turned = pltpu.roll(norm, BLOCK, 1)
        left = lax.broadcasted_iota(jnp.int32, (1, HEAD), 1) < BLOCK
        dots = more[8:9] + more[9:10] + more[10:11]
        for i in range(2):
            b = 2 * g + i
            dot_ref[b : b + 1, :] = dots[:, i * LANES : (i + 1) * LANES]
            one, two = (norm, turned) if i == 0 else (turned, norm)
            for t in range(HEADS // 2):
                norm_ref[b : b + 1, t * HEAD : (t + 1) * HEAD] = jnp.where(
                    left, one[2 * t : 2 * t + 1], two[2 * t + 1 : 2 * t + 2]
                )
            for h in range(HEADS):
                to = slice(b * LANES + h * BLOCK, b * LANES + (h + 1) * BLOCK)
                q_ref[to, :] = p_ref[i * BLOCK : (i + 1) * BLOCK, head(h)]
                do_ref[to, :] = p_ref[ROWS + i * BLOCK : ROWS + (i + 1) * BLOCK, head(h)]
    copies = [
        pltpu.make_async_copy(q_ref, qs_ref.at[0], sem.at[0]),
        pltpu.make_async_copy(do_ref, qs_ref.at[1], sem.at[1]),
    ]
    for copy in copies:
        copy.start()
    for copy in copies:
        copy.wait()


def terms(
    work_ref, held_ref, place_ref, first_ref, own_ref, norm_ref, dot_ref, kv_ref, qs_ref,
    dqt_ref, dkv_ref, acc_ref, half_ref, q_ref, do_ref, sem,
):
    reads = [
        pltpu.make_async_copy(qs_ref.at[0], q_ref, sem.at[0]),
        pltpu.make_async_copy(qs_ref.at[1], do_ref, sem.at[1]),
    ]
    for copy in reads:
        copy.start()
    acc_ref[...] = jnp.zeros_like(acc_ref)
    dqt_ref[...] = jnp.zeros_like(dqt_ref)
    for copy in reads:
        copy.wait()

    def one(t):
        b, j = work_ref[t], work_ref[SLOTS + t]
        a0 = pl.multiple_of(place_ref[j], BLOCK)
        a1 = pl.multiple_of(place_ref[j + 1], BLOCK)
        rows = pl.ds(pl.multiple_of(b * LANES, LANES), LANES)
        q, do = q_ref[rows, :], do_ref[rows, :]
        k = jnp.concatenate([kv_ref[pl.ds(a0, BLOCK), :], kv_ref[pl.ds(a1, BLOCK), :]], 0)
        v = jnp.concatenate(
            [kv_ref[pl.ds(a0 + ROWS, BLOCK), :], kv_ref[pl.ds(a1 + ROWS, BLOCK), :]], 0
        )
        s = lax.dot_general(k, q, NT, preferred_element_type=jnp.float32)
        dp = lax.dot_general(v, do, NT, preferred_element_type=jnp.float32)
        lane = lax.broadcasted_iota(jnp.int32, (BLOCK, LANES), 0)
        pos = jnp.concatenate([lane + held_ref[j] * BLOCK, lane + held_ref[j + 1] * BLOCK], 0)
        at = pl.ds(b, 1)
        ok = (pos >= first_ref[at, :]) & (pos <= own_ref[at, :])
        w = jnp.where(ok, jnp.exp2(s * (SCALE * LOG2E) - norm_ref[at, :]), 0.0)
        ds = (w * (dp - dot_ref[at, :]) * SCALE).astype(jnp.bfloat16)
        dv = jnp.dot(w.astype(jnp.bfloat16), do, preferred_element_type=jnp.float32)
        dk = jnp.dot(ds, q, preferred_element_type=jnp.float32)
        dqt = lax.dot_general(k, ds, TN, preferred_element_type=jnp.float32)
        return b, a0, a1, dqt, dk, dv

    def two(i, carry):
        for b, a0, a1, dqt, dk, dv in [one(2 * i), one(2 * i + 1)]:
            dqt_ref[pl.ds(pl.multiple_of(b * HEAD, HEAD), HEAD), :] += dqt
            acc_ref[pl.ds(a0, BLOCK), :] += dk[:BLOCK]
            acc_ref[pl.ds(a1, BLOCK), :] += dk[BLOCK:]
            acc_ref[pl.ds(a0 + ROWS, BLOCK), :] += dv[:BLOCK]
            acc_ref[pl.ds(a1 + ROWS, BLOCK), :] += dv[BLOCK:]
        return carry

    lax.fori_loop(0, work_ref[2 * SLOTS], two, 0)
    copies = []
    for i in range(4):
        at = pl.ds(i * 2 * PEERS * BLOCK // 2, PEERS * BLOCK)
        half_ref[at, :] = acc_ref[at, :].astype(jnp.bfloat16)
        copies.append(pltpu.make_async_copy(half_ref.at[at], dkv_ref.at[at], sem.at[i]))
        copies[-1].start()
    for copy in copies:
        copy.wait()


def unstage(dqt_ref, dq0_ref, dq1_ref, dq2_ref, dq3_ref):
    for b in range(8):
        out = (dq0_ref, dq1_ref, dq2_ref, dq3_ref)[b // 2]
        at = slice((b % 2) * BLOCK, (b % 2 + 1) * BLOCK)
        dq = dqt_ref[b * HEAD : (b + 1) * HEAD, :].T.astype(out.dtype)
        for h in range(HEADS):
            out[at, head(h)] = dq[h * BLOCK : (h + 1) * BLOCK]


def total(got_ref, k_ref, v_ref):
    both = got_ref[0].astype(jnp.float32)
    for i in range(1, PEERS):
        both = both + got_ref[i].astype(jnp.float32)
    k_ref[...] = both[:ROWS].astype(jnp.bfloat16)
    v_ref[...] = both[ROWS:].astype(jnp.bfloat16)


def plan(doc_lengths, block_order, yh, xh, xl, core):
    docs, nblk = doc_lengths.shape[0], block_order.shape[0]
    nheld = nblk // 4
    upto = jnp.arange(docs)[:, None] >= jnp.arange(docs)[None, :]
    ends = jnp.sum(jnp.where(upto, doc_lengths[None, :], 0), axis=1)
    blocks = jnp.arange(nblk, dtype=jnp.int32)
    held_here = ((blocks // 2) % 2 == core) & ((blocks // 4) % 2 == xl)
    place = (blocks // 8) * (2 * ROWS) + (blocks % 2) * BLOCK
    before = held_here[None, :] & (block_order[None, :] < block_order[:, None])
    rank = jnp.sum(before.astype(jnp.int32), axis=1)
    slots = jnp.arange(nheld + 8, dtype=jnp.int32)
    hit = held_here[None, :] & (rank[None, :] == slots[:, None])
    held = jnp.sum(jnp.where(hit, block_order[None, :], 0), axis=1)
    held = jnp.where(slots < nheld, held, nblk)
    place = jnp.sum(jnp.where(hit, place[None, :], 0), axis=1)
    x, turn = 2 * xh + xl, 1 - 2 * core
    owners = 8 * yh + jnp.stack(
        [
            2 * x + core,
            2 * x + 1 - core,
            2 * ((x + turn) % 4) + core,
            2 * ((x - turn) % 4) + 1 - core,
        ]
    )
    stored = (2 * owners[:, None] + jnp.arange(2)[None, :]).reshape(8)
    mine = jnp.sum(jnp.where(stored[:, None] == blocks[None, :], block_order[None, :], 0), axis=1)
    pos = mine[:, None] * BLOCK + jnp.arange(BLOCK, dtype=jnp.int32)[None, :]
    first = jnp.max(jnp.where(ends[None, None, :] <= pos[:, :, None], ends[None, None, :], 0), axis=2)
    begin = jnp.sum((held[None, :] < (first[:, :1] >> 6)).astype(jnp.int32), axis=1)
    until = jnp.sum((held[None, :] <= mine[:, None]).astype(jnp.int32), axis=1)
    pairs = (until - begin + 1) >> 1
    eight = jnp.arange(8)
    stops = jnp.sum(jnp.where(eight[:, None] >= eight[None, :], pairs[None, :], 0), axis=1)
    place_in = jnp.arange(SLOTS, dtype=jnp.int32)
    done = stops[None, :] <= place_in[:, None]
    of = jnp.sum(done.astype(jnp.int32), axis=1)
    this = of[:, None] == eight[None, :]
    at = jnp.sum(jnp.where(this, begin[None, :] - 2 * (stops - pairs)[None, :], 0), axis=1)
    at = jnp.where(of < 8, at + 2 * place_in, nheld)
    work = jnp.concatenate([jnp.minimum(of, 7), at, (stops[-1:] + 1) >> 1])
    return work, held, place, jnp.tile(first, (1, HEADS)), jnp.tile(pos, (1, HEADS))


def on_device(queries, keys, values, attn_out, grad_out, log_norm, doc_lengths, block_order):
    f32, bf16 = jnp.float32, jnp.bfloat16
    shape = jax.ShapeDtypeStruct
    place = [lax.axis_index(a) for a in CTX]
    dma = pltpu.SemaphoreType.DMA

    swap = [(0, 1), (1, 0)]
    there = [(2 * ((i + 1) % 4), 2 * i) for i in range(4)]
    there += [(2 * i + 1, 2 * ((i + 1) % 4) + 1) for i in range(4)]
    back = [(j, i) for i, j in there]
    across = [(2 * i, 2 * ((i - 1) % 4) + 1) for i in range(4)]
    across += [(2 * i + 1, 2 * ((i + 1) % 4)) for i in range(4)]
    spread, p0 = call(
        pack,
        (pltpu.HBM((PEERS, 2 * ROWS, HEAD), bf16), shape((2 * ROWS + EXTRA, WIDTH), bf16)),
        [HBM] * 5 + [VMEM],
        (HBM, VMEM),
        *map(in_hbm, (keys, values, queries, grad_out, attn_out)), log_norm,
        scratch=[
            pltpu.VMEM((2 * ROWS, HEAD), bf16),
            pltpu.VMEM((ROWS, WIDTH), bf16),
            dma((5,)),
            dma((PEERS,)),
        ],
    )
    p2 = lax.ppermute(p0, NEXT, there)
    kv = lax.all_to_all(spread, KEEPERS, 0, 0, tiled=True)
    p1 = lax.ppermute(p0, "core", swap)
    p3 = lax.ppermute(p2, "core", swap)
    listed = plan(doc_lengths, block_order, *place)
    p3, (work, held, at, first, own) = lax.optimization_barrier((p3, listed))
    qs, norm, dot = call(
        stage,
        (pltpu.HBM((2, 8 * LANES, HEAD), bf16),) + (shape((8, LANES), f32),) * 2,
        [HBM] * 4,
        (HBM, VMEM, VMEM),
        *map(in_hbm, (p0, p1, p2, p3)),
        scratch=[
            pltpu.VMEM((4, 2 * ROWS + EXTRA, WIDTH), bf16),
            pltpu.VMEM((8 * LANES, HEAD), bf16),
            pltpu.VMEM((8 * LANES, HEAD), bf16),
            dma((4,)),
        ],
    )
    nkeys = 2 * PEERS * ROWS
    dqt, dkv = call(
        terms,
        (shape((8 * HEAD, LANES), f32), pltpu.HBM((nkeys, HEAD), bf16)),
        [SMEM] * 3 + [VMEM] * 5 + [HBM],
        (VMEM, HBM),
        work, held, at, first, own, norm, dot, kv.reshape(nkeys, HEAD), in_hbm(qs),
        scratch=[
            pltpu.VMEM((nkeys, HEAD), f32),
            pltpu.VMEM((nkeys, HEAD), bf16),
            pltpu.VMEM((8 * LANES, HEAD), bf16),
            pltpu.VMEM((8 * LANES, HEAD), bf16),
            dma((4,)),
        ],
    )
    got = lax.all_to_all(dkv.reshape(PEERS, 2 * ROWS, HEAD), KEEPERS, 0, 0, tiled=True)
    dq0, *others = call(
        unstage,
        (shape((ROWS, WIDTH), f32),) + (shape((ROWS, WIDTH), bf16),) * 3,
        [VMEM],
        (VMEM,) * 4,
        dqt,
    )
    routes = (("core", swap), (NEXT, back), (NEXT, across))
    parts = [lax.ppermute(x, axes, route) for x, (axes, route) in zip(others, routes)]
    grad_q = (dq0 + sum(x.astype(f32) for x in parts)).astype(bf16)
    grad_k, grad_v = call(total, (shape((ROWS, HEAD), bf16),) * 2, [VMEM], (VMEM,) * 2, got)
    return grad_q, grad_k, grad_v


def solution(mesh):
    parts = Mesh(
        mesh.devices.reshape(2, 4, 2, 2, 2, 8), ("dp", "yh", "xh", "xl", "core", "tensor")
    )
    seq = ("dp",) + CTX
    wide = P(seq, "tensor")
    return jax.shard_map(
        on_device,
        mesh=parts,
        in_specs=(wide,) * 5 + (P("tensor", seq), P("dp"), P("dp")),
        out_specs=(wide, wide, wide),
        check_vma=False,
    )
```

time: 70.6 us -> 67.6 us (0.958)
  the two profiles are of different devices: /device:TPU:384 before, /device:TPU:1 now
where the time goes in v3:
time: 67.6 us; the launch traced here: 66.5 us
  starting transfers between devices  31.5 us (47%)
  Pallas kernels  13.7 us (20%)
  waiting for transfers between devices  11.4 us (17%)
  other arithmetic  5.21 us (8%)
  local copies, waits for them, and re-layouts  3.12 us (5%)
  between operations  1.48 us (2%)
    pallas_call x5, Pallas kernels, call(): pl.pallas_call(kernel, out_shape=out, in_specs=ins, out_specs=outs, scrat...  13.7 us
    ppermute x3, starting transfers between devices, on_device(): lax.ppermute(x, axes, route)  10.5 us
    ppermute x1, starting transfers between devices, on_device(): p1 = lax.ppermute(p0, 'core', swap)  8.79 us
    ppermute x3, waiting for transfers between devices, on_device(): lax.ppermute(x, axes, route)  6.71 us
    all_to_all x1, starting transfers between devices, on_device(): kv = lax.all_to_all(spread, KEEPERS, 0, 0, tiled=True)  4.82 us
    all_to_all x1, starting transfers between devices, on_device(): lax.all_to_all(dkv.reshape(PEERS, 2 * ROWS, HEAD), KEEPERS, 0, 0, tiled=T...  3.5 us
    all_to_all x1, waiting for transfers between devices, on_device(): kv = lax.all_to_all(spread, KEEPERS, 0, 0, tiled=True)  2.65 us
    unnamed x10, local copies, waits for them, and re-layouts  2.29 us
  transfers between devices with their start and end apart: 8, of which 5 were waited for; matrix products, arithmetic and copies ran while one was open for 9% of the time, Pallas kernels for 5%

profile of v3, /device:TPU:1, one launch (start us, length us, event | category | flops | bytes accessed | tf_op | source)
XLA Modules:
  0.0 66.5 jit_solution(16212356327754255540)
XLA Ops:
  0.6 0.0 copy-start.1
  0.6 0.7 %copy-done.1 = f32[8,128]{1,0:T(8,128)S(1)} copy-done((f32[8,128]{1,0:T(8,128)S(1)}, f32[8,128]{1,0:T(8,128)}, u32[]{:S(2)}) %copy-start.1) | copy-done | bytes 4120
  1.3 1.7 %pack.1 = (bf16[8,256,128]{2,1,0:T(8,128)(2,1)}, bf16[272,1024]{1,0:T(8,128)(2,1)S(1)}) custom-call(bf16[128,128]{1,0:T(8,128)(2,1)} %k_ref.1, bf16[128,128]{1,0:T(8,128)(2,1)} %v_ref.1, bf16[128,1024]{1,0:T(8,128)(2,1)} %q_ref.1, bf16[128,1024]{1,0:T(8,128)(2,1)} %do_ref.1, bf16[128,1024]{1,0:T(8,128)(2,1)} %o_ref.1, f32[8,128]{1,0:T(8,128)S(1)} %copy-done.1), custom_call_target="tpu_custom_call" | custom-call | tf_op jit(solution)/shard_map/pack/pallas_call | solution.py:41
  3.1 0.0 copy-start
  3.1 8.8 %collective-permute-start.2 = (bf16[272,1024]{1,0:T(8,128)(2,1)S(1)}, bf16[272,1024]{1,0:T(8,128)(2,1)S(1)}, u32[]{:S(2)}, u32[]{:S(2)}) collective-permute-start(bf16[272,1024]{1,0:T(8,128)(2,1)S(1)} %get-tuple-element.22.p0_ref), channel_id=1, source_target_pairs={{0,8},{8,0},{1,9},{9,1},{2,10},{10,2},{3,11},{11,3},{4,12},{12,4},... | collective-permute-start | bytes 1671176 | tf_op jit(solution)/shard_map/ppermute | solution.py:291
  11.9 1.9 %collective-permute-start = (bf16[272,1024]{1,0:T(8,128)(2,1)S(1)}, bf16[272,1024]{1,0:T(8,128)(2,1)S(1)}, u32[]{:S(2)}, u32[]{:S(2)}) collective-permute-start(bf16[272,1024]{1,0:T(8,128)(2,1)S(1)} %get-tuple-element.22.p0_ref), channel_id=1, source_target_pairs={{16,0},{32,16},{48,32},{0,48},{8,24},{24,40},{40,56},{56,8},{17,1}... | collective-permute-start | bytes 1671176 | tf_op jit(solution)/shard_map/ppermute | solution.py:289
  13.8 4.8 %all-to-all-start = ((bf16[8,256,128]{2,1,0:T(8,128)(2,1)}), bf16[8,256,128]{2,1,0:T(8,128)(2,1)S(1)}, u32[]{:S(2)}, u32[]{:S(2)}) async-start(bf16[8,256,128]{2,1,0:T(8,128)(2,1)} %get-tuple-element.31), calls=%async_computation | async-start | bytes 1048576 | tf_op jit(solution)/shard_map/all_to_all | solution.py:290
  18.7 0.8 %select_reduce_fusion.3 = s32[16]{0:T(128)S(1)} fusion(s32[16]{0:T(128)} %param.14), kind=kLoop, calls=%fused_computation.7 | loop fusion | flops 752 | bytes 128 | tf_op jit(solution)/shard_map/reduce_sum | solution.py:225
  19.4 0.9 %convert_reduce_fusion = s32[64]{0:T(128)S(1)} fusion(s32[64]{0:T(128)} %param.15, pred[64]{0:T(512)(128)(4,1)S(1)} %compare_and_fusion), kind=kLoop, calls=%fused_computation.2 | loop fusion | flops 16320 | bytes 576 | tf_op jit(solution)/shard_map/reduce_sum | solution.py:230
  20.4 0.8 %select_reduce_fusion.1 = (s32[24]{0:T(128)S(1)}, s32[24]{0:T(128)S(1)}) fusion(s32[64]{0:T(128)S(1)} %fusion.2, s32[64]{0:T(128)S(1)} %convert_reduce_fusion, pred[64]{0:T(512)(128)(4,1)S(1)} %compare_and_fusion, s32[64]{0:T(128)} %param.15), kind=kLoop, calls=%fused_computation.3 | loop fusion | flops 9168 | bytes 1024 | tf_op jit(solution)/shard_map/reduce_sum | solution.py:235
  21.2 0.1 fusion.7
  21.2 0.1 iota_add_fusion.1
  21.3 0.1 add.162
  21.4 0.8 %select_reduce_fusion.6 = s32[8]{0:T(128)S(1)} fusion(s32[64]{0:T(128)} %param.15, s32[8]{0:T(128)S(1)} %add.162), kind=kLoop, calls=%fused_computation.18 | loop fusion | flops 1528 | bytes 320 | tf_op jit(solution)/shard_map/reduce_sum | solution.py:246
  22.2 0.1 iota_add_fusion
  22.3 0.1 select_reduce_fusion
  22.4 0.1 shift-right-arithmetic_reduce_fusion
  22.5 0.2 convert_reduce_fusion.2
  22.8 0.1 select_reduce_fusion.5
  22.9 0.6 slice.7
  24.1 0.1 tile.9.first_ref
  24.2 0.1 tile.21.own_ref
  24.3 0.5 collective-permute-done.p2_ref
  24.8 0.0 copy-start.3
  24.8 2.0 %collective-permute-start.1 = (bf16[272,1024]{1,0:T(8,128)(2,1)S(1)}, bf16[272,1024]{1,0:T(8,128)(2,1)S(1)}, u32[]{:S(2)}, u32[]{:S(2)}) collective-permute-start(bf16[272,1024]{1,0:T(8,128)(2,1)S(1)} %collective-permute-done.p2_ref), channel_id=1, source_target_pairs={{0,8},{8,0},{1,9},{9,1},{2,10},{10,2},{3,11},{11,3},{4,12},{12,4},... | collective-permute-start | bytes 1671176 | tf_op jit(solution)/shard_map/ppermute | solution.py:292
  26.7 0.1 convert_reduce_fusion.1
  26.8 0.1 select_reduce_fusion.4
  26.9 0.1 pad_add_fusion.work_ref
  27.0 1.6 %collective-permute-done.1.p3_ref = bf16[272,1024]{1,0:T(8,128)(2,1)S(1)} collective-permute-done((bf16[272,1024]{1,0:T(8,128)(2,1)S(1)}, bf16[272,1024]{1,0:T(8,128)(2,1)S(1)}, u32[]{:S(2)}, u32[]{:S(2)}) %collective-permute-start.1) | collective-permute-done | bytes 557088 | tf_op jit(solution)/shard_map/ppermute | solution.py:292
  28.6 0.0 copy-start.4
  28.6 0.0 collective-permute-done.2.p1_ref
  28.6 0.0 copy-done
  28.6 0.0 copy-done.3
  28.6 0.8 %copy-done.4 = bf16[272,1024]{1,0:T(8,128)(2,1)} copy-done((bf16[272,1024]{1,0:T(8,128)(2,1)}, bf16[272,1024]{1,0:T(8,128)(2,1)S(1)}, u32[]{:S(2)}) %copy-start.4) | copy-done | bytes 557080
  29.4 0.0 copy-start.2
  29.4 0.8 %copy-done.2 = bf16[272,1024]{1,0:T(8,128)(2,1)} copy-done((bf16[272,1024]{1,0:T(8,128)(2,1)}, bf16[272,1024]{1,0:T(8,128)(2,1)S(1)}, u32[]{:S(2)}) %copy-start.2) | copy-done | bytes 557080
  30.2 3.0 %stage.1 = (bf16[2,4096,128]{2,1,0:T(8,128)(2,1)}, f32[8,512]{1,0:T(8,128)S(1)}, f32[8,512]{1,0:T(8,128)S(1)}) custom-call(bf16[272,1024]{1,0:T(8,128)(2,1)} %copy-done, bf16[272,1024]{1,0:T(8,128)(2,1)} %copy-done.2, bf16[272,1024]{1,0:T(8,128)(2,1)} %copy-done.3, bf16[272,1024]{1,0:T(8,128)(2,1)} %copy-done.4), custom_call_target="tpu_custom_call" | custom-call | tf_op jit(solution)/shard_map/stage/pallas_call | solution.py:41
  33.3 2.6 %all-to-all-done = bf16[8,256,128]{2,1,0:T(8,128)(2,1)S(1)} async-done(((bf16[8,256,128]{2,1,0:T(8,128)(2,1)}), bf16[8,256,128]{2,1,0:T(8,128)(2,1)S(1)}, u32[]{:S(2)}, u32[]{:S(2)}) %all-to-all-start) | async-done | bytes 524320 | tf_op jit(solution)/shard_map/all_to_all | solution.py:290
  35.9 7.9 %terms.1 = (f32[1024,512]{1,0:T(8,128)S(1)}, bf16[2048,128]{1,0:T(8,128)(2,1)}) custom-call(s32[145]{0:T(256)S(1)} %pad_add_fusion.work_ref, s32[24]{0:T(128)S(1)} %compare_select_fusion.5.held_ref, s32[24]{0:T(128)S(1)} %get-tuple-element.25.place_ref, s32[8,512]{1,0:T(8,128)S(1)} %tile.9.first_ref, s32[8,512]{1,0:T(8,128)S(1)} %tile.21.own_ref, ...), custom_call_target="tpu_custom_call" | custom-call | tf_op jit(solution)/shard_map/terms/pallas_call | solution.py:41
  43.8 3.5 %all-to-all-start.1 = ((bf16[8,256,128]{2,1,0:T(8,128)(2,1)}), bf16[8,256,128]{2,1,0:T(8,128)(2,1)S(1)}, u32[]{:S(2)}, u32[]{:S(2)}) async-start(bf16[8,256,128]{2,1,0:T(8,128)(2,1)} %bitcast.7), calls=%async_computation.1 | async-start | bytes 1048576 | tf_op jit(solution)/shard_map/all_to_all | solution.py:323
  47.3 0.4 unstage.1
  47.7 1.9 %collective-permute-start.3 = (bf16[128,1024]{1,0:T(8,128)(2,1)S(1)}, bf16[128,1024]{1,0:T(8,128)(2,1)S(1)}, u32[]{:S(2)}, u32[]{:S(2)}) collective-permute-start(bf16[128,1024]{1,0:T(8,128)(2,1)S(1)} %get-tuple-element.35), channel_id=1, source_target_pairs={{0,8},{8,0},{1,9},{9,1},{2,10},{10,2},{3,11},{11,3},{4,12},{12,4},... | collective-permute-start | bytes 786440 | tf_op jit(solution)/shard_map/ppermute | solution.py:332
  49.6 6.7 %collective-permute-start.4 = (bf16[128,1024]{1,0:T(8,128)(2,1)S(1)}, bf16[128,1024]{1,0:T(8,128)(2,1)S(1)}, u32[]{:S(2)}, u32[]{:S(2)}) collective-permute-start(bf16[128,1024]{1,0:T(8,128)(2,1)S(1)} %get-tuple-element.36), channel_id=1, source_target_pairs={{0,16},{16,32},{32,48},{48,0},{24,8},{40,24},{56,40},{8,56},{1,17}... | collective-permute-start | bytes 786440 | tf_op jit(solution)/shard_map/ppermute | solution.py:332
  56.4 1.9 %collective-permute-start.5 = (bf16[128,1024]{1,0:T(8,128)(2,1)S(1)}, bf16[128,1024]{1,0:T(8,128)(2,1)S(1)}, u32[]{:S(2)}, u32[]{:S(2)}) collective-permute-start(bf16[128,1024]{1,0:T(8,128)(2,1)S(1)} %get-tuple-element.37), channel_id=1, source_target_pairs={{0,56},{16,8},{32,24},{48,40},{8,16},{24,32},{40,48},{56,0},{1,57}... | collective-permute-start | bytes 786440 | tf_op jit(solution)/shard_map/ppermute | solution.py:332
  58.3 0.0 collective-permute-done.3
  58.3 5.0 %collective-permute-done.4 = bf16[128,1024]{1,0:T(8,128)(2,1)S(1)} collective-permute-done((bf16[128,1024]{1,0:T(8,128)(2,1)S(1)}, bf16[128,1024]{1,0:T(8,128)(2,1)S(1)}, u32[]{:S(2)}, u32[]{:S(2)}) %collective-permute-start.4) | collective-permute-done | bytes 262176 | tf_op jit(solution)/shard_map/ppermute | solution.py:332
  63.3 1.7 %collective-permute-done.5 = bf16[128,1024]{1,0:T(8,128)(2,1)S(1)} collective-permute-done((bf16[128,1024]{1,0:T(8,128)(2,1)S(1)}, bf16[128,1024]{1,0:T(8,128)(2,1)S(1)}, u32[]{:S(2)}, u32[]{:S(2)}) %collective-permute-start.5) | collective-permute-done | bytes 262176 | tf_op jit(solution)/shard_map/ppermute | solution.py:332
  65.0 0.8 %add_convert_fusion = bf16[128,1024]{1,0:T(8,128)(2,1)} fusion(f32[128,1024]{1,0:T(8,128)S(1)} %get-tuple-element.34, bf16[128,1024]{1,0:T(8,128)(2,1)S(1)} %collective-permute-done.5, bf16[128,1024]{1,0:T(8,128)(2,1)S(1)} %collective-permute-done.4, bf16[128,1024]{1,0:T(8,128)(2,1)S(1)} %collective-permute-done.3), kind=kLoop, calls=%fused_computation | loop fusion | flops 917504 | bytes 1572864 | tf_op jit(solution)/shard_map/convert_element_type | solution.py:333
  65.8 0.0 all-to-all-done.1.got_ref
  65.8 0.7 %total.1 = (bf16[128,128]{1,0:T(8,128)(2,1)}, bf16[128,128]{1,0:T(8,128)(2,1)}) custom-call(bf16[8,256,128]{2,1,0:T(8,128)(2,1)S(1)} %all-to-all-done.1.got_ref), custom_call_target="tpu_custom_call" | custom-call | tf_op jit(solution)/shard_map/total/pallas_call | solution.py:41
  (9 shorter events, 0.1 us)
Async XLA Ops:
  0.6 0.7 %copy-start.1 = (f32[8,128]{1,0:T(8,128)S(1)}, f32[8,128]{1,0:T(8,128)}, u32[]{:S(2)}) copy-start(f32[8,128]{1,0:T(8,128)} %norm_ref.1) | copy-start | bytes 12292
  3.1 25.5 %copy-start = (bf16[272,1024]{1,0:T(8,128)(2,1)}, bf16[272,1024]{1,0:T(8,128)(2,1)S(1)}, u32[]{:S(2)}) copy-start(bf16[272,1024]{1,0:T(8,128)(2,1)S(1)} %get-tuple-element.22.p0_ref) | copy-start | bytes 1671172
  3.1 25.5 %collective-permute-start.2 = (bf16[272,1024]{1,0:T(8,128)(2,1)S(1)}, bf16[272,1024]{1,0:T(8,128)(2,1)S(1)}, u32[]{:S(2)}, u32[]{:S(2)}) collective-permute-start(bf16[272,1024]{1,0:T(8,128)(2,1)S(1)} %get-tuple-element.22.p0_ref), channel_id=1, source_target_pairs={{0,8},{8,0},{1,9},{9,1},{2,10},{10,2},{3,11},{11,3},{4,12},{12,4},... | collective-permute-start | bytes 1671176 | tf_op jit(solution)/shard_map/ppermute | solution.py:291
  11.9 12.9 %collective-permute-start = (bf16[272,1024]{1,0:T(8,128)(2,1)S(1)}, bf16[272,1024]{1,0:T(8,128)(2,1)S(1)}, u32[]{:S(2)}, u32[]{:S(2)}) collective-permute-start(bf16[272,1024]{1,0:T(8,128)(2,1)S(1)} %get-tuple-element.22.p0_ref), channel_id=1, source_target_pairs={{16,0},{32,16},{48,32},{0,48},{8,24},{24,40},{40,56},{56,8},{17,1}... | collective-permute-start | bytes 1671176 | tf_op jit(solution)/shard_map/ppermute | solution.py:289
  13.8 22.1 %all-to-all-start = ((bf16[8,256,128]{2,1,0:T(8,128)(2,1)}), bf16[8,256,128]{2,1,0:T(8,128)(2,1)S(1)}, u32[]{:S(2)}, u32[]{:S(2)}) async-start(bf16[8,256,128]{2,1,0:T(8,128)(2,1)} %get-tuple-element.31), calls=%async_computation | async-start | bytes 1048576 | tf_op jit(solution)/shard_map/all_to_all | solution.py:290
  24.8 3.9 %copy-start.3 = (bf16[272,1024]{1,0:T(8,128)(2,1)}, bf16[272,1024]{1,0:T(8,128)(2,1)S(1)}, u32[]{:S(2)}) copy-start(bf16[272,1024]{1,0:T(8,128)(2,1)S(1)} %collective-permute-done.p2_ref) | copy-start | bytes 1671172
  24.8 3.8 %collective-permute-start.1 = (bf16[272,1024]{1,0:T(8,128)(2,1)S(1)}, bf16[272,1024]{1,0:T(8,128)(2,1)S(1)}, u32[]{:S(2)}, u32[]{:S(2)}) collective-permute-start(bf16[272,1024]{1,0:T(8,128)(2,1)S(1)} %collective-permute-done.p2_ref), channel_id=1, source_target_pairs={{0,8},{8,0},{1,9},{9,1},{2,10},{10,2},{3,11},{11,3},{4,12},{12,4},... | collective-permute-start | bytes 1671176 | tf_op jit(solution)/shard_map/ppermute | solution.py:292
  28.6 0.8 %copy-start.4 = (bf16[272,1024]{1,0:T(8,128)(2,1)}, bf16[272,1024]{1,0:T(8,128)(2,1)S(1)}, u32[]{:S(2)}) copy-start(bf16[272,1024]{1,0:T(8,128)(2,1)S(1)} %collective-permute-done.1.p3_ref) | copy-start | bytes 1671172
  29.4 0.8 %copy-start.2 = (bf16[272,1024]{1,0:T(8,128)(2,1)}, bf16[272,1024]{1,0:T(8,128)(2,1)S(1)}, u32[]{:S(2)}) copy-start(bf16[272,1024]{1,0:T(8,128)(2,1)S(1)} %collective-permute-done.2.p1_ref) | copy-start | bytes 1671172
  43.8 22.1 %all-to-all-start.1 = ((bf16[8,256,128]{2,1,0:T(8,128)(2,1)}), bf16[8,256,128]{2,1,0:T(8,128)(2,1)S(1)}, u32[]{:S(2)}, u32[]{:S(2)}) async-start(bf16[8,256,128]{2,1,0:T(8,128)(2,1)} %bitcast.7), calls=%async_computation.1 | async-start | bytes 1048576 | tf_op jit(solution)/shard_map/all_to_all | solution.py:323
  47.7 10.6 %collective-permute-start.3 = (bf16[128,1024]{1,0:T(8,128)(2,1)S(1)}, bf16[128,1024]{1,0:T(8,128)(2,1)S(1)}, u32[]{:S(2)}, u32[]{:S(2)}) collective-permute-start(bf16[128,1024]{1,0:T(8,128)(2,1)S(1)} %get-tuple-element.35), channel_id=1, source_target_pairs={{0,8},{8,0},{1,9},{9,1},{2,10},{10,2},{3,11},{11,3},{4,12},{12,4},... | collective-permute-start | bytes 786440 | tf_op jit(solution)/shard_map/ppermute | solution.py:332
  49.6 13.6 %collective-permute-start.4 = (bf16[128,1024]{1,0:T(8,128)(2,1)S(1)}, bf16[128,1024]{1,0:T(8,128)(2,1)S(1)}, u32[]{:S(2)}, u32[]{:S(2)}) collective-permute-start(bf16[128,1024]{1,0:T(8,128)(2,1)S(1)} %get-tuple-element.36), channel_id=1, source_target_pairs={{0,16},{16,32},{32,48},{48,0},{24,8},{40,24},{56,40},{8,56},{1,17}... | collective-permute-start | bytes 786440 | tf_op jit(solution)/shard_map/ppermute | solution.py:332
  56.4 8.6 %collective-permute-start.5 = (bf16[128,1024]{1,0:T(8,128)(2,1)S(1)}, bf16[128,1024]{1,0:T(8,128)(2,1)S(1)}, u32[]{:S(2)}, u32[]{:S(2)}) collective-permute-start(bf16[128,1024]{1,0:T(8,128)(2,1)S(1)} %get-tuple-element.37), channel_id=1, source_target_pairs={{0,56},{16,8},{32,24},{48,40},{8,16},{24,32},{40,48},{56,0},{1,57}... | collective-permute-start | bytes 786440 | tf_op jit(solution)/shard_map/ppermute | solution.py:332

commit v4 on v3

--- a/solution.py
+++ b/solution.py
@@ -58,25 +58,33 @@
     return parts
 
 
-def pack(
-    k_ref, v_ref, q_ref, do_ref, o_ref, norm_ref, kv_ref, out_ref, kv_buf, o_buf, sem, kv_sem
-):
+def spread(k_ref, v_ref, kv_ref, kv_buf, sem, kv_sem):
     reads = [
         pltpu.make_async_copy(k_ref, kv_buf.at[:ROWS], sem.at[0]),
         pltpu.make_async_copy(v_ref, kv_buf.at[ROWS:], sem.at[1]),
-        pltpu.make_async_copy(do_ref, out_ref.at[ROWS : 2 * ROWS], sem.at[2]),
-        pltpu.make_async_copy(o_ref, o_buf, sem.at[3]),
-        pltpu.make_async_copy(q_ref, out_ref.at[:ROWS], sem.at[4]),
     ]
     for copy in reads:
         copy.start()
-    reads[0].wait()
-    reads[1].wait()
+    for copy in reads:
+        copy.wait()
     writes = [pltpu.make_async_copy(kv_buf, kv_ref.at[i], kv_sem.at[i]) for i in range(PEERS)]
     for copy in writes:
         copy.start()
-    reads[2].wait()
-    reads[3].wait()
+    for copy in writes:
+        copy.wait()
+
+
+def pack(q_ref, do_ref, o_ref, norm_ref, out_ref, o_buf, norm_buf, sem):
+    reads = [
+        pltpu.make_async_copy(do_ref, out_ref.at[ROWS : 2 * ROWS], sem.at[0]),
+        pltpu.make_async_copy(o_ref, o_buf, sem.at[1]),
+        pltpu.make_async_copy(norm_ref, norm_buf, sem.at[2]),
+        pltpu.make_async_copy(q_ref, out_ref.at[:ROWS], sem.at[3]),
+    ]
+    for copy in reads:
+        copy.start()
+    for copy in reads[:3]:
+        copy.wait()
     ones = jnp.ones((8, HEAD), jnp.float32)
     dots = []
     for b in range(2):
@@ -94,28 +102,16 @@
                 ones, prod, NT, precision=lax.Precision.HIGHEST, preferred_element_type=jnp.float32
             )[:1]
         )
-    norms = terms_of(norm_ref[...])
+    norms = terms_of(norm_buf[...])
     norms = jnp.concatenate(norms + [jnp.zeros((8, WIDTH - 3 * HEAD), jnp.float32)], 1)
     dots = terms_of(jnp.concatenate(dots, 1))
     dots = dots + [jnp.zeros((5, WIDTH), jnp.float32)]
     out_ref[2 * ROWS :] = jnp.concatenate([norms] + dots, 0).astype(jnp.bfloat16)
-    reads[4].wait()
-    for copy in writes:
-        copy.wait()
-
-
-def stage(
-    p0_ref, p1_ref, p2_ref, p3_ref, qs_ref, norm_ref, dot_ref, buf_ref, q_ref, do_ref, sem
-):
-    copies = [
-        pltpu.make_async_copy(p_ref, buf_ref.at[g], sem.at[g])
-        for g, p_ref in enumerate((p0_ref, p1_ref, p2_ref, p3_ref))
-    ]
-    for copy in copies:
-        copy.start()
-    for g, copy in enumerate(copies):
-        copy.wait()
-        p_ref = buf_ref.at[g]
+    reads[3].wait()
+
+
+def stage(p_refs, q_ref, do_ref, norm_ref, dot_ref):
+    for g, p_ref in enumerate(p_refs):
         more = p_ref[2 * ROWS :, :].astype(jnp.float32)
         norm = (more[:8, head(0)] + more[:8, head(1)] + more[:8, head(2)]) * LOG2E
         turned = pltpu.roll(norm, BLOCK, 1)
@@ -133,30 +129,15 @@
                 to = slice(b * LANES + h * BLOCK, b * LANES + (h + 1) * BLOCK)
                 q_ref[to, :] = p_ref[i * BLOCK : (i + 1) * BLOCK, head(h)]
                 do_ref[to, :] = p_ref[ROWS + i * BLOCK : ROWS + (i + 1) * BLOCK, head(h)]
-    copies = [
-        pltpu.make_async_copy(q_ref, qs_ref.at[0], sem.at[0]),
-        pltpu.make_async_copy(do_ref, qs_ref.at[1], sem.at[1]),
-    ]
-    for copy in copies:
-        copy.start()
-    for copy in copies:
-        copy.wait()
 
 
 def terms(
-    work_ref, held_ref, place_ref, first_ref, own_ref, norm_ref, dot_ref, kv_ref, qs_ref,
-    dqt_ref, dkv_ref, acc_ref, half_ref, q_ref, do_ref, sem,
+    work_ref, held_ref, place_ref, first_ref, own_ref, p0_ref, p1_ref, p2_ref, p3_ref, kv_ref,
+    dqs_ref, dkv_ref, acc_ref, half_ref, dqt_ref, q_ref, do_ref, norm_ref, dot_ref, sem,
 ):
-    reads = [
-        pltpu.make_async_copy(qs_ref.at[0], q_ref, sem.at[0]),
-        pltpu.make_async_copy(qs_ref.at[1], do_ref, sem.at[1]),
-    ]
-    for copy in reads:
-        copy.start()
     acc_ref[...] = jnp.zeros_like(acc_ref)
     dqt_ref[...] = jnp.zeros_like(dqt_ref)
-    for copy in reads:
-        copy.wait()
+    stage((p0_ref, p1_ref, p2_ref, p3_ref), q_ref, do_ref, norm_ref, dot_ref)
 
     def one(t):
         b, j = work_ref[t], work_ref[SLOTS + t]
@@ -191,7 +172,8 @@
         return carry
 
     lax.fori_loop(0, work_ref[2 * SLOTS], two, 0)
-    copies = []
+    copies = [pltpu.make_async_copy(dqt_ref, dqs_ref, sem.at[4])]
+    copies[0].start()
     for i in range(4):
         at = pl.ds(i * 2 * PEERS * BLOCK // 2, PEERS * BLOCK)
         half_ref[at, :] = acc_ref[at, :].astype(jnp.bfloat16)
@@ -201,7 +183,14 @@
         copy.wait()
 
 
-def unstage(dqt_ref, dq0_ref, dq1_ref, dq2_ref, dq3_ref):
+def unstage(dqs_ref, dq0_ref, dq1_ref, dq2_ref, dq3_ref, dqt_ref, sem):
+    copies = []
+    for b in (2, 3, 4, 5, 6, 7, 0, 1):
+        at = slice(b * HEAD, (b + 1) * HEAD)
+        copies.append(pltpu.make_async_copy(dqs_ref.at[at], dqt_ref.at[at], sem.at[b]))
+        copies[-1].start()
+    for copy in copies:
+        copy.wait()
     for b in range(8):
         out = (dq0_ref, dq1_ref, dq2_ref, dq3_ref)[b // 2]
         at = slice((b % 2) * BLOCK, (b % 2 + 1) * BLOCK)
@@ -273,60 +262,53 @@
     back = [(j, i) for i, j in there]
     across = [(2 * i, 2 * ((i - 1) % 4) + 1) for i in range(4)]
     across += [(2 * i + 1, 2 * ((i + 1) % 4)) for i in range(4)]
-    spread, p0 = call(
+    sent = call(
+        spread,
+        pltpu.HBM((PEERS, 2 * ROWS, HEAD), bf16),
+        [HBM] * 2,
+        HBM,
+        in_hbm(keys), in_hbm(values),
+        scratch=[pltpu.VMEM((2 * ROWS, HEAD), bf16), dma((2,)), dma((PEERS,))],
+    )
+    kv = lax.all_to_all(sent, KEEPERS, 0, 0, tiled=True)
+    p0 = call(
         pack,
-        (pltpu.HBM((PEERS, 2 * ROWS, HEAD), bf16), shape((2 * ROWS + EXTRA, WIDTH), bf16)),
-        [HBM] * 5 + [VMEM],
-        (HBM, VMEM),
-        *map(in_hbm, (keys, values, queries, grad_out, attn_out)), log_norm,
-        scratch=[
-            pltpu.VMEM((2 * ROWS, HEAD), bf16),
-            pltpu.VMEM((ROWS, WIDTH), bf16),
-            dma((5,)),
-            dma((PEERS,)),
-        ],
+        shape((2 * ROWS + EXTRA, WIDTH), bf16),
+        [HBM] * 4,
+        VMEM,
+        *map(in_hbm, (queries, grad_out, attn_out, log_norm)),
+        scratch=[pltpu.VMEM((ROWS, WIDTH), bf16), pltpu.VMEM((HEADS, ROWS), f32), dma((4,))],
     )
     p2 = lax.ppermute(p0, NEXT, there)
-    kv = lax.all_to_all(spread, KEEPERS, 0, 0, tiled=True)
-    p1 = lax.ppermute(p0, "core", swap)
     p3 = lax.ppermute(p2, "core", swap)
-    listed = plan(doc_lengths, block_order, *place)
-    p3, (work, held, at, first, own) = lax.optimization_barrier((p3, listed))
-    qs, norm, dot = call(
-        stage,
-        (pltpu.HBM((2, 8 * LANES, HEAD), bf16),) + (shape((8, LANES), f32),) * 2,
-        [HBM] * 4,
-        (HBM, VMEM, VMEM),
-        *map(in_hbm, (p0, p1, p2, p3)),
-        scratch=[
-            pltpu.VMEM((4, 2 * ROWS + EXTRA, WIDTH), bf16),
-            pltpu.VMEM((8 * LANES, HEAD), bf16),
-            pltpu.VMEM((8 * LANES, HEAD), bf16),
-            dma((4,)),
-        ],
-    )
+    p1 = lax.ppermute(lax.optimization_barrier((p0, p2))[0], "core", swap)
+    work, held, at, first, own = plan(doc_lengths, block_order, *place)
     nkeys = 2 * PEERS * ROWS
-    dqt, dkv = call(
+    dqs, dkv = call(
         terms,
-        (shape((8 * HEAD, LANES), f32), pltpu.HBM((nkeys, HEAD), bf16)),
-        [SMEM] * 3 + [VMEM] * 5 + [HBM],
-        (VMEM, HBM),
-        work, held, at, first, own, norm, dot, kv.reshape(nkeys, HEAD), in_hbm(qs),
+        (pltpu.HBM((8 * HEAD, LANES), f32), pltpu.HBM((nkeys, HEAD), bf16)),
+        [SMEM] * 3 + [VMEM] * 7,
+        (HBM, HBM),
+        work, held, at, first, own, p0, p1, p2, p3, kv.reshape(nkeys, HEAD),
         scratch=[
             pltpu.VMEM((nkeys, HEAD), f32),
             pltpu.VMEM((nkeys, HEAD), bf16),
+            pltpu.VMEM((8 * HEAD, LANES), f32),
             pltpu.VMEM((8 * LANES, HEAD), bf16),
             pltpu.VMEM((8 * LANES, HEAD), bf16),
-            dma((4,)),
+            pltpu.VMEM((8, LANES), f32),
+            pltpu.VMEM((8, LANES), f32),
+            dma((5,)),
         ],
     )
     got = lax.all_to_all(dkv.reshape(PEERS, 2 * ROWS, HEAD), KEEPERS, 0, 0, tiled=True)
     dq0, *others = call(
         unstage,
         (shape((ROWS, WIDTH), f32),) + (shape((ROWS, WIDTH), bf16),) * 3,
-        [VMEM],
+        [HBM],
         (VMEM,) * 4,
-        dqt,
+        in_hbm(dqs),
+        scratch=[pltpu.VMEM((8 * HEAD, LANES), f32), dma((8,))],
     )
     routes = (("core", swap), (NEXT, back), (NEXT, across))
     parts = [lax.ppermute(x, axes, route) for x, (axes, route) in zip(others, routes)]

time: 67.6 us -> 71.8 us (1.062)
  the two profiles are of different devices: /device:TPU:1 before, /device:TPU:448 now
where the time goes in v4:
time: 71.8 us; the launch traced here: 71.3 us
  starting transfers between devices  39.3 us (55%)
  waiting for transfers between devices  17.1 us (24%)
  Pallas kernels  10 us (14%)
  other arithmetic  2.5 us (3%)
  between operations  1.53 us (2%)
  local copies, waits for them, and re-layouts  0.84 us (1%)
    pallas_call x5, Pallas kernels, call(): pl.pallas_call(kernel, out_shape=out, in_specs=ins, out_specs=outs, scrat...  10 us
    all_to_all x1, starting transfers between devices, on_device(): lax.all_to_all(dkv.reshape(PEERS, 2 * ROWS, HEAD), KEEPERS, 0, 0, tiled=T...  9.97 us
    ppermute x3, starting transfers between devices, on_device(): lax.ppermute(x, axes, route)  9.76 us
    all_to_all x1, starting transfers between devices, on_device(): kv = lax.all_to_all(sent, KEEPERS, 0, 0, tiled=True)  9.57 us
    ppermute x3, waiting for transfers between devices, on_device(): lax.ppermute(x, axes, route)  9.34 us
    ppermute x1, waiting for transfers between devices, on_device(): p2 = lax.ppermute(p0, NEXT, there)  6.08 us
    ppermute x1, starting transfers between devices, on_device(): p2 = lax.ppermute(p0, NEXT, there)  5.17 us
    ppermute x1, starting transfers between devices, on_device(): p1 = lax.ppermute(lax.optimization_barrier((p0, p2))[0], 'core', swap)  2.9 us
  transfers between devices with their start and end apart: 8, of which 4 were waited for; matrix products, arithmetic and copies ran while one was open for 5% of the time, Pallas kernels for 5%

profile of v4, /device:TPU:448, one launch (start us, length us, event | category | flops | bytes accessed | tf_op | source)
XLA Modules:
  0.0 71.3 jit_solution(13462896194721242334)
XLA Ops:
  0.6 0.0 copy-start.1
  0.6 0.0 copy-start
  0.7 1.7 %spread.1 = bf16[8,256,128]{2,1,0:T(8,128)(2,1)} custom-call(bf16[128,128]{1,0:T(8,128)(2,1)} %k_ref.1, bf16[128,128]{1,0:T(8,128)(2,1)} %v_ref.1), custom_call_target="tpu_custom_call" | custom-call | tf_op jit(solution)/shard_map/spread/pallas_call | solution.py:41
  2.3 9.6 %all-to-all-start = ((bf16[8,256,128]{2,1,0:T(8,128)(2,1)}), bf16[8,256,128]{2,1,0:T(8,128)(2,1)S(1)}, u32[]{:S(2)}, u32[]{:S(2)}) async-start(bf16[8,256,128]{2,1,0:T(8,128)(2,1)} %spread.1), calls=%async_computation | async-start | bytes 1048576 | tf_op jit(solution)/shard_map/all_to_all | solution.py:273
  11.9 1.6 %pack.1.p0_ref = bf16[272,1024]{1,0:T(8,128)(2,1)S(1)} custom-call(bf16[128,1024]{1,0:T(8,128)(2,1)} %q_ref.1, bf16[128,1024]{1,0:T(8,128)(2,1)} %do_ref.1, bf16[128,1024]{1,0:T(8,128)(2,1)} %o_ref.1, f32[8,128]{1,0:T(8,128)} %norm_ref.1), custom_call_target="tpu_custom_call" | custom-call | tf_op jit(solution)/shard_map/pack/pallas_call | solution.py:41
  13.5 5.2 %collective-permute-start = (bf16[272,1024]{1,0:T(8,128)(2,1)S(1)}, bf16[272,1024]{1,0:T(8,128)(2,1)S(1)}, u32[]{:S(2)}, u32[]{:S(2)}) collective-permute-start(bf16[272,1024]{1,0:T(8,128)(2,1)S(1)} %pack.1.p0_ref), channel_id=1, source_target_pairs={{16,0},{32,16},{48,32},{0,48},{8,24},{24,40},{40,56},{56,8},{17,1}... | collective-permute-start | bytes 1671176 | tf_op jit(solution)/shard_map/ppermute | solution.py:282
  18.8 0.0 copy-done.1
  18.8 0.1 select_reduce_fusion.3
  18.9 0.0 copy-done
  18.9 0.2 convert_reduce_fusion
  19.1 0.1 select_reduce_fusion.1
  19.2 0.1 fusion.7
  19.3 0.1 iota_add_fusion.1
  19.4 0.1 add.162
  19.5 0.2 select_reduce_fusion.6
  19.7 0.1 iota_add_fusion
  19.7 0.1 select_reduce_fusion
  19.8 0.1 shift-right-arithmetic_reduce_fusion
  20.0 0.2 convert_reduce_fusion.2
  20.2 0.1 select_reduce_fusion.5
  20.3 0.6 slice.7
  21.6 0.1 tile.9.first_ref
  21.6 0.1 tile.21.own_ref
  21.7 6.1 %collective-permute-done.p2_ref = bf16[272,1024]{1,0:T(8,128)(2,1)S(1)} collective-permute-done((bf16[272,1024]{1,0:T(8,128)(2,1)S(1)}, bf16[272,1024]{1,0:T(8,128)(2,1)S(1)}, u32[]{:S(2)}, u32[]{:S(2)}) %collective-permute-start) | collective-permute-done | bytes 557088 | tf_op jit(solution)/shard_map/ppermute | solution.py:282
  27.8 2.9 %collective-permute-start.1 = (bf16[272,1024]{1,0:T(8,128)(2,1)S(1)}, bf16[272,1024]{1,0:T(8,128)(2,1)S(1)}, u32[]{:S(2)}, u32[]{:S(2)}) collective-permute-start(bf16[272,1024]{1,0:T(8,128)(2,1)S(1)} %pack.1.p0_ref), channel_id=1, source_target_pairs={{0,8},{8,0},{1,9},{9,1},{2,10},{10,2},{3,11},{11,3},{4,12},{12,4},... | collective-permute-start | bytes 1671176 | tf_op jit(solution)/shard_map/ppermute | solution.py:284
  30.7 1.9 %collective-permute-start.2 = (bf16[272,1024]{1,0:T(8,128)(2,1)S(1)}, bf16[272,1024]{1,0:T(8,128)(2,1)S(1)}, u32[]{:S(2)}, u32[]{:S(2)}) collective-permute-start(bf16[272,1024]{1,0:T(8,128)(2,1)S(1)} %collective-permute-done.p2_ref), channel_id=1, source_target_pairs={{0,8},{8,0},{1,9},{9,1},{2,10},{10,2},{3,11},{11,3},{4,12},{12,4},... | collective-permute-start | bytes 1671176 | tf_op jit(solution)/shard_map/ppermute | solution.py:283
  32.6 0.1 convert_reduce_fusion.1
  32.7 0.1 select_reduce_fusion.4
  32.8 0.1 pad_add_fusion.work_ref
  32.9 0.0 all-to-all-done
  32.9 0.0 collective-permute-done.1.p1_ref
  32.9 1.7 %collective-permute-done.2.p3_ref = bf16[272,1024]{1,0:T(8,128)(2,1)S(1)} collective-permute-done((bf16[272,1024]{1,0:T(8,128)(2,1)S(1)}, bf16[272,1024]{1,0:T(8,128)(2,1)S(1)}, u32[]{:S(2)}, u32[]{:S(2)}) %collective-permute-start.2) | collective-permute-done | bytes 557088 | tf_op jit(solution)/shard_map/ppermute | solution.py:283
  34.6 4.1 %terms.1 = (f32[1024,512]{1,0:T(8,128)}, bf16[2048,128]{1,0:T(8,128)(2,1)}) custom-call(s32[145]{0:T(256)S(1)} %pad_add_fusion.work_ref, s32[24]{0:T(128)S(1)} %compare_select_fusion.5.held_ref, s32[24]{0:T(128)S(1)} %get-tuple-element.21.place_ref, s32[8,512]{1,0:T(8,128)S(1)} %tile.9.first_ref, s32[8,512]{1,0:T(8,128)S(1)} %tile.21.own_ref, ...), custom_call_target="tpu_custom_call" | custom-call | tf_op jit(solution)/shard_map/terms/pallas_call | solution.py:41
  38.7 10.0 %all-to-all-start.1 = ((bf16[8,256,128]{2,1,0:T(8,128)(2,1)}), bf16[8,256,128]{2,1,0:T(8,128)(2,1)S(1)}, u32[]{:S(2)}, u32[]{:S(2)}) async-start(bf16[8,256,128]{2,1,0:T(8,128)(2,1)} %bitcast.7), calls=%async_computation.1 | async-start | bytes 1048576 | tf_op jit(solution)/shard_map/all_to_all | solution.py:304
  48.6 2.0 %unstage.1 = (f32[128,1024]{1,0:T(8,128)S(1)}, bf16[128,1024]{1,0:T(8,128)(2,1)S(1)}, bf16[128,1024]{1,0:T(8,128)(2,1)S(1)}, bf16[128,1024]{1,0:T(8,128)(2,1)S(1)}) custom-call(f32[1024,512]{1,0:T(8,128)} %get-tuple-element.13.dqs_ref), custom_call_target="tpu_custom_call" | custom-call | tf_op jit(solution)/shard_map/unstage/pallas_call | solution.py:41
  50.6 2.8 %collective-permute-start.3 = (bf16[128,1024]{1,0:T(8,128)(2,1)S(1)}, bf16[128,1024]{1,0:T(8,128)(2,1)S(1)}, u32[]{:S(2)}, u32[]{:S(2)}) collective-permute-start(bf16[128,1024]{1,0:T(8,128)(2,1)S(1)} %get-tuple-element.15), channel_id=1, source_target_pairs={{0,8},{8,0},{1,9},{9,1},{2,10},{10,2},{3,11},{11,3},{4,12},{12,4},... | collective-permute-start | bytes 786440 | tf_op jit(solution)/shard_map/ppermute | solution.py:314
  53.4 1.9 %collective-permute-start.4 = (bf16[128,1024]{1,0:T(8,128)(2,1)S(1)}, bf16[128,1024]{1,0:T(8,128)(2,1)S(1)}, u32[]{:S(2)}, u32[]{:S(2)}) collective-permute-start(bf16[128,1024]{1,0:T(8,128)(2,1)S(1)} %get-tuple-element.16), channel_id=1, source_target_pairs={{0,16},{16,32},{32,48},{48,0},{24,8},{40,24},{56,40},{8,56},{1,17}... | collective-permute-start | bytes 786440 | tf_op jit(solution)/shard_map/ppermute | solution.py:314
  55.3 5.0 %collective-permute-start.5 = (bf16[128,1024]{1,0:T(8,128)(2,1)S(1)}, bf16[128,1024]{1,0:T(8,128)(2,1)S(1)}, u32[]{:S(2)}, u32[]{:S(2)}) collective-permute-start(bf16[128,1024]{1,0:T(8,128)(2,1)S(1)} %get-tuple-element.17), channel_id=1, source_target_pairs={{0,56},{16,8},{32,24},{48,40},{8,16},{24,32},{40,48},{56,0},{1,57}... | collective-permute-start | bytes 786440 | tf_op jit(solution)/shard_map/ppermute | solution.py:314
  60.4 0.0 collective-permute-done.3
  60.4 9.0 %collective-permute-done.4 = bf16[128,1024]{1,0:T(8,128)(2,1)S(1)} collective-permute-done((bf16[128,1024]{1,0:T(8,128)(2,1)S(1)}, bf16[128,1024]{1,0:T(8,128)(2,1)S(1)}, u32[]{:S(2)}, u32[]{:S(2)}) %collective-permute-start.4) | collective-permute-done | bytes 262176 | tf_op jit(solution)/shard_map/ppermute | solution.py:314
  69.4 0.3 collective-permute-done.5
  69.7 0.8 %add_convert_fusion = bf16[128,1024]{1,0:T(8,128)(2,1)} fusion(f32[128,1024]{1,0:T(8,128)S(1)} %get-tuple-element.14, bf16[128,1024]{1,0:T(8,128)(2,1)S(1)} %collective-permute-done.5, bf16[128,1024]{1,0:T(8,128)(2,1)S(1)} %collective-permute-done.4, bf16[128,1024]{1,0:T(8,128)(2,1)S(1)} %collective-permute-done.3), kind=kLoop, calls=%fused_computation | loop fusion | flops 917504 | bytes 1572864 | tf_op jit(solution)/shard_map/convert_element_type | solution.py:315
  70.6 0.0 all-to-all-done.1.got_ref
  70.6 0.7 total.1
  (9 shorter events, 0.1 us)
Async XLA Ops:
  0.6 18.2 %copy-start.1 = (s32[16]{0:T(128)S(1)}, s32[16]{0:T(128)}, u32[]{:S(2)}) copy-start(s32[16]{0:T(128)} %param.14) | copy-start | bytes 196
  0.6 18.3 %copy-start = (s32[64]{0:T(128)S(1)}, s32[64]{0:T(128)}, u32[]{:S(2)}) copy-start(s32[64]{0:T(128)} %param.15) | copy-start | bytes 772
  2.3 30.6 %all-to-all-start = ((bf16[8,256,128]{2,1,0:T(8,128)(2,1)}), bf16[8,256,128]{2,1,0:T(8,128)(2,1)S(1)}, u32[]{:S(2)}, u32[]{:S(2)}) async-start(bf16[8,256,128]{2,1,0:T(8,128)(2,1)} %spread.1), calls=%async_computation | async-start | bytes 1048576 | tf_op jit(solution)/shard_map/all_to_all | solution.py:273
  13.5 14.3 %collective-permute-start = (bf16[272,1024]{1,0:T(8,128)(2,1)S(1)}, bf16[272,1024]{1,0:T(8,128)(2,1)S(1)}, u32[]{:S(2)}, u32[]{:S(2)}) collective-permute-start(bf16[272,1024]{1,0:T(8,128)(2,1)S(1)} %pack.1.p0_ref), channel_id=1, source_target_pairs={{16,0},{32,16},{48,32},{0,48},{8,24},{24,40},{40,56},{56,8},{17,1}... | collective-permute-start | bytes 1671176 | tf_op jit(solution)/shard_map/ppermute | solution.py:282
  27.8 5.1 %collective-permute-start.1 = (bf16[272,1024]{1,0:T(8,128)(2,1)S(1)}, bf16[272,1024]{1,0:T(8,128)(2,1)S(1)}, u32[]{:S(2)}, u32[]{:S(2)}) collective-permute-start(bf16[272,1024]{1,0:T(8,128)(2,1)S(1)} %pack.1.p0_ref), channel_id=1, source_target_pairs={{0,8},{8,0},{1,9},{9,1},{2,10},{10,2},{3,11},{11,3},{4,12},{12,4},... | collective-permute-start | bytes 1671176 | tf_op jit(solution)/shard_map/ppermute | solution.py:284
  30.7 3.9 %collective-permute-start.2 = (bf16[272,1024]{1,0:T(8,128)(2,1)S(1)}, bf16[272,1024]{1,0:T(8,128)(2,1)S(1)}, u32[]{:S(2)}, u32[]{:S(2)}) collective-permute-start(bf16[272,1024]{1,0:T(8,128)(2,1)S(1)} %collective-permute-done.p2_ref), channel_id=1, source_target_pairs={{0,8},{8,0},{1,9},{9,1},{2,10},{10,2},{3,11},{11,3},{4,12},{12,4},... | collective-permute-start | bytes 1671176 | tf_op jit(solution)/shard_map/ppermute | solution.py:283
  38.7 31.9 %all-to-all-start.1 = ((bf16[8,256,128]{2,1,0:T(8,128)(2,1)}), bf16[8,256,128]{2,1,0:T(8,128)(2,1)S(1)}, u32[]{:S(2)}, u32[]{:S(2)}) async-start(bf16[8,256,128]{2,1,0:T(8,128)(2,1)} %bitcast.7), calls=%async_computation.1 | async-start | bytes 1048576 | tf_op jit(solution)/shard_map/all_to_all | solution.py:304
  50.6 9.8 %collective-permute-start.3 = (bf16[128,1024]{1,0:T(8,128)(2,1)S(1)}, bf16[128,1024]{1,0:T(8,128)(2,1)S(1)}, u32[]{:S(2)}, u32[]{:S(2)}) collective-permute-start(bf16[128,1024]{1,0:T(8,128)(2,1)S(1)} %get-tuple-element.15), channel_id=1, source_target_pairs={{0,8},{8,0},{1,9},{9,1},{2,10},{10,2},{3,11},{11,3},{4,12},{12,4},... | collective-permute-start | bytes 786440 | tf_op jit(solution)/shard_map/ppermute | solution.py:314
  53.4 16.0 %collective-permute-start.4 = (bf16[128,1024]{1,0:T(8,128)(2,1)S(1)}, bf16[128,1024]{1,0:T(8,128)(2,1)S(1)}, u32[]{:S(2)}, u32[]{:S(2)}) collective-permute-start(bf16[128,1024]{1,0:T(8,128)(2,1)S(1)} %get-tuple-element.16), channel_id=1, source_target_pairs={{0,16},{16,32},{32,48},{48,0},{24,8},{40,24},{56,40},{8,56},{1,17}... | collective-permute-start | bytes 786440 | tf_op jit(solution)/shard_map/ppermute | solution.py:314
  55.3 14.4 %collective-permute-start.5 = (bf16[128,1024]{1,0:T(8,128)(2,1)S(1)}, bf16[128,1024]{1,0:T(8,128)(2,1)S(1)}, u32[]{:S(2)}, u32[]{:S(2)}) collective-permute-start(bf16[128,1024]{1,0:T(8,128)(2,1)S(1)} %get-tuple-element.17), channel_id=1, source_target_pairs={{0,56},{16,8},{32,24},{48,40},{8,16},{24,32},{40,48},{56,0},{1,57}... | collective-permute-start | bytes 786440 | tf_op jit(solution)/shard_map/ppermute | solution.py:314

commit v5 on v4

--- a/solution.py
+++ b/solution.py
@@ -58,32 +58,26 @@
     return parts
 
 
-def spread(k_ref, v_ref, kv_ref, kv_buf, sem, kv_sem):
+def pack(
+    k_ref, v_ref, q_ref, do_ref, o_ref, norm_ref,
+    kv_ref, out_ref, kv_buf, o_buf, norm_buf, sem, kv_sem,
+):
     reads = [
         pltpu.make_async_copy(k_ref, kv_buf.at[:ROWS], sem.at[0]),
         pltpu.make_async_copy(v_ref, kv_buf.at[ROWS:], sem.at[1]),
+        pltpu.make_async_copy(do_ref, out_ref.at[ROWS : 2 * ROWS], sem.at[2]),
+        pltpu.make_async_copy(o_ref, o_buf, sem.at[3]),
+        pltpu.make_async_copy(norm_ref, norm_buf, sem.at[4]),
+        pltpu.make_async_copy(q_ref, out_ref.at[:ROWS], sem.at[5]),
     ]
     for copy in reads:
         copy.start()
-    for copy in reads:
+    for copy in reads[:2]:
         copy.wait()
     writes = [pltpu.make_async_copy(kv_buf, kv_ref.at[i], kv_sem.at[i]) for i in range(PEERS)]
     for copy in writes:
         copy.start()
-    for copy in writes:
-        copy.wait()
-
-
-def pack(q_ref, do_ref, o_ref, norm_ref, out_ref, o_buf, norm_buf, sem):
-    reads = [
-        pltpu.make_async_copy(do_ref, out_ref.at[ROWS : 2 * ROWS], sem.at[0]),
-        pltpu.make_async_copy(o_ref, o_buf, sem.at[1]),
-        pltpu.make_async_copy(norm_ref, norm_buf, sem.at[2]),
-        pltpu.make_async_copy(q_ref, out_ref.at[:ROWS], sem.at[3]),
-    ]
-    for copy in reads:
-        copy.start()
-    for copy in reads[:3]:
+    for copy in reads[2:5]:
         copy.wait()
     ones = jnp.ones((8, HEAD), jnp.float32)
     dots = []
@@ -107,7 +101,9 @@
     dots = terms_of(jnp.concatenate(dots, 1))
     dots = dots + [jnp.zeros((5, WIDTH), jnp.float32)]
     out_ref[2 * ROWS :] = jnp.concatenate([norms] + dots, 0).astype(jnp.bfloat16)
-    reads[3].wait()
+    reads[5].wait()
+    for copy in writes:
+        copy.wait()
 
 
 def stage(p_refs, q_ref, do_ref, norm_ref, dot_ref):
@@ -133,7 +129,8 @@
 
 def terms(
     work_ref, held_ref, place_ref, first_ref, own_ref, p0_ref, p1_ref, p2_ref, p3_ref, kv_ref,
-    dqs_ref, dkv_ref, acc_ref, half_ref, dqt_ref, q_ref, do_ref, norm_ref, dot_ref, sem,
+    dq0_ref, dq1_ref, dq2_ref, dq3_ref, dkv_ref,
+    acc_ref, half_ref, dqt_ref, own_buf, send_buf, q_ref, do_ref, norm_ref, dot_ref, sem,
 ):
     acc_ref[...] = jnp.zeros_like(acc_ref)
     dqt_ref[...] = jnp.zeros_like(dqt_ref)
@@ -172,31 +169,24 @@
         return carry
 
     lax.fori_loop(0, work_ref[2 * SLOTS], two, 0)
-    copies = [pltpu.make_async_copy(dqt_ref, dqs_ref, sem.at[4])]
-    copies[0].start()
+    copies = []
     for i in range(4):
-        at = pl.ds(i * 2 * PEERS * BLOCK // 2, PEERS * BLOCK)
+        at = pl.ds(i * PEERS * BLOCK, PEERS * BLOCK)
         half_ref[at, :] = acc_ref[at, :].astype(jnp.bfloat16)
         copies.append(pltpu.make_async_copy(half_ref.at[at], dkv_ref.at[at], sem.at[i]))
         copies[-1].start()
-    for copy in copies:
-        copy.wait()
-
-
-def unstage(dqs_ref, dq0_ref, dq1_ref, dq2_ref, dq3_ref, dqt_ref, sem):
-    copies = []
-    for b in (2, 3, 4, 5, 6, 7, 0, 1):
-        at = slice(b * HEAD, (b + 1) * HEAD)
-        copies.append(pltpu.make_async_copy(dqs_ref.at[at], dqt_ref.at[at], sem.at[b]))
+    for g in (3, 2, 1, 0):
+        out = send_buf.at[g - 1] if g else own_buf
+        for i in range(2):
+            b = 2 * g + i
+            dq = dqt_ref[b * HEAD : (b + 1) * HEAD, :].T.astype(out.dtype)
+            for h in range(HEADS):
+                out[i * BLOCK : (i + 1) * BLOCK, head(h)] = dq[h * BLOCK : (h + 1) * BLOCK]
+        to = (dq0_ref, dq1_ref, dq2_ref, dq3_ref)[g]
+        copies.append(pltpu.make_async_copy(out, to, sem.at[4 + g]))
         copies[-1].start()
     for copy in copies:
         copy.wait()
-    for b in range(8):
-        out = (dq0_ref, dq1_ref, dq2_ref, dq3_ref)[b // 2]
-        at = slice((b % 2) * BLOCK, (b % 2 + 1) * BLOCK)
-        dq = dqt_ref[b * HEAD : (b + 1) * HEAD, :].T.astype(out.dtype)
-        for h in range(HEADS):
-            out[at, head(h)] = dq[h * BLOCK : (h + 1) * BLOCK]
 
 
 def total(got_ref, k_ref, v_ref):
@@ -262,54 +252,48 @@
     back = [(j, i) for i, j in there]
     across = [(2 * i, 2 * ((i - 1) % 4) + 1) for i in range(4)]
     across += [(2 * i + 1, 2 * ((i + 1) % 4)) for i in range(4)]
-    sent = call(
-        spread,
-        pltpu.HBM((PEERS, 2 * ROWS, HEAD), bf16),
-        [HBM] * 2,
-        HBM,
-        in_hbm(keys), in_hbm(values),
-        scratch=[pltpu.VMEM((2 * ROWS, HEAD), bf16), dma((2,)), dma((PEERS,))],
+    sent, p0 = call(
+        pack,
+        (pltpu.HBM((PEERS, 2 * ROWS, HEAD), bf16), shape((2 * ROWS + EXTRA, WIDTH), bf16)),
+        [HBM] * 6,
+        (HBM, VMEM),
+        *map(in_hbm, (keys, values, queries, grad_out, attn_out, log_norm)),
+        scratch=[
+            pltpu.VMEM((2 * ROWS, HEAD), bf16),
+            pltpu.VMEM((ROWS, WIDTH), bf16),
+            pltpu.VMEM((HEADS, ROWS), f32),
+            dma((6,)),
+            dma((PEERS,)),
+        ],
     )
     kv = lax.all_to_all(sent, KEEPERS, 0, 0, tiled=True)
-    p0 = call(
-        pack,
-        shape((2 * ROWS + EXTRA, WIDTH), bf16),
-        [HBM] * 4,
-        VMEM,
-        *map(in_hbm, (queries, grad_out, attn_out, log_norm)),
-        scratch=[pltpu.VMEM((ROWS, WIDTH), bf16), pltpu.VMEM((HEADS, ROWS), f32), dma((4,))],
-    )
     p2 = lax.ppermute(p0, NEXT, there)
     p3 = lax.ppermute(p2, "core", swap)
-    p1 = lax.ppermute(lax.optimization_barrier((p0, p2))[0], "core", swap)
+    p1 = lax.ppermute(p0, "core", swap)
     work, held, at, first, own = plan(doc_lengths, block_order, *place)
     nkeys = 2 * PEERS * ROWS
-    dqs, dkv = call(
+    dq0, *others, dkv = call(
         terms,
-        (pltpu.HBM((8 * HEAD, LANES), f32), pltpu.HBM((nkeys, HEAD), bf16)),
+        (pltpu.HBM((ROWS, WIDTH), f32),)
+        + (pltpu.HBM((ROWS, WIDTH), bf16),) * 3
+        + (pltpu.HBM((nkeys, HEAD), bf16),),
         [SMEM] * 3 + [VMEM] * 7,
-        (HBM, HBM),
+        (HBM,) * 5,
         work, held, at, first, own, p0, p1, p2, p3, kv.reshape(nkeys, HEAD),
         scratch=[
             pltpu.VMEM((nkeys, HEAD), f32),
             pltpu.VMEM((nkeys, HEAD), bf16),
             pltpu.VMEM((8 * HEAD, LANES), f32),
+            pltpu.VMEM((ROWS, WIDTH), f32),
+            pltpu.VMEM((3, ROWS, WIDTH), bf16),
             pltpu.VMEM((8 * LANES, HEAD), bf16),
             pltpu.VMEM((8 * LANES, HEAD), bf16),
             pltpu.VMEM((8, LANES), f32),
             pltpu.VMEM((8, LANES), f32),
-            dma((5,)),
+            dma((8,)),
         ],
     )
     got = lax.all_to_all(dkv.reshape(PEERS, 2 * ROWS, HEAD), KEEPERS, 0, 0, tiled=True)
-    dq0, *others = call(
-        unstage,
-        (shape((ROWS, WIDTH), f32),) + (shape((ROWS, WIDTH), bf16),) * 3,
-        [HBM],
-        (VMEM,) * 4,
-        in_hbm(dqs),
-        scratch=[pltpu.VMEM((8 * HEAD, LANES), f32), dma((8,))],
-    )
     routes = (("core", swap), (NEXT, back), (NEXT, across))
     parts = [lax.ppermute(x, axes, route) for x, (axes, route) in zip(others, routes)]
     grad_q = (dq0 + sum(x.astype(f32) for x in parts)).astype(bf16)

time: 71.8 us -> 66.3 us (0.923)
  the two profiles are of different devices: /device:TPU:448 before, /device:TPU:384 now
where the time goes in v5:
time: 66.3 us; the launch traced here: 65.8 us
  starting transfers between devices  33.9 us (51%)
  waiting for transfers between devices  18.8 us (28%)
  Pallas kernels  7.05 us (11%)
  other arithmetic  2.5 us (4%)
  local copies, waits for them, and re-layouts  2.04 us (3%)
  between operations  1.49 us (2%)
    all_to_all x1, waiting for transfers between devices, on_device(): kv = lax.all_to_all(sent, KEEPERS, 0, 0, tiled=True)  10.6 us
    ppermute x3, starting transfers between devices, on_device(): lax.ppermute(x, axes, route)  9.64 us
    all_to_all x1, starting transfers between devices, on_device(): lax.all_to_all(dkv.reshape(PEERS, 2 * ROWS, HEAD), KEEPERS, 0, 0, tiled=T...  8.23 us
    ppermute x3, waiting for transfers between devices, on_device(): lax.ppermute(x, axes, route)  8.2 us
    all_to_all x1, starting transfers between devices, on_device(): kv = lax.all_to_all(sent, KEEPERS, 0, 0, tiled=True)  7.55 us
    pallas_call x3, Pallas kernels, call(): pl.pallas_call(kernel, out_shape=out, in_specs=ins, out_specs=outs, scrat...  7.05 us
    ppermute x1, starting transfers between devices, on_device(): p2 = lax.ppermute(p0, NEXT, there)  4.67 us
    ppermute x1, starting transfers between devices, on_device(): p3 = lax.ppermute(p2, 'core', swap)  1.92 us
  transfers between devices with their start and end apart: 8, of which 3 were waited for; matrix products, arithmetic and copies ran while one was open for 5% of the time, Pallas kernels for 0%

profile of v5, /device:TPU:384, one launch (start us, length us, event | category | flops | bytes accessed | tf_op | source)
XLA Modules:
  0.0 65.8 jit_solution(1330803721725716944)
XLA Ops:
  0.6 1.8 %pack.1 = (bf16[8,256,128]{2,1,0:T(8,128)(2,1)}, bf16[272,1024]{1,0:T(8,128)(2,1)S(1)}) custom-call(bf16[128,128]{1,0:T(8,128)(2,1)} %k_ref.1, bf16[128,128]{1,0:T(8,128)(2,1)} %v_ref.1, bf16[128,1024]{1,0:T(8,128)(2,1)} %q_ref.1, bf16[128,1024]{1,0:T(8,128)(2,1)} %do_ref.1, bf16[128,1024]{1,0:T(8,128)(2,1)} %o_ref.1, f32[8,128]{1,0:T(8,128)} %norm_ref.1), custom_call_target="tpu_custom_call" | custom-call | tf_op jit(solution)/shard_map/pack/pallas_call | solution.py:41
  2.4 4.7 %collective-permute-start.1 = (bf16[272,1024]{1,0:T(8,128)(2,1)S(1)}, bf16[272,1024]{1,0:T(8,128)(2,1)S(1)}, u32[]{:S(2)}, u32[]{:S(2)}) collective-permute-start(bf16[272,1024]{1,0:T(8,128)(2,1)S(1)} %get-tuple-element.12.p0_ref), channel_id=1, source_target_pairs={{16,0},{32,16},{48,32},{0,48},{8,24},{24,40},{40,56},{56,8},{17,1}... | collective-permute-start | bytes 1671176 | tf_op jit(solution)/shard_map/ppermute | solution.py:270
  7.1 1.9 %collective-permute-start = (bf16[272,1024]{1,0:T(8,128)(2,1)S(1)}, bf16[272,1024]{1,0:T(8,128)(2,1)S(1)}, u32[]{:S(2)}, u32[]{:S(2)}) collective-permute-start(bf16[272,1024]{1,0:T(8,128)(2,1)S(1)} %get-tuple-element.12.p0_ref), channel_id=1, source_target_pairs={{0,8},{8,0},{1,9},{9,1},{2,10},{10,2},{3,11},{11,3},{4,12},{12,4},... | collective-permute-start | bytes 1671176 | tf_op jit(solution)/shard_map/ppermute | solution.py:272
  9.0 7.6 %all-to-all-start = ((bf16[8,256,128]{2,1,0:T(8,128)(2,1)}), bf16[8,256,128]{2,1,0:T(8,128)(2,1)S(1)}, u32[]{:S(2)}, u32[]{:S(2)}) async-start(bf16[8,256,128]{2,1,0:T(8,128)(2,1)} %get-tuple-element.13), calls=%async_computation | async-start | bytes 1048576 | tf_op jit(solution)/shard_map/all_to_all | solution.py:269
  16.6 0.0 copy-start.4
  16.6 0.6 copy-done.4
  17.3 0.0 copy-start.1
  17.3 0.1 select_reduce_fusion.3
  17.4 0.5 copy-done.1
  17.9 0.2 convert_reduce_fusion
  18.1 0.1 select_reduce_fusion.1
  18.2 0.1 fusion.7
  18.3 0.1 iota_add_fusion.1
  18.4 0.1 add.162
  18.5 0.2 select_reduce_fusion.6
  18.7 0.1 iota_add_fusion
  18.7 0.1 select_reduce_fusion
  18.8 0.1 shift-right-arithmetic_reduce_fusion
  19.0 0.2 convert_reduce_fusion.2
  19.2 0.1 select_reduce_fusion.5
  19.3 0.6 slice.7
  20.6 0.1 tile.9.first_ref
  20.6 0.1 tile.21.own_ref
  20.7 0.0 collective-permute-done.1.p2_ref
  20.7 1.9 %collective-permute-start.2 = (bf16[272,1024]{1,0:T(8,128)(2,1)S(1)}, bf16[272,1024]{1,0:T(8,128)(2,1)S(1)}, u32[]{:S(2)}, u32[]{:S(2)}) collective-permute-start(bf16[272,1024]{1,0:T(8,128)(2,1)S(1)} %collective-permute-done.1.p2_ref), channel_id=1, source_target_pairs={{0,8},{8,0},{1,9},{9,1},{2,10},{10,2},{3,11},{11,3},{4,12},{12,4},... | collective-permute-start | bytes 1671176 | tf_op jit(solution)/shard_map/ppermute | solution.py:271
  22.7 0.1 convert_reduce_fusion.1
  22.7 0.1 select_reduce_fusion.4
  22.8 0.1 pad_add_fusion.work_ref
  22.9 0.0 collective-permute-done.p1_ref
  22.9 10.6 %all-to-all-done = bf16[8,256,128]{2,1,0:T(8,128)(2,1)S(1)} async-done(((bf16[8,256,128]{2,1,0:T(8,128)(2,1)}), bf16[8,256,128]{2,1,0:T(8,128)(2,1)S(1)}, u32[]{:S(2)}, u32[]{:S(2)}) %all-to-all-start) | async-done | bytes 524320 | tf_op jit(solution)/shard_map/all_to_all | solution.py:269
  33.5 0.0 collective-permute-done.2.p3_ref
  33.5 4.6 %terms.1 = (f32[128,1024]{1,0:T(8,128)}, bf16[128,1024]{1,0:T(8,128)(2,1)}, bf16[128,1024]{1,0:T(8,128)(2,1)}, bf16[128,1024]{1,0:T(8,128)(2,1)}, bf16[2048,128]{1,0:T(8,128)(2,1)}) custom-call(s32[145]{0:T(256)S(1)} %pad_add_fusion.work_ref, s32[24]{0:T(128)S(1)} %compare_select_fusion.5.held_ref, s32[24]{0:T(128)S(1)} %get-tuple-element.21.place_ref, ...), custom_call_target="tpu_custom_call" | custom-call | tf_op jit(solution)/shard_map/terms/pallas_call | solution.py:41
  38.1 0.0 copy-start.3
  38.1 0.0 copy-start.2
  38.1 0.0 copy-start
  38.1 8.2 %all-to-all-start.1 = ((bf16[8,256,128]{2,1,0:T(8,128)(2,1)}), bf16[8,256,128]{2,1,0:T(8,128)(2,1)S(1)}, u32[]{:S(2)}, u32[]{:S(2)}) async-start(bf16[8,256,128]{2,1,0:T(8,128)(2,1)} %bitcast.7), calls=%async_computation.1 | async-start | bytes 1048576 | tf_op jit(solution)/shard_map/all_to_all | solution.py:296
  46.4 1.9 %collective-permute-start.3 = (bf16[128,1024]{1,0:T(8,128)(2,1)}, bf16[128,1024]{1,0:T(8,128)(2,1)S(1)}, u32[]{:S(2)}, u32[]{:S(2)}) collective-permute-start(bf16[128,1024]{1,0:T(8,128)(2,1)} %get-tuple-element.15), channel_id=1, source_target_pairs={{0,8},{8,0},{1,9},{9,1},{2,10},{10,2},{3,11},{11,3},{4,12},{12,4},... | collective-permute-start | bytes 786440 | tf_op jit(solution)/shard_map/ppermute | solution.py:298
  48.3 0.0 copy-done.3
  48.3 2.1 %collective-permute-start.4 = (bf16[128,1024]{1,0:T(8,128)(2,1)S(1)}, bf16[128,1024]{1,0:T(8,128)(2,1)S(1)}, u32[]{:S(2)}, u32[]{:S(2)}) collective-permute-start(bf16[128,1024]{1,0:T(8,128)(2,1)S(1)} %copy-done.3), channel_id=1, source_target_pairs={{0,16},{16,32},{32,48},{48,0},{24,8},{40,24},{56,40},{8,56},{1,17}... | collective-permute-start | bytes 786440 | tf_op jit(solution)/shard_map/ppermute | solution.py:298
  50.4 0.0 copy-done.2
  50.4 5.6 %collective-permute-start.5 = (bf16[128,1024]{1,0:T(8,128)(2,1)S(1)}, bf16[128,1024]{1,0:T(8,128)(2,1)S(1)}, u32[]{:S(2)}, u32[]{:S(2)}) collective-permute-start(bf16[128,1024]{1,0:T(8,128)(2,1)S(1)} %copy-done.2), channel_id=1, source_target_pairs={{0,56},{16,8},{32,24},{48,40},{8,16},{24,32},{40,48},{56,0},{1,57}... | collective-permute-start | bytes 786440 | tf_op jit(solution)/shard_map/ppermute | solution.py:298
  56.0 0.0 collective-permute-done.3
  56.0 6.8 %collective-permute-done.4 = bf16[128,1024]{1,0:T(8,128)(2,1)S(1)} collective-permute-done((bf16[128,1024]{1,0:T(8,128)(2,1)S(1)}, bf16[128,1024]{1,0:T(8,128)(2,1)S(1)}, u32[]{:S(2)}, u32[]{:S(2)}) %collective-permute-start.4) | collective-permute-done | bytes 262176 | tf_op jit(solution)/shard_map/ppermute | solution.py:298
  62.9 1.4 %collective-permute-done.5 = bf16[128,1024]{1,0:T(8,128)(2,1)S(1)} collective-permute-done((bf16[128,1024]{1,0:T(8,128)(2,1)S(1)}, bf16[128,1024]{1,0:T(8,128)(2,1)S(1)}, u32[]{:S(2)}, u32[]{:S(2)}) %collective-permute-start.5) | collective-permute-done | bytes 262176 | tf_op jit(solution)/shard_map/ppermute | solution.py:298
  64.2 0.0 copy-done
  64.3 0.8 %add_convert_fusion = bf16[128,1024]{1,0:T(8,128)(2,1)} fusion(f32[128,1024]{1,0:T(8,128)S(1)} %copy-done, bf16[128,1024]{1,0:T(8,128)(2,1)S(1)} %collective-permute-done.5, bf16[128,1024]{1,0:T(8,128)(2,1)S(1)} %collective-permute-done.4, bf16[128,1024]{1,0:T(8,128)(2,1)S(1)} %collective-permute-done.3), kind=kLoop, calls=%fused_computation | loop fusion | flops 917504 | bytes 1572864 | tf_op jit(solution)/shard_map/convert_element_type | solution.py:299
  65.1 0.0 all-to-all-done.1.got_ref
  65.1 0.7 %total.1 = (bf16[128,128]{1,0:T(8,128)(2,1)}, bf16[128,128]{1,0:T(8,128)(2,1)}) custom-call(bf16[8,256,128]{2,1,0:T(8,128)(2,1)S(1)} %all-to-all-done.1.got_ref), custom_call_target="tpu_custom_call" | custom-call | tf_op jit(solution)/shard_map/total/pallas_call | solution.py:41
  (9 shorter events, 0.1 us)
Async XLA Ops:
  2.4 18.3 %collective-permute-start.1 = (bf16[272,1024]{1,0:T(8,128)(2,1)S(1)}, bf16[272,1024]{1,0:T(8,128)(2,1)S(1)}, u32[]{:S(2)}, u32[]{:S(2)}) collective-permute-start(bf16[272,1024]{1,0:T(8,128)(2,1)S(1)} %get-tuple-element.12.p0_ref), channel_id=1, source_target_pairs={{16,0},{32,16},{48,32},{0,48},{8,24},{24,40},{40,56},{56,8},{17,1}... | collective-permute-start | bytes 1671176 | tf_op jit(solution)/shard_map/ppermute | solution.py:270
  7.1 15.8 %collective-permute-start = (bf16[272,1024]{1,0:T(8,128)(2,1)S(1)}, bf16[272,1024]{1,0:T(8,128)(2,1)S(1)}, u32[]{:S(2)}, u32[]{:S(2)}) collective-permute-start(bf16[272,1024]{1,0:T(8,128)(2,1)S(1)} %get-tuple-element.12.p0_ref), channel_id=1, source_target_pairs={{0,8},{8,0},{1,9},{9,1},{2,10},{10,2},{3,11},{11,3},{4,12},{12,4},... | collective-permute-start | bytes 1671176 | tf_op jit(solution)/shard_map/ppermute | solution.py:272
  9.0 24.5 %all-to-all-start = ((bf16[8,256,128]{2,1,0:T(8,128)(2,1)}), bf16[8,256,128]{2,1,0:T(8,128)(2,1)S(1)}, u32[]{:S(2)}, u32[]{:S(2)}) async-start(bf16[8,256,128]{2,1,0:T(8,128)(2,1)} %get-tuple-element.13), calls=%async_computation | async-start | bytes 1048576 | tf_op jit(solution)/shard_map/all_to_all | solution.py:269
  16.6 0.7 %copy-start.4 = (s32[16]{0:T(128)S(1)}, s32[16]{0:T(128)}, u32[]{:S(2)}) copy-start(s32[16]{0:T(128)} %param.14) | copy-start | bytes 196
  17.3 0.7 copy-start.1
  20.7 12.8 %collective-permute-start.2 = (bf16[272,1024]{1,0:T(8,128)(2,1)S(1)}, bf16[272,1024]{1,0:T(8,128)(2,1)S(1)}, u32[]{:S(2)}, u32[]{:S(2)}) collective-permute-start(bf16[272,1024]{1,0:T(8,128)(2,1)S(1)} %collective-permute-done.1.p2_ref), channel_id=1, source_target_pairs={{0,8},{8,0},{1,9},{9,1},{2,10},{10,2},{3,11},{11,3},{4,12},{12,4},... | collective-permute-start | bytes 1671176 | tf_op jit(solution)/shard_map/ppermute | solution.py:271
  38.1 10.2 %copy-start.3 = (bf16[128,1024]{1,0:T(8,128)(2,1)S(1)}, bf16[128,1024]{1,0:T(8,128)(2,1)}, u32[]{:S(2)}) copy-start(bf16[128,1024]{1,0:T(8,128)(2,1)} %get-tuple-element.16) | copy-start | bytes 786436
  38.1 12.3 %copy-start.2 = (bf16[128,1024]{1,0:T(8,128)(2,1)S(1)}, bf16[128,1024]{1,0:T(8,128)(2,1)}, u32[]{:S(2)}) copy-start(bf16[128,1024]{1,0:T(8,128)(2,1)} %get-tuple-element.17) | copy-start | bytes 786436
  38.1 26.1 %copy-start = (f32[128,1024]{1,0:T(8,128)S(1)}, f32[128,1024]{1,0:T(8,128)}, u32[]{:S(2)}) copy-start(f32[128,1024]{1,0:T(8,128)} %get-tuple-element.14) | copy-start | bytes 1572868
  38.1 27.0 %all-to-all-start.1 = ((bf16[8,256,128]{2,1,0:T(8,128)(2,1)}), bf16[8,256,128]{2,1,0:T(8,128)(2,1)S(1)}, u32[]{:S(2)}, u32[]{:S(2)}) async-start(bf16[8,256,128]{2,1,0:T(8,128)(2,1)} %bitcast.7), calls=%async_computation.1 | async-start | bytes 1048576 | tf_op jit(solution)/shard_map/all_to_all | solution.py:296
  46.4 9.7 %collective-permute-start.3 = (bf16[128,1024]{1,0:T(8,128)(2,1)}, bf16[128,1024]{1,0:T(8,128)(2,1)S(1)}, u32[]{:S(2)}, u32[]{:S(2)}) collective-permute-start(bf16[128,1024]{1,0:T(8,128)(2,1)} %get-tuple-element.15), channel_id=1, source_target_pairs={{0,8},{8,0},{1,9},{9,1},{2,10},{10,2},{3,11},{11,3},{4,12},{12,4},... | collective-permute-start | bytes 786440 | tf_op jit(solution)/shard_map/ppermute | solution.py:298
  48.3 14.6 %collective-permute-start.4 = (bf16[128,1024]{1,0:T(8,128)(2,1)S(1)}, bf16[128,1024]{1,0:T(8,128)(2,1)S(1)}, u32[]{:S(2)}, u32[]{:S(2)}) collective-permute-start(bf16[128,1024]{1,0:T(8,128)(2,1)S(1)} %copy-done.3), channel_id=1, source_target_pairs={{0,16},{16,32},{32,48},{48,0},{24,8},{40,24},{56,40},{8,56},{1,17}... | collective-permute-start | bytes 786440 | tf_op jit(solution)/shard_map/ppermute | solution.py:298
  50.4 13.9 %collective-permute-start.5 = (bf16[128,1024]{1,0:T(8,128)(2,1)S(1)}, bf16[128,1024]{1,0:T(8,128)(2,1)S(1)}, u32[]{:S(2)}, u32[]{:S(2)}) collective-permute-start(bf16[128,1024]{1,0:T(8,128)(2,1)S(1)} %copy-done.2), channel_id=1, source_target_pairs={{0,56},{16,8},{32,24},{48,40},{8,16},{24,32},{40,48},{56,0},{1,57}... | collective-permute-start | bytes 786440 | tf_op jit(solution)/shard_map/ppermute | solution.py:298

commit v6 on v5

--- a/solution.py
+++ b/solution.py
@@ -269,8 +269,9 @@
     kv = lax.all_to_all(sent, KEEPERS, 0, 0, tiled=True)
     p2 = lax.ppermute(p0, NEXT, there)
     p3 = lax.ppermute(p2, "core", swap)
-    p1 = lax.ppermute(p0, "core", swap)
     work, held, at, first, own = plan(doc_lengths, block_order, *place)
+    later, held = lax.optimization_barrier((p0, held))
+    p1 = lax.ppermute(later, "core", swap)
     nkeys = 2 * PEERS * ROWS
     dq0, *others, dkv = call(
         terms,
@@ -294,8 +295,8 @@
         ],
     )
     got = lax.all_to_all(dkv.reshape(PEERS, 2 * ROWS, HEAD), KEEPERS, 0, 0, tiled=True)
-    routes = (("core", swap), (NEXT, back), (NEXT, across))
-    parts = [lax.ppermute(x, axes, route) for x, (axes, route) in zip(others, routes)]
+    routes = ((NEXT, across), (NEXT, back), ("core", swap))
+    parts = [lax.ppermute(x, axes, route) for x, (axes, route) in zip(others[::-1], routes)]
     grad_q = (dq0 + sum(x.astype(f32) for x in parts)).astype(bf16)
     grad_k, grad_v = call(total, (shape((ROWS, HEAD), bf16),) * 2, [VMEM], (VMEM,) * 2, got)
     return grad_q, grad_k, grad_v

time: 66.3 us -> 63.9 us (0.964)
  the two profiles are of different devices: /device:TPU:384 before, /device:TPU:1 now
where the time goes in v6:
time: 63.9 us; the launch traced here: 63.4 us
  starting transfers between devices  37.6 us (59%)
  waiting for transfers between devices  10.4 us (16%)
  Pallas kernels  9.2 us (14%)
  other arithmetic  2.5 us (4%)
  local copies, waits for them, and re-layouts  2.14 us (3%)
  between operations  1.53 us (2%)
    all_to_all x1, starting transfers between devices, on_device(): kv = lax.all_to_all(sent, KEEPERS, 0, 0, tiled=True)  10.1 us
    pallas_call x3, Pallas kernels, call(): pl.pallas_call(kernel, out_shape=out, in_specs=ins, out_specs=outs, scrat...  9.2 us
    all_to_all x1, starting transfers between devices, on_device(): lax.all_to_all(dkv.reshape(PEERS, 2 * ROWS, HEAD), KEEPERS, 0, 0, tiled=T...  8.28 us
    ppermute x3, starting transfers between devices, on_device(): lax.ppermute(x, axes, route)  7.85 us
    ppermute x3, waiting for transfers between devices, on_device(): lax.ppermute(x, axes, route)  6.05 us
    ppermute x1, starting transfers between devices, on_device(): p1 = lax.ppermute(later, 'core', swap)  5.81 us
    ppermute x1, starting transfers between devices, on_device(): p3 = lax.ppermute(p2, 'core', swap)  3.31 us
    ppermute x1, starting transfers between devices, on_device(): p2 = lax.ppermute(p0, NEXT, there)  2.21 us
  transfers between devices with their start and end apart: 8, of which 5 were waited for; matrix products, arithmetic and copies ran while one was open for 5% of the time, Pallas kernels for 0%

profile of v6, /device:TPU:1, one launch (start us, length us, event | category | flops | bytes accessed | tf_op | source)
XLA Modules:
  0.0 63.4 jit_solution(3204312437816719963)
XLA Ops:
  0.6 1.8 %pack.1 = (bf16[8,256,128]{2,1,0:T(8,128)(2,1)}, bf16[272,1024]{1,0:T(8,128)(2,1)S(1)}) custom-call(bf16[128,128]{1,0:T(8,128)(2,1)} %k_ref.1, bf16[128,128]{1,0:T(8,128)(2,1)} %v_ref.1, bf16[128,1024]{1,0:T(8,128)(2,1)} %q_ref.1, bf16[128,1024]{1,0:T(8,128)(2,1)} %do_ref.1, bf16[128,1024]{1,0:T(8,128)(2,1)} %o_ref.1, f32[8,128]{1,0:T(8,128)} %norm_ref.1), custom_call_target="tpu_custom_call" | custom-call | tf_op jit(solution)/shard_map/pack/pallas_call | solution.py:41
  2.4 10.1 %all-to-all-start = ((bf16[8,256,128]{2,1,0:T(8,128)(2,1)}), bf16[8,256,128]{2,1,0:T(8,128)(2,1)S(1)}, u32[]{:S(2)}, u32[]{:S(2)}) async-start(bf16[8,256,128]{2,1,0:T(8,128)(2,1)} %get-tuple-element.17), calls=%async_computation | async-start | bytes 1048576 | tf_op jit(solution)/shard_map/all_to_all | solution.py:269
  12.5 2.2 %collective-permute-start.1 = (bf16[272,1024]{1,0:T(8,128)(2,1)S(1)}, bf16[272,1024]{1,0:T(8,128)(2,1)S(1)}, u32[]{:S(2)}, u32[]{:S(2)}) collective-permute-start(bf16[272,1024]{1,0:T(8,128)(2,1)S(1)} %get-tuple-element.16.p0_ref), channel_id=1, source_target_pairs={{16,0},{32,16},{48,32},{0,48},{8,24},{24,40},{40,56},{56,8},{17,1}... | collective-permute-start | bytes 1671176 | tf_op jit(solution)/shard_map/ppermute | solution.py:270
  14.8 0.0 copy-start.1
  14.8 0.6 copy-done.1
  15.4 0.2 convert_reduce_fusion
  15.6 0.1 select_reduce_fusion.1
  15.7 5.8 %collective-permute-start = (bf16[272,1024]{1,0:T(8,128)(2,1)S(1)}, bf16[272,1024]{1,0:T(8,128)(2,1)S(1)}, u32[]{:S(2)}, u32[]{:S(2)}) collective-permute-start(bf16[272,1024]{1,0:T(8,128)(2,1)S(1)} %get-tuple-element.16.p0_ref), channel_id=1, source_target_pairs={{0,8},{8,0},{1,9},{9,1},{2,10},{10,2},{3,11},{11,3},{4,12},{12,4},... | collective-permute-start | bytes 1671176 | tf_op jit(solution)/shard_map/ppermute | solution.py:274
  21.6 0.0 copy-start.4
  21.6 0.6 %copy-done.4 = s32[16]{0:T(128)S(1)} copy-done((s32[16]{0:T(128)S(1)}, s32[16]{0:T(128)}, u32[]{:S(2)}) %copy-start.4) | copy-done | bytes 88
  22.3 0.1 select_reduce_fusion.3
  22.4 0.1 fusion.7
  22.4 0.1 iota_add_fusion.1
  22.5 0.1 add.162
  22.6 0.2 select_reduce_fusion.6
  22.8 0.1 iota_add_fusion
  22.9 0.1 select_reduce_fusion
  23.0 0.1 shift-right-arithmetic_reduce_fusion
  23.1 0.2 convert_reduce_fusion.2
  23.3 0.1 select_reduce_fusion.5
  23.4 0.6 slice.7
  24.7 0.1 tile.9.first_ref
  24.8 0.1 tile.21.own_ref
  24.9 2.2 %collective-permute-done.1.p2_ref = bf16[272,1024]{1,0:T(8,128)(2,1)S(1)} collective-permute-done((bf16[272,1024]{1,0:T(8,128)(2,1)S(1)}, bf16[272,1024]{1,0:T(8,128)(2,1)S(1)}, u32[]{:S(2)}, u32[]{:S(2)}) %collective-permute-start.1) | collective-permute-done | bytes 557088 | tf_op jit(solution)/shard_map/ppermute | solution.py:270
  27.0 3.3 %collective-permute-start.2 = (bf16[272,1024]{1,0:T(8,128)(2,1)S(1)}, bf16[272,1024]{1,0:T(8,128)(2,1)S(1)}, u32[]{:S(2)}, u32[]{:S(2)}) collective-permute-start(bf16[272,1024]{1,0:T(8,128)(2,1)S(1)} %collective-permute-done.1.p2_ref), channel_id=1, source_target_pairs={{0,8},{8,0},{1,9},{9,1},{2,10},{10,2},{3,11},{11,3},{4,12},{12,4},... | collective-permute-start | bytes 1671176 | tf_op jit(solution)/shard_map/ppermute | solution.py:271
  30.4 0.1 convert_reduce_fusion.1
  30.4 0.1 select_reduce_fusion.4
  30.5 0.1 pad_add_fusion.work_ref
  30.6 0.0 collective-permute-done.p1_ref
  30.6 0.0 all-to-all-done
  30.6 1.3 %collective-permute-done.2.p3_ref = bf16[272,1024]{1,0:T(8,128)(2,1)S(1)} collective-permute-done((bf16[272,1024]{1,0:T(8,128)(2,1)S(1)}, bf16[272,1024]{1,0:T(8,128)(2,1)S(1)}, u32[]{:S(2)}, u32[]{:S(2)}) %collective-permute-start.2) | collective-permute-done | bytes 557088 | tf_op jit(solution)/shard_map/ppermute | solution.py:271
  31.9 6.8 %terms.1 = (f32[128,1024]{1,0:T(8,128)}, bf16[128,1024]{1,0:T(8,128)(2,1)}, bf16[128,1024]{1,0:T(8,128)(2,1)}, bf16[128,1024]{1,0:T(8,128)(2,1)}, bf16[2048,128]{1,0:T(8,128)(2,1)}) custom-call(s32[145]{0:T(256)S(1)} %pad_add_fusion.work_ref, s32[24]{0:T(128)S(1)} %compare_select_fusion.5.held_ref, s32[24]{0:T(128)S(1)} %get-tuple-element.25.place_ref, ...), custom_call_target="tpu_custom_call" | custom-call | tf_op jit(solution)/shard_map/terms/pallas_call | solution.py:41
  38.7 0.0 copy-start.3
  38.7 0.0 copy-start.2
  38.7 0.0 copy-start
  38.7 8.3 %all-to-all-start.1 = ((bf16[8,256,128]{2,1,0:T(8,128)(2,1)}), bf16[8,256,128]{2,1,0:T(8,128)(2,1)S(1)}, u32[]{:S(2)}, u32[]{:S(2)}) async-start(bf16[8,256,128]{2,1,0:T(8,128)(2,1)} %bitcast.7), calls=%async_computation.1 | async-start | bytes 1048576 | tf_op jit(solution)/shard_map/all_to_all | solution.py:297
  47.0 1.9 %collective-permute-start.3 = (bf16[128,1024]{1,0:T(8,128)(2,1)}, bf16[128,1024]{1,0:T(8,128)(2,1)S(1)}, u32[]{:S(2)}, u32[]{:S(2)}) collective-permute-start(bf16[128,1024]{1,0:T(8,128)(2,1)} %get-tuple-element.19), channel_id=1, source_target_pairs={{0,56},{16,8},{32,24},{48,40},{8,16},{24,32},{40,48},{56,0},{1,57}... | collective-permute-start | bytes 786440 | tf_op jit(solution)/shard_map/ppermute | solution.py:299
  48.9 0.0 copy-done.3
  48.9 3.0 %collective-permute-start.4 = (bf16[128,1024]{1,0:T(8,128)(2,1)S(1)}, bf16[128,1024]{1,0:T(8,128)(2,1)S(1)}, u32[]{:S(2)}, u32[]{:S(2)}) collective-permute-start(bf16[128,1024]{1,0:T(8,128)(2,1)S(1)} %copy-done.3), channel_id=1, source_target_pairs={{0,16},{16,32},{32,48},{48,0},{24,8},{40,24},{56,40},{8,56},{1,17}... | collective-permute-start | bytes 786440 | tf_op jit(solution)/shard_map/ppermute | solution.py:299
  51.9 0.0 copy-done.2
  51.9 3.0 %collective-permute-start.5 = (bf16[128,1024]{1,0:T(8,128)(2,1)S(1)}, bf16[128,1024]{1,0:T(8,128)(2,1)S(1)}, u32[]{:S(2)}, u32[]{:S(2)}) collective-permute-start(bf16[128,1024]{1,0:T(8,128)(2,1)S(1)} %copy-done.2), channel_id=1, source_target_pairs={{0,8},{8,0},{1,9},{9,1},{2,10},{10,2},{3,11},{11,3},{4,12},{12,4},... | collective-permute-start | bytes 786440 | tf_op jit(solution)/shard_map/ppermute | solution.py:299
  54.9 5.9 %collective-permute-done.3 = bf16[128,1024]{1,0:T(8,128)(2,1)S(1)} collective-permute-done((bf16[128,1024]{1,0:T(8,128)(2,1)}, bf16[128,1024]{1,0:T(8,128)(2,1)S(1)}, u32[]{:S(2)}, u32[]{:S(2)}) %collective-permute-start.3) | collective-permute-done | bytes 262176 | tf_op jit(solution)/shard_map/ppermute | solution.py:299
  60.7 0.2 collective-permute-done.4
  60.9 0.0 collective-permute-done.5
  60.9 0.0 copy-done
  61.0 0.8 %add_convert_fusion = bf16[128,1024]{1,0:T(8,128)(2,1)} fusion(f32[128,1024]{1,0:T(8,128)S(1)} %copy-done, bf16[128,1024]{1,0:T(8,128)(2,1)S(1)} %collective-permute-done.5, bf16[128,1024]{1,0:T(8,128)(2,1)S(1)} %collective-permute-done.4, bf16[128,1024]{1,0:T(8,128)(2,1)S(1)} %collective-permute-done.3), kind=kLoop, calls=%fused_computation | loop fusion | flops 917504 | bytes 1572864 | tf_op jit(solution)/shard_map/convert_element_type | solution.py:300
  61.8 0.9 %all-to-all-done.1.got_ref = bf16[8,256,128]{2,1,0:T(8,128)(2,1)S(1)} async-done(((bf16[8,256,128]{2,1,0:T(8,128)(2,1)}), bf16[8,256,128]{2,1,0:T(8,128)(2,1)S(1)}, u32[]{:S(2)}, u32[]{:S(2)}) %all-to-all-start.1) | async-done | bytes 524320 | tf_op jit(solution)/shard_map/all_to_all | solution.py:297
  62.7 0.7 %total.1 = (bf16[128,128]{1,0:T(8,128)(2,1)}, bf16[128,128]{1,0:T(8,128)(2,1)}) custom-call(bf16[8,256,128]{2,1,0:T(8,128)(2,1)S(1)} %all-to-all-done.1.got_ref), custom_call_target="tpu_custom_call" | custom-call | tf_op jit(solution)/shard_map/total/pallas_call | solution.py:41
  (9 shorter events, 0.1 us)
Async XLA Ops:
  2.4 28.2 %all-to-all-start = ((bf16[8,256,128]{2,1,0:T(8,128)(2,1)}), bf16[8,256,128]{2,1,0:T(8,128)(2,1)S(1)}, u32[]{:S(2)}, u32[]{:S(2)}) async-start(bf16[8,256,128]{2,1,0:T(8,128)(2,1)} %get-tuple-element.17), calls=%async_computation | async-start | bytes 1048576 | tf_op jit(solution)/shard_map/all_to_all | solution.py:269
  12.5 14.5 %collective-permute-start.1 = (bf16[272,1024]{1,0:T(8,128)(2,1)S(1)}, bf16[272,1024]{1,0:T(8,128)(2,1)S(1)}, u32[]{:S(2)}, u32[]{:S(2)}) collective-permute-start(bf16[272,1024]{1,0:T(8,128)(2,1)S(1)} %get-tuple-element.16.p0_ref), channel_id=1, source_target_pairs={{16,0},{32,16},{48,32},{0,48},{8,24},{24,40},{40,56},{56,8},{17,1}... | collective-permute-start | bytes 1671176 | tf_op jit(solution)/shard_map/ppermute | solution.py:270
  14.8 0.7 %copy-start.1 = (s32[64]{0:T(128)S(1)}, s32[64]{0:T(128)}, u32[]{:S(2)}) copy-start(s32[64]{0:T(128)} %param.15) | copy-start | bytes 772
  15.7 14.9 %collective-permute-start = (bf16[272,1024]{1,0:T(8,128)(2,1)S(1)}, bf16[272,1024]{1,0:T(8,128)(2,1)S(1)}, u32[]{:S(2)}, u32[]{:S(2)}) collective-permute-start(bf16[272,1024]{1,0:T(8,128)(2,1)S(1)} %get-tuple-element.16.p0_ref), channel_id=1, source_target_pairs={{0,8},{8,0},{1,9},{9,1},{2,10},{10,2},{3,11},{11,3},{4,12},{12,4},... | collective-permute-start | bytes 1671176 | tf_op jit(solution)/shard_map/ppermute | solution.py:274
  21.6 0.7 %copy-start.4 = (s32[16]{0:T(128)S(1)}, s32[16]{0:T(128)}, u32[]{:S(2)}) copy-start(s32[16]{0:T(128)} %param.14) | copy-start | bytes 196
  27.0 4.9 %collective-permute-start.2 = (bf16[272,1024]{1,0:T(8,128)(2,1)S(1)}, bf16[272,1024]{1,0:T(8,128)(2,1)S(1)}, u32[]{:S(2)}, u32[]{:S(2)}) collective-permute-start(bf16[272,1024]{1,0:T(8,128)(2,1)S(1)} %collective-permute-done.1.p2_ref), channel_id=1, source_target_pairs={{0,8},{8,0},{1,9},{9,1},{2,10},{10,2},{3,11},{11,3},{4,12},{12,4},... | collective-permute-start | bytes 1671176 | tf_op jit(solution)/shard_map/ppermute | solution.py:271
  38.7 10.2 %copy-start.3 = (bf16[128,1024]{1,0:T(8,128)(2,1)S(1)}, bf16[128,1024]{1,0:T(8,128)(2,1)}, u32[]{:S(2)}) copy-start(bf16[128,1024]{1,0:T(8,128)(2,1)} %get-tuple-element.20) | copy-start | bytes 786436
  38.7 13.2 %copy-start.2 = (bf16[128,1024]{1,0:T(8,128)(2,1)S(1)}, bf16[128,1024]{1,0:T(8,128)(2,1)}, u32[]{:S(2)}) copy-start(bf16[128,1024]{1,0:T(8,128)(2,1)} %get-tuple-element.21) | copy-start | bytes 786436
  38.7 22.2 %copy-start = (f32[128,1024]{1,0:T(8,128)S(1)}, f32[128,1024]{1,0:T(8,128)}, u32[]{:S(2)}) copy-start(f32[128,1024]{1,0:T(8,128)} %get-tuple-element.18) | copy-start | bytes 1572868
  38.7 24.0 %all-to-all-start.1 = ((bf16[8,256,128]{2,1,0:T(8,128)(2,1)}), bf16[8,256,128]{2,1,0:T(8,128)(2,1)S(1)}, u32[]{:S(2)}, u32[]{:S(2)}) async-start(bf16[8,256,128]{2,1,0:T(8,128)(2,1)} %bitcast.7), calls=%async_computation.1 | async-start | bytes 1048576 | tf_op jit(solution)/shard_map/all_to_all | solution.py:297
  47.0 13.8 %collective-permute-start.3 = (bf16[128,1024]{1,0:T(8,128)(2,1)}, bf16[128,1024]{1,0:T(8,128)(2,1)S(1)}, u32[]{:S(2)}, u32[]{:S(2)}) collective-permute-start(bf16[128,1024]{1,0:T(8,128)(2,1)} %get-tuple-element.19), channel_id=1, source_target_pairs={{0,56},{16,8},{32,24},{48,40},{8,16},{24,32},{40,48},{56,0},{1,57}... | collective-permute-start | bytes 786440 | tf_op jit(solution)/shard_map/ppermute | solution.py:299
  48.9 12.0 %collective-permute-start.4 = (bf16[128,1024]{1,0:T(8,128)(2,1)S(1)}, bf16[128,1024]{1,0:T(8,128)(2,1)S(1)}, u32[]{:S(2)}, u32[]{:S(2)}) collective-permute-start(bf16[128,1024]{1,0:T(8,128)(2,1)S(1)} %copy-done.3), channel_id=1, source_target_pairs={{0,16},{16,32},{32,48},{48,0},{24,8},{40,24},{56,40},{8,56},{1,17}... | collective-permute-start | bytes 786440 | tf_op jit(solution)/shard_map/ppermute | solution.py:299
  51.9 9.0 %collective-permute-start.5 = (bf16[128,1024]{1,0:T(8,128)(2,1)S(1)}, bf16[128,1024]{1,0:T(8,128)(2,1)S(1)}, u32[]{:S(2)}, u32[]{:S(2)}) collective-permute-start(bf16[128,1024]{1,0:T(8,128)(2,1)S(1)} %copy-done.2), channel_id=1, source_target_pairs={{0,8},{8,0},{1,9},{9,1},{2,10},{10,2},{3,11},{11,3},{4,12},{12,4},... | collective-permute-start | bytes 786440 | tf_op jit(solution)/shard_map/ppermute | solution.py:299

commit v7 on v6

--- a/solution.py
+++ b/solution.py
@@ -20,7 +20,7 @@
 SCALE = 1.0 / math.sqrt(HEAD)
 LOG2E = math.log2(math.e)
 CTX = ("yh", "xh", "xl", "core")
-KEEPERS = ("yh", "xh")
+KEEPERS = ("yh", "xl")
 NEXT = ("xh", "xl", "core")
 NT = (((1,), (1,)), ((), ()))
 TN = (((0,), (0,)), ((), ()))
@@ -189,12 +189,15 @@
         copy.wait()
 
 
-def total(got_ref, k_ref, v_ref):
-    both = got_ref[0].astype(jnp.float32)
+def finish(got_ref, own_ref, a_ref, b_ref, c_ref, dq_ref, k_ref, v_ref):
+    f32, bf16 = jnp.float32, jnp.bfloat16
+    both = got_ref[0].astype(f32)
     for i in range(1, PEERS):
-        both = both + got_ref[i].astype(jnp.float32)
-    k_ref[...] = both[:ROWS].astype(jnp.bfloat16)
-    v_ref[...] = both[ROWS:].astype(jnp.bfloat16)
+        both = both + got_ref[i].astype(f32)
+    k_ref[...] = both[:ROWS].astype(bf16)
+    v_ref[...] = both[ROWS:].astype(bf16)
+    parts = a_ref[...].astype(f32) + b_ref[...].astype(f32) + c_ref[...].astype(f32)
+    dq_ref[...] = (own_ref[...] + parts).astype(bf16)
 
 
 def plan(doc_lengths, block_order, yh, xh, xl, core):
@@ -203,8 +206,8 @@
     upto = jnp.arange(docs)[:, None] >= jnp.arange(docs)[None, :]
     ends = jnp.sum(jnp.where(upto, doc_lengths[None, :], 0), axis=1)
     blocks = jnp.arange(nblk, dtype=jnp.int32)
-    held_here = ((blocks // 2) % 2 == core) & ((blocks // 4) % 2 == xl)
-    place = (blocks // 8) * (2 * ROWS) + (blocks % 2) * BLOCK
+    held_here = ((blocks // 2) % 2 == core) & ((blocks // 8) % 2 == xh)
+    place = ((blocks // 16) * 2 + (blocks // 4) % 2) * (2 * ROWS) + (blocks % 2) * BLOCK
     before = held_here[None, :] & (block_order[None, :] < block_order[:, None])
     rank = jnp.sum(before.astype(jnp.int32), axis=1)
     slots = jnp.arange(nheld + 8, dtype=jnp.int32)
@@ -212,14 +215,10 @@
     held = jnp.sum(jnp.where(hit, block_order[None, :], 0), axis=1)
     held = jnp.where(slots < nheld, held, nblk)
     place = jnp.sum(jnp.where(hit, place[None, :], 0), axis=1)
-    x, turn = 2 * xh + xl, 1 - 2 * core
+    x = 2 * xh + xl
+    partner = (x + 2 * xl - 1) % 4
     owners = 8 * yh + jnp.stack(
-        [
-            2 * x + core,
-            2 * x + 1 - core,
-            2 * ((x + turn) % 4) + core,
-            2 * ((x - turn) % 4) + 1 - core,
-        ]
+        [2 * x + core, 2 * x + 1 - core, 2 * partner + core, 2 * partner + 1 - core]
     )
     stored = (2 * owners[:, None] + jnp.arange(2)[None, :]).reshape(8)
     mine = jnp.sum(jnp.where(stored[:, None] == blocks[None, :], block_order[None, :], 0), axis=1)
@@ -247,11 +246,9 @@
     dma = pltpu.SemaphoreType.DMA
 
     swap = [(0, 1), (1, 0)]
-    there = [(2 * ((i + 1) % 4), 2 * i) for i in range(4)]
-    there += [(2 * i + 1, 2 * ((i + 1) % 4) + 1) for i in range(4)]
-    back = [(j, i) for i, j in there]
-    across = [(2 * i, 2 * ((i - 1) % 4) + 1) for i in range(4)]
-    across += [(2 * i + 1, 2 * ((i + 1) % 4)) for i in range(4)]
+    partner = [3, 2, 1, 0]
+    facing = [(2 * i + c, 2 * partner[i] + c) for i in range(4) for c in range(2)]
+    across = [(2 * i + c, 2 * partner[i] + 1 - c) for i in range(4) for c in range(2)]
     sent, p0 = call(
         pack,
         (pltpu.HBM((PEERS, 2 * ROWS, HEAD), bf16), shape((2 * ROWS + EXTRA, WIDTH), bf16)),
@@ -267,7 +264,7 @@
         ],
     )
     kv = lax.all_to_all(sent, KEEPERS, 0, 0, tiled=True)
-    p2 = lax.ppermute(p0, NEXT, there)
+    p2 = lax.ppermute(p0, NEXT, facing)
     p3 = lax.ppermute(p2, "core", swap)
     work, held, at, first, own = plan(doc_lengths, block_order, *place)
     later, held = lax.optimization_barrier((p0, held))
@@ -295,10 +292,15 @@
         ],
     )
     got = lax.all_to_all(dkv.reshape(PEERS, 2 * ROWS, HEAD), KEEPERS, 0, 0, tiled=True)
-    routes = ((NEXT, across), (NEXT, back), ("core", swap))
+    routes = ((NEXT, across), (NEXT, facing), ("core", swap))
     parts = [lax.ppermute(x, axes, route) for x, (axes, route) in zip(others[::-1], routes)]
-    grad_q = (dq0 + sum(x.astype(f32) for x in parts)).astype(bf16)
-    grad_k, grad_v = call(total, (shape((ROWS, HEAD), bf16),) * 2, [VMEM], (VMEM,) * 2, got)
+    grad_q, grad_k, grad_v = call(
+        finish,
+        (shape((ROWS, WIDTH), bf16),) + (shape((ROWS, HEAD), bf16),) * 2,
+        [VMEM] * 5,
+        (VMEM,) * 3,
+        got, dq0, *parts,
+    )
     return grad_q, grad_k, grad_v
 
 

time: 63.9 us -> 64.2 us (level)
  waiting for transfers between devices: 10.4 us -> 11.9 us
  Pallas kernels: 9.2 us -> 7.98 us
  starting transfers between devices: 37.6 us -> 38.5 us
  other arithmetic: 2.5 us -> 1.66 us
    ppermute x1, starting transfers between devices: 2.21 us -> 4.62 us  [on_device(): p2 = lax.ppermute(p0, NEXT, facing)]
    ppermute x1, starting transfers between devices: 5.81 us -> 3.42 us  [on_device(): p1 = lax.ppermute(later, 'core', swap)]
    ppermute x3, starting transfers between devices: 7.85 us -> 10.2 us  [on_device(): lax.ppermute(x, axes, route)]
    all_to_all x1, starting transfers between devices: 10.1 us -> 8.59 us  [on_device(): kv = lax.all_to_all(sent, KEEPERS, 0, 0, tiled=True)]
    ppermute x3, waiting for transfers between devices: 6.05 us -> 7.43 us  [on_device(): lax.ppermute(x, axes, route)]
    ppermute x1, starting transfers between devices: 3.31 us -> 4.57 us  [on_device(): p3 = lax.ppermute(p2, 'core', swap)]
    pallas_call x3, Pallas kernels: 9.2 us -> 7.98 us  [call(): pl.pallas_call(kernel, out_shape=out, in_specs=ins, out_specs=outs, scrat...]
    all_to_all x1, starting transfers between devices: 8.28 us -> 7.12 us  [on_device(): lax.all_to_all(dkv.reshape(PEERS, 2 * ROWS, HEAD), KEEPERS, 0, 0, tiled=T...]
  transfers between devices with their start and end apart: 8 -> 8, of which waited for: 5 -> 4; matrix products, arithmetic and copies ran while one was open for 5% -> 4% of each run, Pallas kernels for 0% -> 0%
where the time goes in v7:
time: 64.2 us; the launch traced here: 63.7 us
  starting transfers between devices  38.5 us (60%)
  waiting for transfers between devices  11.9 us (19%)
  Pallas kernels  7.98 us (12%)
  local copies, waits for them, and re-layouts  2.14 us (3%)
  other arithmetic  1.66 us (3%)
  between operations  1.51 us (2%)
    ppermute x3, starting transfers between devices, on_device(): lax.ppermute(x, axes, route)  10.2 us
    all_to_all x1, starting transfers between devices, on_device(): kv = lax.all_to_all(sent, KEEPERS, 0, 0, tiled=True)  8.59 us
    pallas_call x3, Pallas kernels, call(): pl.pallas_call(kernel, out_shape=out, in_specs=ins, out_specs=outs, scrat...  7.98 us
    ppermute x3, waiting for transfers between devices, on_device(): lax.ppermute(x, axes, route)  7.43 us
    all_to_all x1, starting transfers between devices, on_device(): lax.all_to_all(dkv.reshape(PEERS, 2 * ROWS, HEAD), KEEPERS, 0, 0, tiled=T...  7.12 us
    ppermute x1, starting transfers between devices, on_device(): p2 = lax.ppermute(p0, NEXT, facing)  4.62 us
    ppermute x1, starting transfers between devices, on_device(): p3 = lax.ppermute(p2, 'core', swap)  4.57 us
    ppermute x1, starting transfers between devices, on_device(): p1 = lax.ppermute(later, 'core', swap)  3.42 us
  transfers between devices with their start and end apart: 8, of which 4 were waited for; matrix products, arithmetic and copies ran while one was open for 4% of the time, Pallas kernels for 0%

profile of v7, /device:TPU:1, one launch (start us, length us, event | category | flops | bytes accessed | tf_op | source)
XLA Modules:
  0.0 63.7 jit_solution(14192179102826753039)
XLA Ops:
  0.6 1.8 %pack.1 = (bf16[8,256,128]{2,1,0:T(8,128)(2,1)}, bf16[272,1024]{1,0:T(8,128)(2,1)S(1)}) custom-call(bf16[128,128]{1,0:T(8,128)(2,1)} %k_ref.1, bf16[128,128]{1,0:T(8,128)(2,1)} %v_ref.1, bf16[128,1024]{1,0:T(8,128)(2,1)} %q_ref.1, bf16[128,1024]{1,0:T(8,128)(2,1)} %do_ref.1, bf16[128,1024]{1,0:T(8,128)(2,1)} %o_ref.1, f32[8,128]{1,0:T(8,128)} %norm_ref.1), custom_call_target="tpu_custom_call" | custom-call | tf_op jit(solution)/shard_map/pack/pallas_call | solution.py:41
  2.4 8.6 %all-to-all-start = ((bf16[8,256,128]{2,1,0:T(8,128)(2,1)}), bf16[8,256,128]{2,1,0:T(8,128)(2,1)S(1)}, u32[]{:S(2)}, u32[]{:S(2)}) async-start(bf16[8,256,128]{2,1,0:T(8,128)(2,1)} %get-tuple-element.15), calls=%async_computation | async-start | bytes 1048576 | tf_op jit(solution)/shard_map/all_to_all | solution.py:266
  11.0 4.6 %collective-permute-start.1 = (bf16[272,1024]{1,0:T(8,128)(2,1)S(1)}, bf16[272,1024]{1,0:T(8,128)(2,1)S(1)}, u32[]{:S(2)}, u32[]{:S(2)}) collective-permute-start(bf16[272,1024]{1,0:T(8,128)(2,1)S(1)} %get-tuple-element.14.p0_ref), channel_id=1, source_target_pairs={{0,48},{8,56},{16,32},{24,40},{32,16},{40,24},{48,0},{56,8},{1,49}... | collective-permute-start | bytes 1671176 | tf_op jit(solution)/shard_map/ppermute | solution.py:267
  15.6 0.0 copy-start.1
  15.7 0.6 copy-done.1
  16.3 0.2 convert_reduce_fusion
  16.5 0.1 select_reduce_fusion.1
  16.6 3.4 %collective-permute-start = (bf16[272,1024]{1,0:T(8,128)(2,1)S(1)}, bf16[272,1024]{1,0:T(8,128)(2,1)S(1)}, u32[]{:S(2)}, u32[]{:S(2)}) collective-permute-start(bf16[272,1024]{1,0:T(8,128)(2,1)S(1)} %get-tuple-element.14.p0_ref), channel_id=1, source_target_pairs={{0,8},{8,0},{1,9},{9,1},{2,10},{10,2},{3,11},{11,3},{4,12},{12,4},... | collective-permute-start | bytes 1671176 | tf_op jit(solution)/shard_map/ppermute | solution.py:271
  20.1 0.0 copy-start.4
  20.1 0.6 %copy-done.4 = s32[16]{0:T(128)S(1)} copy-done((s32[16]{0:T(128)S(1)}, s32[16]{0:T(128)}, u32[]{:S(2)}) %copy-start.4) | copy-done | bytes 88
  20.7 0.1 select_reduce_fusion.3
  20.8 0.1 fusion.10
  20.9 0.1 iota_add_fusion.1
  21.0 0.1 add.170
  21.1 0.2 select_reduce_fusion.6
  21.3 0.1 iota_add_fusion
  21.4 0.1 select_reduce_fusion
  21.5 0.1 shift-right-arithmetic_reduce_fusion
  21.6 0.2 convert_reduce_fusion.2
  21.8 0.1 select_reduce_fusion.5
  21.9 0.6 slice.7
  23.2 0.1 tile.9.first_ref
  23.3 0.1 tile.21.own_ref
  23.3 3.2 %collective-permute-done.1.p2_ref = bf16[272,1024]{1,0:T(8,128)(2,1)S(1)} collective-permute-done((bf16[272,1024]{1,0:T(8,128)(2,1)S(1)}, bf16[272,1024]{1,0:T(8,128)(2,1)S(1)}, u32[]{:S(2)}, u32[]{:S(2)}) %collective-permute-start.1) | collective-permute-done | bytes 557088 | tf_op jit(solution)/shard_map/ppermute | solution.py:267
  26.5 4.6 %collective-permute-start.2 = (bf16[272,1024]{1,0:T(8,128)(2,1)S(1)}, bf16[272,1024]{1,0:T(8,128)(2,1)S(1)}, u32[]{:S(2)}, u32[]{:S(2)}) collective-permute-start(bf16[272,1024]{1,0:T(8,128)(2,1)S(1)} %collective-permute-done.1.p2_ref), channel_id=1, source_target_pairs={{0,8},{8,0},{1,9},{9,1},{2,10},{10,2},{3,11},{11,3},{4,12},{12,4},... | collective-permute-start | bytes 1671176 | tf_op jit(solution)/shard_map/ppermute | solution.py:268
  31.1 0.1 convert_reduce_fusion.1
  31.2 0.1 select_reduce_fusion.4
  31.3 0.1 pad_add_fusion.work_ref
  31.3 0.0 collective-permute-done.p1_ref
  31.4 0.0 all-to-all-done
  31.4 1.3 %collective-permute-done.2.p3_ref = bf16[272,1024]{1,0:T(8,128)(2,1)S(1)} collective-permute-done((bf16[272,1024]{1,0:T(8,128)(2,1)S(1)}, bf16[272,1024]{1,0:T(8,128)(2,1)S(1)}, u32[]{:S(2)}, u32[]{:S(2)}) %collective-permute-start.2) | collective-permute-done | bytes 557088 | tf_op jit(solution)/shard_map/ppermute | solution.py:268
  32.7 5.3 %terms.1 = (f32[128,1024]{1,0:T(8,128)}, bf16[128,1024]{1,0:T(8,128)(2,1)}, bf16[128,1024]{1,0:T(8,128)(2,1)}, bf16[128,1024]{1,0:T(8,128)(2,1)}, bf16[2048,128]{1,0:T(8,128)(2,1)}) custom-call(s32[145]{0:T(256)S(1)} %pad_add_fusion.work_ref, s32[24]{0:T(128)S(1)} %compare_select_fusion.7.held_ref, s32[24]{0:T(128)S(1)} %get-tuple-element.21.place_ref, ...), custom_call_target="tpu_custom_call" | custom-call | tf_op jit(solution)/shard_map/terms/pallas_call | solution.py:41
  38.0 0.0 copy-start.3
  38.0 0.0 copy-start.2
  38.0 0.0 copy-start
  38.0 7.1 %all-to-all-start.1 = ((bf16[8,256,128]{2,1,0:T(8,128)(2,1)}), bf16[8,256,128]{2,1,0:T(8,128)(2,1)S(1)}, u32[]{:S(2)}, u32[]{:S(2)}) async-start(bf16[8,256,128]{2,1,0:T(8,128)(2,1)} %bitcast.7), calls=%async_computation.1 | async-start | bytes 1048576 | tf_op jit(solution)/shard_map/all_to_all | solution.py:294
  45.2 5.9 %collective-permute-start.3 = (bf16[128,1024]{1,0:T(8,128)(2,1)}, bf16[128,1024]{1,0:T(8,128)(2,1)S(1)}, u32[]{:S(2)}, u32[]{:S(2)}) collective-permute-start(bf16[128,1024]{1,0:T(8,128)(2,1)} %get-tuple-element.18), channel_id=1, source_target_pairs={{0,56},{8,48},{16,40},{24,32},{32,24},{40,16},{48,8},{56,0},{1,57}... | collective-permute-start | bytes 786440 | tf_op jit(solution)/shard_map/ppermute | solution.py:296
  51.1 0.0 copy-done.3
  51.1 1.9 %collective-permute-start.4 = (bf16[128,1024]{1,0:T(8,128)(2,1)S(1)}, bf16[128,1024]{1,0:T(8,128)(2,1)S(1)}, u32[]{:S(2)}, u32[]{:S(2)}) collective-permute-start(bf16[128,1024]{1,0:T(8,128)(2,1)S(1)} %copy-done.3), channel_id=1, source_target_pairs={{0,48},{8,56},{16,32},{24,40},{32,16},{40,24},{48,0},{56,8},{1,49}... | collective-permute-start | bytes 786440 | tf_op jit(solution)/shard_map/ppermute | solution.py:296
  53.0 0.0 copy-done.2
  53.1 2.3 %collective-permute-start.5 = (bf16[128,1024]{1,0:T(8,128)(2,1)S(1)}, bf16[128,1024]{1,0:T(8,128)(2,1)S(1)}, u32[]{:S(2)}, u32[]{:S(2)}) collective-permute-start(bf16[128,1024]{1,0:T(8,128)(2,1)S(1)} %copy-done.2), channel_id=1, source_target_pairs={{0,8},{8,0},{1,9},{9,1},{2,10},{10,2},{3,11},{11,3},{4,12},{12,4},... | collective-permute-start | bytes 786440 | tf_op jit(solution)/shard_map/ppermute | solution.py:296
  55.4 2.9 %collective-permute-done.3.a_ref = bf16[128,1024]{1,0:T(8,128)(2,1)S(1)} collective-permute-done((bf16[128,1024]{1,0:T(8,128)(2,1)}, bf16[128,1024]{1,0:T(8,128)(2,1)S(1)}, u32[]{:S(2)}, u32[]{:S(2)}) %collective-permute-start.3) | collective-permute-done | bytes 262176 | tf_op jit(solution)/shard_map/ppermute | solution.py:296
  58.3 4.5 %collective-permute-done.4.b_ref = bf16[128,1024]{1,0:T(8,128)(2,1)S(1)} collective-permute-done((bf16[128,1024]{1,0:T(8,128)(2,1)S(1)}, bf16[128,1024]{1,0:T(8,128)(2,1)S(1)}, u32[]{:S(2)}, u32[]{:S(2)}) %collective-permute-start.4) | collective-permute-done | bytes 262176 | tf_op jit(solution)/shard_map/ppermute | solution.py:296
  62.8 0.0 collective-permute-done.5.c_ref
  62.8 0.0 all-to-all-done.1.got_ref
  62.8 0.0 copy-done
  62.8 0.9 %finish.1 = (bf16[128,1024]{1,0:T(8,128)(2,1)}, bf16[128,128]{1,0:T(8,128)(2,1)}, bf16[128,128]{1,0:T(8,128)(2,1)}) custom-call(bf16[8,256,128]{2,1,0:T(8,128)(2,1)S(1)} %all-to-all-done.1.got_ref, f32[128,1024]{1,0:T(8,128)S(1)} %copy-done, bf16[128,1024]{1,0:T(8,128)(2,1)S(1)} %collective-permute-done.3.a_ref, ...), custom_call_target="tpu_custom_call" | custom-call | tf_op jit(solution)/shard_map/finish/pallas_call | solution.py:41
  (9 shorter events, 0.1 us)
Async XLA Ops:
  2.4 29.0 %all-to-all-start = ((bf16[8,256,128]{2,1,0:T(8,128)(2,1)}), bf16[8,256,128]{2,1,0:T(8,128)(2,1)S(1)}, u32[]{:S(2)}, u32[]{:S(2)}) async-start(bf16[8,256,128]{2,1,0:T(8,128)(2,1)} %get-tuple-element.15), calls=%async_computation | async-start | bytes 1048576 | tf_op jit(solution)/shard_map/all_to_all | solution.py:266
  11.0 15.5 %collective-permute-start.1 = (bf16[272,1024]{1,0:T(8,128)(2,1)S(1)}, bf16[272,1024]{1,0:T(8,128)(2,1)S(1)}, u32[]{:S(2)}, u32[]{:S(2)}) collective-permute-start(bf16[272,1024]{1,0:T(8,128)(2,1)S(1)} %get-tuple-element.14.p0_ref), channel_id=1, source_target_pairs={{0,48},{8,56},{16,32},{24,40},{32,16},{40,24},{48,0},{56,8},{1,49}... | collective-permute-start | bytes 1671176 | tf_op jit(solution)/shard_map/ppermute | solution.py:267
  15.6 0.7 %copy-start.1 = (s32[64]{0:T(128)S(1)}, s32[64]{0:T(128)}, u32[]{:S(2)}) copy-start(s32[64]{0:T(128)} %param.15) | copy-start | bytes 772
  16.6 14.7 %collective-permute-start = (bf16[272,1024]{1,0:T(8,128)(2,1)S(1)}, bf16[272,1024]{1,0:T(8,128)(2,1)S(1)}, u32[]{:S(2)}, u32[]{:S(2)}) collective-permute-start(bf16[272,1024]{1,0:T(8,128)(2,1)S(1)} %get-tuple-element.14.p0_ref), channel_id=1, source_target_pairs={{0,8},{8,0},{1,9},{9,1},{2,10},{10,2},{3,11},{11,3},{4,12},{12,4},... | collective-permute-start | bytes 1671176 | tf_op jit(solution)/shard_map/ppermute | solution.py:271
  20.1 0.7 %copy-start.4 = (s32[16]{0:T(128)S(1)}, s32[16]{0:T(128)}, u32[]{:S(2)}) copy-start(s32[16]{0:T(128)} %param.14) | copy-start | bytes 196
  26.5 6.1 %collective-permute-start.2 = (bf16[272,1024]{1,0:T(8,128)(2,1)S(1)}, bf16[272,1024]{1,0:T(8,128)(2,1)S(1)}, u32[]{:S(2)}, u32[]{:S(2)}) collective-permute-start(bf16[272,1024]{1,0:T(8,128)(2,1)S(1)} %collective-permute-done.1.p2_ref), channel_id=1, source_target_pairs={{0,8},{8,0},{1,9},{9,1},{2,10},{10,2},{3,11},{11,3},{4,12},{12,4},... | collective-permute-start | bytes 1671176 | tf_op jit(solution)/shard_map/ppermute | solution.py:268
  38.0 13.1 %copy-start.3 = (bf16[128,1024]{1,0:T(8,128)(2,1)S(1)}, bf16[128,1024]{1,0:T(8,128)(2,1)}, u32[]{:S(2)}) copy-start(bf16[128,1024]{1,0:T(8,128)(2,1)} %get-tuple-element.19) | copy-start | bytes 786436
  38.0 15.0 %copy-start.2 = (bf16[128,1024]{1,0:T(8,128)(2,1)S(1)}, bf16[128,1024]{1,0:T(8,128)(2,1)}, u32[]{:S(2)}) copy-start(bf16[128,1024]{1,0:T(8,128)(2,1)} %get-tuple-element.20) | copy-start | bytes 786436
  38.0 24.8 %copy-start = (f32[128,1024]{1,0:T(8,128)S(1)}, f32[128,1024]{1,0:T(8,128)}, u32[]{:S(2)}) copy-start(f32[128,1024]{1,0:T(8,128)} %get-tuple-element.17.own_ref) | copy-start | bytes 1572868
  38.0 24.8 %all-to-all-start.1 = ((bf16[8,256,128]{2,1,0:T(8,128)(2,1)}), bf16[8,256,128]{2,1,0:T(8,128)(2,1)S(1)}, u32[]{:S(2)}, u32[]{:S(2)}) async-start(bf16[8,256,128]{2,1,0:T(8,128)(2,1)} %bitcast.7), calls=%async_computation.1 | async-start | bytes 1048576 | tf_op jit(solution)/shard_map/all_to_all | solution.py:294
  45.2 13.1 %collective-permute-start.3 = (bf16[128,1024]{1,0:T(8,128)(2,1)}, bf16[128,1024]{1,0:T(8,128)(2,1)S(1)}, u32[]{:S(2)}, u32[]{:S(2)}) collective-permute-start(bf16[128,1024]{1,0:T(8,128)(2,1)} %get-tuple-element.18), channel_id=1, source_target_pairs={{0,56},{8,48},{16,40},{24,32},{32,24},{40,16},{48,8},{56,0},{1,57}... | collective-permute-start | bytes 786440 | tf_op jit(solution)/shard_map/ppermute | solution.py:296
  51.1 11.7 %collective-permute-start.4 = (bf16[128,1024]{1,0:T(8,128)(2,1)S(1)}, bf16[128,1024]{1,0:T(8,128)(2,1)S(1)}, u32[]{:S(2)}, u32[]{:S(2)}) collective-permute-start(bf16[128,1024]{1,0:T(8,128)(2,1)S(1)} %copy-done.3), channel_id=1, source_target_pairs={{0,48},{8,56},{16,32},{24,40},{32,16},{40,24},{48,0},{56,8},{1,49}... | collective-permute-start | bytes 786440 | tf_op jit(solution)/shard_map/ppermute | solution.py:296
  53.1 9.7 %collective-permute-start.5 = (bf16[128,1024]{1,0:T(8,128)(2,1)S(1)}, bf16[128,1024]{1,0:T(8,128)(2,1)S(1)}, u32[]{:S(2)}, u32[]{:S(2)}) collective-permute-start(bf16[128,1024]{1,0:T(8,128)(2,1)S(1)} %copy-done.2), channel_id=1, source_target_pairs={{0,8},{8,0},{1,9},{9,1},{2,10},{10,2},{3,11},{11,3},{4,12},{12,4},... | collective-permute-start | bytes 786440 | tf_op jit(solution)/shard_map/ppermute | solution.py:296

commit v8 on v7

--- a/solution.py
+++ b/solution.py
@@ -129,8 +129,8 @@
 
 def terms(
     work_ref, held_ref, place_ref, first_ref, own_ref, p0_ref, p1_ref, p2_ref, p3_ref, kv_ref,
-    dq0_ref, dq1_ref, dq2_ref, dq3_ref, dkv_ref,
-    acc_ref, half_ref, dqt_ref, own_buf, send_buf, q_ref, do_ref, norm_ref, dot_ref, sem,
+    dq0_ref, dq2_ref, side_ref, dkv_ref,
+    acc_ref, half_ref, dqt_ref, keep_buf, side_buf, q_ref, do_ref, norm_ref, dot_ref, sem,
 ):
     acc_ref[...] = jnp.zeros_like(acc_ref)
     dqt_ref[...] = jnp.zeros_like(dqt_ref)
@@ -175,28 +175,32 @@
         half_ref[at, :] = acc_ref[at, :].astype(jnp.bfloat16)
         copies.append(pltpu.make_async_copy(half_ref.at[at], dkv_ref.at[at], sem.at[i]))
         copies[-1].start()
-    for g in (3, 2, 1, 0):
-        out = send_buf.at[g - 1] if g else own_buf
+    for g in (1, 3, 2, 0):
+        buf, to = (side_buf, side_ref) if g % 2 else (keep_buf, (dq0_ref, dq2_ref)[g // 2])
         for i in range(2):
             b = 2 * g + i
-            dq = dqt_ref[b * HEAD : (b + 1) * HEAD, :].T.astype(out.dtype)
+            dq = dqt_ref[b * HEAD : (b + 1) * HEAD, :].T.astype(buf.dtype)
             for h in range(HEADS):
-                out[i * BLOCK : (i + 1) * BLOCK, head(h)] = dq[h * BLOCK : (h + 1) * BLOCK]
-        to = (dq0_ref, dq1_ref, dq2_ref, dq3_ref)[g]
-        copies.append(pltpu.make_async_copy(out, to, sem.at[4 + g]))
+                buf[g // 2, i * BLOCK : (i + 1) * BLOCK, head(h)] = dq[h * BLOCK : (h + 1) * BLOCK]
+        to = to.at[g // 2] if g % 2 else to
+        copies.append(pltpu.make_async_copy(buf.at[g // 2], to, sem.at[4 + g]))
         copies[-1].start()
     for copy in copies:
         copy.wait()
 
 
-def finish(got_ref, own_ref, a_ref, b_ref, c_ref, dq_ref, k_ref, v_ref):
+def pass_on(dq_ref, side_ref, out_ref):
+    out_ref[...] = (dq_ref[...] + side_ref[1].astype(jnp.float32)).astype(jnp.bfloat16)
+
+
+def finish(got_ref, own_ref, side_ref, far_ref, dq_ref, k_ref, v_ref):
     f32, bf16 = jnp.float32, jnp.bfloat16
     both = got_ref[0].astype(f32)
     for i in range(1, PEERS):
         both = both + got_ref[i].astype(f32)
     k_ref[...] = both[:ROWS].astype(bf16)
     v_ref[...] = both[ROWS:].astype(bf16)
-    parts = a_ref[...].astype(f32) + b_ref[...].astype(f32) + c_ref[...].astype(f32)
+    parts = side_ref[0].astype(f32) + far_ref[...].astype(f32)
     dq_ref[...] = (own_ref[...] + parts).astype(bf16)
 
 
@@ -248,7 +252,6 @@
     swap = [(0, 1), (1, 0)]
     partner = [3, 2, 1, 0]
     facing = [(2 * i + c, 2 * partner[i] + c) for i in range(4) for c in range(2)]
-    across = [(2 * i + c, 2 * partner[i] + 1 - c) for i in range(4) for c in range(2)]
     sent, p0 = call(
         pack,
         (pltpu.HBM((PEERS, 2 * ROWS, HEAD), bf16), shape((2 * ROWS + EXTRA, WIDTH), bf16)),
@@ -270,20 +273,19 @@
     later, held = lax.optimization_barrier((p0, held))
     p1 = lax.ppermute(later, "core", swap)
     nkeys = 2 * PEERS * ROWS
-    dq0, *others, dkv = call(
+    dq0, dq2, side, dkv = call(
         terms,
-        (pltpu.HBM((ROWS, WIDTH), f32),)
-        + (pltpu.HBM((ROWS, WIDTH), bf16),) * 3
-        + (pltpu.HBM((nkeys, HEAD), bf16),),
+        (pltpu.HBM((ROWS, WIDTH), f32),) * 2
+        + (pltpu.HBM((2, ROWS, WIDTH), bf16), pltpu.HBM((nkeys, HEAD), bf16)),
         [SMEM] * 3 + [VMEM] * 7,
-        (HBM,) * 5,
+        (HBM,) * 4,
         work, held, at, first, own, p0, p1, p2, p3, kv.reshape(nkeys, HEAD),
         scratch=[
             pltpu.VMEM((nkeys, HEAD), f32),
             pltpu.VMEM((nkeys, HEAD), bf16),
             pltpu.VMEM((8 * HEAD, LANES), f32),
-            pltpu.VMEM((ROWS, WIDTH), f32),
-            pltpu.VMEM((3, ROWS, WIDTH), bf16),
+            pltpu.VMEM((2, ROWS, WIDTH), f32),
+            pltpu.VMEM((2, ROWS, WIDTH), bf16),
             pltpu.VMEM((8 * LANES, HEAD), bf16),
             pltpu.VMEM((8 * LANES, HEAD), bf16),
             pltpu.VMEM((8, LANES), f32),
@@ -292,14 +294,15 @@
         ],
     )
     got = lax.all_to_all(dkv.reshape(PEERS, 2 * ROWS, HEAD), KEEPERS, 0, 0, tiled=True)
-    routes = ((NEXT, across), (NEXT, facing), ("core", swap))
-    parts = [lax.ppermute(x, axes, route) for x, (axes, route) in zip(others[::-1], routes)]
+    side = lax.ppermute(side, "core", swap)
+    far = call(pass_on, shape((ROWS, WIDTH), bf16), [VMEM] * 2, VMEM, dq2, side)
+    far = lax.ppermute(far, NEXT, facing)
     grad_q, grad_k, grad_v = call(
         finish,
         (shape((ROWS, WIDTH), bf16),) + (shape((ROWS, HEAD), bf16),) * 2,
-        [VMEM] * 5,
+        [VMEM] * 4,
         (VMEM,) * 3,
-        got, dq0, *parts,
+        got, dq0, side, far,
     )
     return grad_q, grad_k, grad_v
 

time: 64.2 us -> 63.3 us (0.986)
  starting transfers between devices: 38.5 us -> 35.5 us
  waiting for transfers between devices: 11.9 us -> 12.9 us
  Pallas kernels: 7.98 us -> 8.83 us
    ppermute x3 -> x2, starting transfers between devices: 10.2 us -> 7.88 us  [the longest x1 5.96 us: on_device(): far = lax.ppermute(far, NEXT, facing)]
    ppermute x3 -> x2, waiting for transfers between devices: 7.43 us -> 8.41 us  [the longest x1 6.53 us: on_device(): far = lax.ppermute(far, NEXT, facing)]
    pallas_call x3 -> x4, Pallas kernels: 7.98 us -> 8.83 us  [call(): pl.pallas_call(kernel, out_shape=out, in_specs=ins, out_specs=outs, scrat...]
    all_to_all x1, starting transfers between devices: 7.12 us -> 6.42 us  [on_device(): lax.all_to_all(dkv.reshape(PEERS, 2 * ROWS, HEAD), KEEPERS, 0, 0, tiled=T...]
  transfers between devices with their start and end apart: 8 -> 7, of which waited for: 4 -> 4; matrix products, arithmetic and copies ran while one was open for 4% -> 4% of each run, Pallas kernels for 0% -> 0%
where the time goes in v8:
time: 63.3 us; the launch traced here: 62.5 us
  starting transfers between devices  35.5 us (56%)
  waiting for transfers between devices  12.9 us (20%)
  Pallas kernels  8.83 us (14%)
  local copies, waits for them, and re-layouts  2.13 us (3%)
  other arithmetic  1.66 us (3%)
  between operations  1.49 us (2%)
    pallas_call x4, Pallas kernels, call(): pl.pallas_call(kernel, out_shape=out, in_specs=ins, out_specs=outs, scrat...  8.83 us
    all_to_all x1, starting transfers between devices, on_device(): kv = lax.all_to_all(sent, KEEPERS, 0, 0, tiled=True)  8.59 us
    ppermute x1, waiting for transfers between devices, on_device(): far = lax.ppermute(far, NEXT, facing)  6.53 us
    all_to_all x1, starting transfers between devices, on_device(): lax.all_to_all(dkv.reshape(PEERS, 2 * ROWS, HEAD), KEEPERS, 0, 0, tiled=T...  6.42 us
    ppermute x1, starting transfers between devices, on_device(): far = lax.ppermute(far, NEXT, facing)  5.96 us
    ppermute x1, starting transfers between devices, on_device(): p2 = lax.ppermute(p0, NEXT, facing)  4.62 us
    ppermute x1, starting transfers between devices, on_device(): p3 = lax.ppermute(p2, 'core', swap)  4.57 us
    ppermute x1, starting transfers between devices, on_device(): p1 = lax.ppermute(later, 'core', swap)  3.42 us
  transfers between devices with their start and end apart: 7, of which 4 were waited for; matrix products, arithmetic and copies ran while one was open for 4% of the time, Pallas kernels for 0%

profile of v8, /device:TPU:1, one launch (start us, length us, event | category | flops | bytes accessed | tf_op | source)
XLA Modules:
  0.0 62.5 jit_solution(3590404915418406467)
XLA Ops:
  0.6 1.8 %pack.1 = (bf16[8,256,128]{2,1,0:T(8,128)(2,1)}, bf16[272,1024]{1,0:T(8,128)(2,1)S(1)}) custom-call(bf16[128,128]{1,0:T(8,128)(2,1)} %k_ref.1, bf16[128,128]{1,0:T(8,128)(2,1)} %v_ref.1, bf16[128,1024]{1,0:T(8,128)(2,1)} %q_ref.1, bf16[128,1024]{1,0:T(8,128)(2,1)} %do_ref.1, bf16[128,1024]{1,0:T(8,128)(2,1)} %o_ref.1, f32[8,128]{1,0:T(8,128)} %norm_ref.1), custom_call_target="tpu_custom_call" | custom-call | tf_op jit(solution)/shard_map/pack/pallas_call | solution.py:41
  2.4 8.6 %all-to-all-start = ((bf16[8,256,128]{2,1,0:T(8,128)(2,1)}), bf16[8,256,128]{2,1,0:T(8,128)(2,1)S(1)}, u32[]{:S(2)}, u32[]{:S(2)}) async-start(bf16[8,256,128]{2,1,0:T(8,128)(2,1)} %get-tuple-element.14), calls=%async_computation | async-start | bytes 1048576 | tf_op jit(solution)/shard_map/all_to_all | solution.py:269
  11.0 4.6 %collective-permute-start.1 = (bf16[272,1024]{1,0:T(8,128)(2,1)S(1)}, bf16[272,1024]{1,0:T(8,128)(2,1)S(1)}, u32[]{:S(2)}, u32[]{:S(2)}) collective-permute-start(bf16[272,1024]{1,0:T(8,128)(2,1)S(1)} %get-tuple-element.13.p0_ref), channel_id=1, source_target_pairs={{0,48},{8,56},{16,32},{24,40},{32,16},{40,24},{48,0},{56,8},{1,49}... | collective-permute-start | bytes 1671176 | tf_op jit(solution)/shard_map/ppermute | solution.py:270
  15.6 0.0 copy-start.2
  15.7 0.6 %copy-done.2 = s32[64]{0:T(128)S(1)} copy-done((s32[64]{0:T(128)S(1)}, s32[64]{0:T(128)}, u32[]{:S(2)}) %copy-start.2) | copy-done | bytes 280
  16.3 0.2 convert_reduce_fusion
  16.5 0.1 select_reduce_fusion.1
  16.6 3.4 %collective-permute-start = (bf16[272,1024]{1,0:T(8,128)(2,1)S(1)}, bf16[272,1024]{1,0:T(8,128)(2,1)S(1)}, u32[]{:S(2)}, u32[]{:S(2)}) collective-permute-start(bf16[272,1024]{1,0:T(8,128)(2,1)S(1)} %get-tuple-element.13.p0_ref), channel_id=1, source_target_pairs={{0,8},{8,0},{1,9},{9,1},{2,10},{10,2},{3,11},{11,3},{4,12},{12,4},... | collective-permute-start | bytes 1671176 | tf_op jit(solution)/shard_map/ppermute | solution.py:274
  20.1 0.0 copy-start.4
  20.1 0.6 %copy-done.4 = s32[16]{0:T(128)S(1)} copy-done((s32[16]{0:T(128)S(1)}, s32[16]{0:T(128)}, u32[]{:S(2)}) %copy-start.4) | copy-done | bytes 88
  20.7 0.1 select_reduce_fusion.3
  20.8 0.1 fusion.10
  20.9 0.1 iota_add_fusion.1
  21.0 0.1 add.170
  21.1 0.2 select_reduce_fusion.6
  21.3 0.1 iota_add_fusion
  21.4 0.1 select_reduce_fusion
  21.5 0.1 shift-right-arithmetic_reduce_fusion
  21.6 0.2 convert_reduce_fusion.2
  21.8 0.1 select_reduce_fusion.5
  21.9 0.6 slice.7
  23.2 0.1 tile.9.first_ref
  23.3 0.1 tile.21.own_ref
  23.3 3.2 %collective-permute-done.1.p2_ref = bf16[272,1024]{1,0:T(8,128)(2,1)S(1)} collective-permute-done((bf16[272,1024]{1,0:T(8,128)(2,1)S(1)}, bf16[272,1024]{1,0:T(8,128)(2,1)S(1)}, u32[]{:S(2)}, u32[]{:S(2)}) %collective-permute-start.1) | collective-permute-done | bytes 557088 | tf_op jit(solution)/shard_map/ppermute | solution.py:270
  26.5 4.6 %collective-permute-start.2 = (bf16[272,1024]{1,0:T(8,128)(2,1)S(1)}, bf16[272,1024]{1,0:T(8,128)(2,1)S(1)}, u32[]{:S(2)}, u32[]{:S(2)}) collective-permute-start(bf16[272,1024]{1,0:T(8,128)(2,1)S(1)} %collective-permute-done.1.p2_ref), channel_id=1, source_target_pairs={{0,8},{8,0},{1,9},{9,1},{2,10},{10,2},{3,11},{11,3},{4,12},{12,4},... | collective-permute-start | bytes 1671176 | tf_op jit(solution)/shard_map/ppermute | solution.py:271
  31.1 0.1 convert_reduce_fusion.1
  31.2 0.1 select_reduce_fusion.4
  31.3 0.1 pad_add_fusion.work_ref
  31.3 0.0 collective-permute-done.p1_ref
  31.4 0.0 all-to-all-done
  31.4 1.3 %collective-permute-done.2.p3_ref = bf16[272,1024]{1,0:T(8,128)(2,1)S(1)} collective-permute-done((bf16[272,1024]{1,0:T(8,128)(2,1)S(1)}, bf16[272,1024]{1,0:T(8,128)(2,1)S(1)}, u32[]{:S(2)}, u32[]{:S(2)}) %collective-permute-start.2) | collective-permute-done | bytes 557088 | tf_op jit(solution)/shard_map/ppermute | solution.py:271
  32.7 6.2 %terms.1 = (f32[128,1024]{1,0:T(8,128)}, f32[128,1024]{1,0:T(8,128)}, bf16[2,128,1024]{2,1,0:T(8,128)(2,1)}, bf16[2048,128]{1,0:T(8,128)(2,1)}) custom-call(s32[145]{0:T(256)S(1)} %pad_add_fusion.work_ref, s32[24]{0:T(128)S(1)} %compare_select_fusion.7.held_ref, s32[24]{0:T(128)S(1)} %get-tuple-element.19.place_ref, s32[8,512]{1,0:T(8,128)S(1)} %tile.9.first_ref, ...), custom_call_target="tpu_custom_call" | custom-call | tf_op jit(solution)/shard_map/terms/pallas_call | solution.py:41
  38.8 0.0 copy-start.3
  38.8 0.0 copy-start.1
  38.9 6.4 %all-to-all-start.1 = ((bf16[8,256,128]{2,1,0:T(8,128)(2,1)}), bf16[8,256,128]{2,1,0:T(8,128)(2,1)S(1)}, u32[]{:S(2)}, u32[]{:S(2)}) async-start(bf16[8,256,128]{2,1,0:T(8,128)(2,1)} %bitcast.7), calls=%async_computation.1 | async-start | bytes 1048576 | tf_op jit(solution)/shard_map/all_to_all | solution.py:296
  45.3 0.0 copy-done.3
  45.3 1.9 %collective-permute-start.3 = (bf16[2,128,1024]{2,1,0:T(8,128)(2,1)S(1)}, bf16[2,128,1024]{2,1,0:T(8,128)(2,1)S(1)}, u32[]{:S(2)}, u32[]{:S(2)}) collective-permute-start(bf16[2,128,1024]{2,1,0:T(8,128)(2,1)S(1)} %copy-done.3), channel_id=1, source_target_pairs={{0,8},{8,0},{1,9},{9,1},{2,10},{10,2},{3,11},{11,3},{4,12},{12,4},... | collective-permute-start | bytes 1572872 | tf_op jit(solution)/shard_map/ppermute | solution.py:297
  47.2 1.9 %collective-permute-done.3.side_ref = bf16[2,128,1024]{2,1,0:T(8,128)(2,1)S(1)} collective-permute-done((bf16[2,128,1024]{2,1,0:T(8,128)(2,1)S(1)}, bf16[2,128,1024]{2,1,0:T(8,128)(2,1)S(1)}, u32[]{:S(2)}, u32[]{:S(2)}) %collective-permute-start.3) | collective-permute-done | bytes 524320 | tf_op jit(solution)/shard_map/ppermute | solution.py:297
  49.1 0.0 copy-done.1
  49.1 0.0 copy-start
  49.1 6.0 %collective-permute-start.4 = (bf16[128,1024]{1,0:T(8,128)(2,1)S(1)}, bf16[128,1024]{1,0:T(8,128)(2,1)S(1)}, u32[]{:S(2)}, u32[]{:S(2)}) collective-permute-start(bf16[128,1024]{1,0:T(8,128)(2,1)S(1)} %pass_on.1), channel_id=1, source_target_pairs={{0,48},{8,56},{16,32},{24,40},{32,16},{40,24},{48,0},{56,8},{1,49}... | collective-permute-start | bytes 786440 | tf_op jit(solution)/shard_map/ppermute | solution.py:299
  55.1 6.5 %collective-permute-done.4.far_ref = bf16[128,1024]{1,0:T(8,128)(2,1)S(1)} collective-permute-done((bf16[128,1024]{1,0:T(8,128)(2,1)S(1)}, bf16[128,1024]{1,0:T(8,128)(2,1)S(1)}, u32[]{:S(2)}, u32[]{:S(2)}) %collective-permute-start.4) | collective-permute-done | bytes 262176 | tf_op jit(solution)/shard_map/ppermute | solution.py:299
  61.6 0.0 all-to-all-done.1.got_ref
  61.6 0.0 copy-done
  61.6 0.9 %finish.1 = (bf16[128,1024]{1,0:T(8,128)(2,1)}, bf16[128,128]{1,0:T(8,128)(2,1)}, bf16[128,128]{1,0:T(8,128)(2,1)}) custom-call(bf16[8,256,128]{2,1,0:T(8,128)(2,1)S(1)} %all-to-all-done.1.got_ref, f32[128,1024]{1,0:T(8,128)S(1)} %copy-done, bf16[2,128,1024]{2,1,0:T(8,128)(2,1)S(1)} %collective-permute-done.3.side_ref, ...), custom_call_target="tpu_custom_call" | custom-call | tf_op jit(solution)/shard_map/finish/pallas_call | solution.py:41
  (10 shorter events, 0.1 us)
Async XLA Ops:
  2.4 29.0 %all-to-all-start = ((bf16[8,256,128]{2,1,0:T(8,128)(2,1)}), bf16[8,256,128]{2,1,0:T(8,128)(2,1)S(1)}, u32[]{:S(2)}, u32[]{:S(2)}) async-start(bf16[8,256,128]{2,1,0:T(8,128)(2,1)} %get-tuple-element.14), calls=%async_computation | async-start | bytes 1048576 | tf_op jit(solution)/shard_map/all_to_all | solution.py:269
  11.0 15.5 %collective-permute-start.1 = (bf16[272,1024]{1,0:T(8,128)(2,1)S(1)}, bf16[272,1024]{1,0:T(8,128)(2,1)S(1)}, u32[]{:S(2)}, u32[]{:S(2)}) collective-permute-start(bf16[272,1024]{1,0:T(8,128)(2,1)S(1)} %get-tuple-element.13.p0_ref), channel_id=1, source_target_pairs={{0,48},{8,56},{16,32},{24,40},{32,16},{40,24},{48,0},{56,8},{1,49}... | collective-permute-start | bytes 1671176 | tf_op jit(solution)/shard_map/ppermute | solution.py:270
  15.6 0.7 %copy-start.2 = (s32[64]{0:T(128)S(1)}, s32[64]{0:T(128)}, u32[]{:S(2)}) copy-start(s32[64]{0:T(128)} %param.15) | copy-start | bytes 772
  16.6 14.7 %collective-permute-start = (bf16[272,1024]{1,0:T(8,128)(2,1)S(1)}, bf16[272,1024]{1,0:T(8,128)(2,1)S(1)}, u32[]{:S(2)}, u32[]{:S(2)}) collective-permute-start(bf16[272,1024]{1,0:T(8,128)(2,1)S(1)} %get-tuple-element.13.p0_ref), channel_id=1, source_target_pairs={{0,8},{8,0},{1,9},{9,1},{2,10},{10,2},{3,11},{11,3},{4,12},{12,4},... | collective-permute-start | bytes 1671176 | tf_op jit(solution)/shard_map/ppermute | solution.py:274
  20.1 0.7 %copy-start.4 = (s32[16]{0:T(128)S(1)}, s32[16]{0:T(128)}, u32[]{:S(2)}) copy-start(s32[16]{0:T(128)} %param.14) | copy-start | bytes 196
  26.5 6.1 %collective-permute-start.2 = (bf16[272,1024]{1,0:T(8,128)(2,1)S(1)}, bf16[272,1024]{1,0:T(8,128)(2,1)S(1)}, u32[]{:S(2)}, u32[]{:S(2)}) collective-permute-start(bf16[272,1024]{1,0:T(8,128)(2,1)S(1)} %collective-permute-done.1.p2_ref), channel_id=1, source_target_pairs={{0,8},{8,0},{1,9},{9,1},{2,10},{10,2},{3,11},{11,3},{4,12},{12,4},... | collective-permute-start | bytes 1671176 | tf_op jit(solution)/shard_map/ppermute | solution.py:271
  38.8 6.4 %copy-start.3 = (bf16[2,128,1024]{2,1,0:T(8,128)(2,1)S(1)}, bf16[2,128,1024]{2,1,0:T(8,128)(2,1)}, u32[]{:S(2)}) copy-start(bf16[2,128,1024]{2,1,0:T(8,128)(2,1)} %get-tuple-element.17) | copy-start | bytes 1572868
  38.8 10.2 %copy-start.1 = (f32[128,1024]{1,0:T(8,128)S(1)}, f32[128,1024]{1,0:T(8,128)}, u32[]{:S(2)}) copy-start(f32[128,1024]{1,0:T(8,128)} %get-tuple-element.18.dq_ref) | copy-start | bytes 1572868
  38.9 22.8 %all-to-all-start.1 = ((bf16[8,256,128]{2,1,0:T(8,128)(2,1)}), bf16[8,256,128]{2,1,0:T(8,128)(2,1)S(1)}, u32[]{:S(2)}, u32[]{:S(2)}) async-start(bf16[8,256,128]{2,1,0:T(8,128)(2,1)} %bitcast.7), calls=%async_computation.1 | async-start | bytes 1048576 | tf_op jit(solution)/shard_map/all_to_all | solution.py:296
  45.3 3.8 %collective-permute-start.3 = (bf16[2,128,1024]{2,1,0:T(8,128)(2,1)S(1)}, bf16[2,128,1024]{2,1,0:T(8,128)(2,1)S(1)}, u32[]{:S(2)}, u32[]{:S(2)}) collective-permute-start(bf16[2,128,1024]{2,1,0:T(8,128)(2,1)S(1)} %copy-done.3), channel_id=1, source_target_pairs={{0,8},{8,0},{1,9},{9,1},{2,10},{10,2},{3,11},{11,3},{4,12},{12,4},... | collective-permute-start | bytes 1572872 | tf_op jit(solution)/shard_map/ppermute | solution.py:297
  49.1 12.6 %copy-start = (f32[128,1024]{1,0:T(8,128)S(1)}, f32[128,1024]{1,0:T(8,128)}, u32[]{:S(2)}) copy-start(f32[128,1024]{1,0:T(8,128)} %get-tuple-element.16.own_ref) | copy-start | bytes 1572868
  49.1 12.5 %collective-permute-start.4 = (bf16[128,1024]{1,0:T(8,128)(2,1)S(1)}, bf16[128,1024]{1,0:T(8,128)(2,1)S(1)}, u32[]{:S(2)}, u32[]{:S(2)}) collective-permute-start(bf16[128,1024]{1,0:T(8,128)(2,1)S(1)} %pass_on.1), channel_id=1, source_target_pairs={{0,48},{8,56},{16,32},{24,40},{32,16},{40,24},{48,0},{56,8},{1,49}... | collective-permute-start | bytes 786440 | tf_op jit(solution)/shard_map/ppermute | solution.py:299

commit v9 on v8

--- a/solution.py
+++ b/solution.py
@@ -20,7 +20,7 @@
 SCALE = 1.0 / math.sqrt(HEAD)
 LOG2E = math.log2(math.e)
 CTX = ("yh", "xh", "xl", "core")
-KEEPERS = ("yh", "xl")
+KEEPERS = ("yh", "xh")
 NEXT = ("xh", "xl", "core")
 NT = (((1,), (1,)), ((), ()))
 TN = (((0,), (0,)), ((), ()))
@@ -210,8 +210,8 @@
     upto = jnp.arange(docs)[:, None] >= jnp.arange(docs)[None, :]
     ends = jnp.sum(jnp.where(upto, doc_lengths[None, :], 0), axis=1)
     blocks = jnp.arange(nblk, dtype=jnp.int32)
-    held_here = ((blocks // 2) % 2 == core) & ((blocks // 8) % 2 == xh)
-    place = ((blocks // 16) * 2 + (blocks // 4) % 2) * (2 * ROWS) + (blocks % 2) * BLOCK
+    held_here = ((blocks // 2) % 2 == core) & ((blocks // 4) % 2 == xl)
+    place = (blocks // 8) * (2 * ROWS) + (blocks % 2) * BLOCK
     before = held_here[None, :] & (block_order[None, :] < block_order[:, None])
     rank = jnp.sum(before.astype(jnp.int32), axis=1)
     slots = jnp.arange(nheld + 8, dtype=jnp.int32)
@@ -219,10 +219,14 @@
     held = jnp.sum(jnp.where(hit, block_order[None, :], 0), axis=1)
     held = jnp.where(slots < nheld, held, nblk)
     place = jnp.sum(jnp.where(hit, place[None, :], 0), axis=1)
-    x = 2 * xh + xl
-    partner = (x + 2 * xl - 1) % 4
+    x, turn = 2 * xh + xl, 1 - 2 * core
     owners = 8 * yh + jnp.stack(
-        [2 * x + core, 2 * x + 1 - core, 2 * partner + core, 2 * partner + 1 - core]
+        [
+            2 * x + core,
+            2 * x + 1 - core,
+            2 * ((x + turn) % 4) + core,
+            2 * ((x - turn) % 4) + 1 - core,
+        ]
     )
     stored = (2 * owners[:, None] + jnp.arange(2)[None, :]).reshape(8)
     mine = jnp.sum(jnp.where(stored[:, None] == blocks[None, :], block_order[None, :], 0), axis=1)
@@ -250,8 +254,9 @@
     dma = pltpu.SemaphoreType.DMA
 
     swap = [(0, 1), (1, 0)]
-    partner = [3, 2, 1, 0]
-    facing = [(2 * i + c, 2 * partner[i] + c) for i in range(4) for c in range(2)]
+    there = [(2 * ((i + 1) % 4), 2 * i) for i in range(4)]
+    there += [(2 * i + 1, 2 * ((i + 1) % 4) + 1) for i in range(4)]
+    back = [(j, i) for i, j in there]
     sent, p0 = call(
         pack,
         (pltpu.HBM((PEERS, 2 * ROWS, HEAD), bf16), shape((2 * ROWS + EXTRA, WIDTH), bf16)),
@@ -267,7 +272,7 @@
         ],
     )
     kv = lax.all_to_all(sent, KEEPERS, 0, 0, tiled=True)
-    p2 = lax.ppermute(p0, NEXT, facing)
+    p2 = lax.ppermute(p0, NEXT, there)
     p3 = lax.ppermute(p2, "core", swap)
     work, held, at, first, own = plan(doc_lengths, block_order, *place)
     later, held = lax.optimization_barrier((p0, held))
@@ -296,7 +301,7 @@
     got = lax.all_to_all(dkv.reshape(PEERS, 2 * ROWS, HEAD), KEEPERS, 0, 0, tiled=True)
     side = lax.ppermute(side, "core", swap)
     far = call(pass_on, shape((ROWS, WIDTH), bf16), [VMEM] * 2, VMEM, dq2, side)
-    far = lax.ppermute(far, NEXT, facing)
+    far = lax.ppermute(far, NEXT, back)
     grad_q, grad_k, grad_v = call(
         finish,
         (shape((ROWS, WIDTH), bf16),) + (shape((ROWS, HEAD), bf16),) * 2,

time: 63.3 us -> 65.8 us (1.039)
  starting transfers between devices: 35.5 us -> 39.2 us
  waiting for transfers between devices: 12.9 us -> 12 us
  Pallas kernels: 8.83 us -> 8.12 us
    ppermute x2, starting transfers between devices: 10.6 us -> 6.25 us  [the longest x1 4.04 us: on_device(): far = lax.ppermute(far, NEXT, back)]
    all_to_all x1, starting transfers between devices: 6.42 us -> 9.7 us  [on_device(): lax.all_to_all(dkv.reshape(PEERS, 2 * ROWS, HEAD), KEEPERS, 0, 0, tiled=T...]
    ppermute x2, waiting for transfers between devices: 9.7 us -> 6.67 us  [the longest x1 4.49 us: on_device(): far = lax.ppermute(far, NEXT, back)]
    all_to_all x1, waiting for transfers between devices: 0.01 us -> 2.51 us  [on_device(): lax.all_to_all(dkv.reshape(PEERS, 2 * ROWS, HEAD), KEEPERS, 0, 0, tiled=T...]
    ppermute x1, starting transfers between devices: 3.42 us -> 5.81 us  [on_device(): p1 = lax.ppermute(later, 'core', swap)]
    ppermute x1, starting transfers between devices: 1.92 us -> 3.98 us  [on_device(): side = lax.ppermute(side, 'core', swap)]
    all_to_all x1, starting transfers between devices: 8.59 us -> 10.1 us  [on_device(): kv = lax.all_to_all(sent, KEEPERS, 0, 0, tiled=True)]
    ppermute x1, starting transfers between devices: 4.57 us -> 3.31 us  [on_device(): p3 = lax.ppermute(p2, 'core', swap)]
  transfers between devices with their start and end apart: 7 -> 7, of which waited for: 4 -> 5; matrix products, arithmetic and copies ran while one was open for 4% -> 4% of each run, Pallas kernels for 0% -> 0%
where the time goes in v9:
time: 65.8 us; the launch traced here: 64.6 us
  starting transfers between devices  39.2 us (60%)
  waiting for transfers between devices  12 us (18%)
  Pallas kernels  8.12 us (12%)
  local copies, waits for them, and re-layouts  2.13 us (3%)
  other arithmetic  1.66 us (3%)
  between operations  1.5 us (2%)
    all_to_all x1, starting transfers between devices, on_device(): kv = lax.all_to_all(sent, KEEPERS, 0, 0, tiled=True)  10.1 us
    all_to_all x1, starting transfers between devices, on_device(): lax.all_to_all(dkv.reshape(PEERS, 2 * ROWS, HEAD), KEEPERS, 0, 0, tiled=T...  9.7 us
    pallas_call x4, Pallas kernels, call(): pl.pallas_call(kernel, out_shape=out, in_specs=ins, out_specs=outs, scrat...  8.12 us
    ppermute x1, starting transfers between devices, on_device(): p1 = lax.ppermute(later, 'core', swap)  5.81 us
    ppermute x1, waiting for transfers between devices, on_device(): far = lax.ppermute(far, NEXT, back)  4.49 us
    ppermute x1, starting transfers between devices, on_device(): far = lax.ppermute(far, NEXT, back)  4.04 us
    ppermute x1, starting transfers between devices, on_device(): side = lax.ppermute(side, 'core', swap)  3.98 us
    ppermute x1, starting transfers between devices, on_device(): p3 = lax.ppermute(p2, 'core', swap)  3.31 us
  transfers between devices with their start and end apart: 7, of which 5 were waited for; matrix products, arithmetic and copies ran while one was open for 4% of the time, Pallas kernels for 0%

profile of v9, /device:TPU:1, one launch (start us, length us, event | category | flops | bytes accessed | tf_op | source)
XLA Modules:
  0.0 64.6 jit_solution(13739823758668867611)
XLA Ops:
  0.6 1.8 %pack.1 = (bf16[8,256,128]{2,1,0:T(8,128)(2,1)}, bf16[272,1024]{1,0:T(8,128)(2,1)S(1)}) custom-call(bf16[128,128]{1,0:T(8,128)(2,1)} %k_ref.1, bf16[128,128]{1,0:T(8,128)(2,1)} %v_ref.1, bf16[128,1024]{1,0:T(8,128)(2,1)} %q_ref.1, bf16[128,1024]{1,0:T(8,128)(2,1)} %do_ref.1, bf16[128,1024]{1,0:T(8,128)(2,1)} %o_ref.1, f32[8,128]{1,0:T(8,128)} %norm_ref.1), custom_call_target="tpu_custom_call" | custom-call | tf_op jit(solution)/shard_map/pack/pallas_call | solution.py:41
  2.4 10.1 %all-to-all-start = ((bf16[8,256,128]{2,1,0:T(8,128)(2,1)}), bf16[8,256,128]{2,1,0:T(8,128)(2,1)S(1)}, u32[]{:S(2)}, u32[]{:S(2)}) async-start(bf16[8,256,128]{2,1,0:T(8,128)(2,1)} %get-tuple-element.14), calls=%async_computation | async-start | bytes 1048576 | tf_op jit(solution)/shard_map/all_to_all | solution.py:274
  12.5 2.2 %collective-permute-start.1 = (bf16[272,1024]{1,0:T(8,128)(2,1)S(1)}, bf16[272,1024]{1,0:T(8,128)(2,1)S(1)}, u32[]{:S(2)}, u32[]{:S(2)}) collective-permute-start(bf16[272,1024]{1,0:T(8,128)(2,1)S(1)} %get-tuple-element.13.p0_ref), channel_id=1, source_target_pairs={{16,0},{32,16},{48,32},{0,48},{8,24},{24,40},{40,56},{56,8},{17,1}... | collective-permute-start | bytes 1671176 | tf_op jit(solution)/shard_map/ppermute | solution.py:275
  14.8 0.0 copy-start.2
  14.8 0.6 copy-done.2
  15.4 0.2 convert_reduce_fusion
  15.6 0.1 select_reduce_fusion.1
  15.7 5.8 %collective-permute-start = (bf16[272,1024]{1,0:T(8,128)(2,1)S(1)}, bf16[272,1024]{1,0:T(8,128)(2,1)S(1)}, u32[]{:S(2)}, u32[]{:S(2)}) collective-permute-start(bf16[272,1024]{1,0:T(8,128)(2,1)S(1)} %get-tuple-element.13.p0_ref), channel_id=1, source_target_pairs={{0,8},{8,0},{1,9},{9,1},{2,10},{10,2},{3,11},{11,3},{4,12},{12,4},... | collective-permute-start | bytes 1671176 | tf_op jit(solution)/shard_map/ppermute | solution.py:279
  21.6 0.0 copy-start.4
  21.6 0.6 %copy-done.4 = s32[16]{0:T(128)S(1)} copy-done((s32[16]{0:T(128)S(1)}, s32[16]{0:T(128)}, u32[]{:S(2)}) %copy-start.4) | copy-done | bytes 88
  22.3 0.1 select_reduce_fusion.3
  22.4 0.1 fusion.7
  22.4 0.1 iota_add_fusion.1
  22.5 0.1 add.153
  22.6 0.2 select_reduce_fusion.6
  22.8 0.1 iota_add_fusion
  22.9 0.1 select_reduce_fusion
  23.0 0.1 shift-right-arithmetic_reduce_fusion
  23.1 0.2 convert_reduce_fusion.2
  23.3 0.1 select_reduce_fusion.5
  23.4 0.6 slice.7
  24.7 0.1 tile.9.first_ref
  24.8 0.1 tile.21.own_ref
  24.9 2.2 %collective-permute-done.1.p2_ref = bf16[272,1024]{1,0:T(8,128)(2,1)S(1)} collective-permute-done((bf16[272,1024]{1,0:T(8,128)(2,1)S(1)}, bf16[272,1024]{1,0:T(8,128)(2,1)S(1)}, u32[]{:S(2)}, u32[]{:S(2)}) %collective-permute-start.1) | collective-permute-done | bytes 557088 | tf_op jit(solution)/shard_map/ppermute | solution.py:275
  27.0 3.3 %collective-permute-start.2 = (bf16[272,1024]{1,0:T(8,128)(2,1)S(1)}, bf16[272,1024]{1,0:T(8,128)(2,1)S(1)}, u32[]{:S(2)}, u32[]{:S(2)}) collective-permute-start(bf16[272,1024]{1,0:T(8,128)(2,1)S(1)} %collective-permute-done.1.p2_ref), channel_id=1, source_target_pairs={{0,8},{8,0},{1,9},{9,1},{2,10},{10,2},{3,11},{11,3},{4,12},{12,4},... | collective-permute-start | bytes 1671176 | tf_op jit(solution)/shard_map/ppermute | solution.py:276
  30.4 0.1 convert_reduce_fusion.1
  30.4 0.1 select_reduce_fusion.4
  30.5 0.1 pad_add_fusion.work_ref
  30.6 0.0 collective-permute-done.p1_ref
  30.6 0.0 all-to-all-done
  30.6 1.3 %collective-permute-done.2.p3_ref = bf16[272,1024]{1,0:T(8,128)(2,1)S(1)} collective-permute-done((bf16[272,1024]{1,0:T(8,128)(2,1)S(1)}, bf16[272,1024]{1,0:T(8,128)(2,1)S(1)}, u32[]{:S(2)}, u32[]{:S(2)}) %collective-permute-start.2) | collective-permute-done | bytes 557088 | tf_op jit(solution)/shard_map/ppermute | solution.py:276
  31.9 5.5 %terms.1 = (f32[128,1024]{1,0:T(8,128)}, f32[128,1024]{1,0:T(8,128)}, bf16[2,128,1024]{2,1,0:T(8,128)(2,1)}, bf16[2048,128]{1,0:T(8,128)(2,1)}) custom-call(s32[145]{0:T(256)S(1)} %pad_add_fusion.work_ref, s32[24]{0:T(128)S(1)} %compare_select_fusion.5.held_ref, s32[24]{0:T(128)S(1)} %get-tuple-element.19.place_ref, s32[8,512]{1,0:T(8,128)S(1)} %tile.9.first_ref, ...), custom_call_target="tpu_custom_call" | custom-call | tf_op jit(solution)/shard_map/terms/pallas_call | solution.py:41
  37.4 0.0 copy-start.3
  37.4 0.0 copy-start.1
  37.4 9.7 %all-to-all-start.1 = ((bf16[8,256,128]{2,1,0:T(8,128)(2,1)}), bf16[8,256,128]{2,1,0:T(8,128)(2,1)S(1)}, u32[]{:S(2)}, u32[]{:S(2)}) async-start(bf16[8,256,128]{2,1,0:T(8,128)(2,1)} %bitcast.7), calls=%async_computation.1 | async-start | bytes 1048576 | tf_op jit(solution)/shard_map/all_to_all | solution.py:301
  47.1 0.0 copy-done.3
  47.1 4.0 %collective-permute-start.3 = (bf16[2,128,1024]{2,1,0:T(8,128)(2,1)S(1)}, bf16[2,128,1024]{2,1,0:T(8,128)(2,1)S(1)}, u32[]{:S(2)}, u32[]{:S(2)}) collective-permute-start(bf16[2,128,1024]{2,1,0:T(8,128)(2,1)S(1)} %copy-done.3), channel_id=1, source_target_pairs={{0,8},{8,0},{1,9},{9,1},{2,10},{10,2},{3,11},{11,3},{4,12},{12,4},... | collective-permute-start | bytes 1572872 | tf_op jit(solution)/shard_map/ppermute | solution.py:302
  51.1 1.5 %collective-permute-done.3.side_ref = bf16[2,128,1024]{2,1,0:T(8,128)(2,1)S(1)} collective-permute-done((bf16[2,128,1024]{2,1,0:T(8,128)(2,1)S(1)}, bf16[2,128,1024]{2,1,0:T(8,128)(2,1)S(1)}, u32[]{:S(2)}, u32[]{:S(2)}) %collective-permute-start.3) | collective-permute-done | bytes 524320 | tf_op jit(solution)/shard_map/ppermute | solution.py:302
  52.6 0.0 copy-done.1
  52.6 0.0 copy-start
  52.7 4.0 %collective-permute-start.4 = (bf16[128,1024]{1,0:T(8,128)(2,1)S(1)}, bf16[128,1024]{1,0:T(8,128)(2,1)S(1)}, u32[]{:S(2)}, u32[]{:S(2)}) collective-permute-start(bf16[128,1024]{1,0:T(8,128)(2,1)S(1)} %pass_on.1), channel_id=1, source_target_pairs={{0,16},{16,32},{32,48},{48,0},{24,8},{40,24},{56,40},{8,56},{1,17}... | collective-permute-start | bytes 786440 | tf_op jit(solution)/shard_map/ppermute | solution.py:304
  56.7 4.5 %collective-permute-done.4.far_ref = bf16[128,1024]{1,0:T(8,128)(2,1)S(1)} collective-permute-done((bf16[128,1024]{1,0:T(8,128)(2,1)S(1)}, bf16[128,1024]{1,0:T(8,128)(2,1)S(1)}, u32[]{:S(2)}, u32[]{:S(2)}) %collective-permute-start.4) | collective-permute-done | bytes 262176 | tf_op jit(solution)/shard_map/ppermute | solution.py:304
  61.2 2.5 %all-to-all-done.1.got_ref = bf16[8,256,128]{2,1,0:T(8,128)(2,1)S(1)} async-done(((bf16[8,256,128]{2,1,0:T(8,128)(2,1)}), bf16[8,256,128]{2,1,0:T(8,128)(2,1)S(1)}, u32[]{:S(2)}, u32[]{:S(2)}) %all-to-all-start.1) | async-done | bytes 524320 | tf_op jit(solution)/shard_map/all_to_all | solution.py:301
  63.7 0.0 copy-done
  63.7 0.8 %finish.1 = (bf16[128,1024]{1,0:T(8,128)(2,1)}, bf16[128,128]{1,0:T(8,128)(2,1)}, bf16[128,128]{1,0:T(8,128)(2,1)}) custom-call(bf16[8,256,128]{2,1,0:T(8,128)(2,1)S(1)} %all-to-all-done.1.got_ref, f32[128,1024]{1,0:T(8,128)S(1)} %copy-done, bf16[2,128,1024]{2,1,0:T(8,128)(2,1)S(1)} %collective-permute-done.3.side_ref, ...), custom_call_target="tpu_custom_call" | custom-call | tf_op jit(solution)/shard_map/finish/pallas_call | solution.py:41
  (10 shorter events, 0.1 us)
Async XLA Ops:
  2.4 28.2 %all-to-all-start = ((bf16[8,256,128]{2,1,0:T(8,128)(2,1)}), bf16[8,256,128]{2,1,0:T(8,128)(2,1)S(1)}, u32[]{:S(2)}, u32[]{:S(2)}) async-start(bf16[8,256,128]{2,1,0:T(8,128)(2,1)} %get-tuple-element.14), calls=%async_computation | async-start | bytes 1048576 | tf_op jit(solution)/shard_map/all_to_all | solution.py:274
  12.5 14.5 %collective-permute-start.1 = (bf16[272,1024]{1,0:T(8,128)(2,1)S(1)}, bf16[272,1024]{1,0:T(8,128)(2,1)S(1)}, u32[]{:S(2)}, u32[]{:S(2)}) collective-permute-start(bf16[272,1024]{1,0:T(8,128)(2,1)S(1)} %get-tuple-element.13.p0_ref), channel_id=1, source_target_pairs={{16,0},{32,16},{48,32},{0,48},{8,24},{24,40},{40,56},{56,8},{17,1}... | collective-permute-start | bytes 1671176 | tf_op jit(solution)/shard_map/ppermute | solution.py:275
  14.8 0.7 %copy-start.2 = (s32[64]{0:T(128)S(1)}, s32[64]{0:T(128)}, u32[]{:S(2)}) copy-start(s32[64]{0:T(128)} %param.15) | copy-start | bytes 772
  15.7 14.9 %collective-permute-start = (bf16[272,1024]{1,0:T(8,128)(2,1)S(1)}, bf16[272,1024]{1,0:T(8,128)(2,1)S(1)}, u32[]{:S(2)}, u32[]{:S(2)}) collective-permute-start(bf16[272,1024]{1,0:T(8,128)(2,1)S(1)} %get-tuple-element.13.p0_ref), channel_id=1, source_target_pairs={{0,8},{8,0},{1,9},{9,1},{2,10},{10,2},{3,11},{11,3},{4,12},{12,4},... | collective-permute-start | bytes 1671176 | tf_op jit(solution)/shard_map/ppermute | solution.py:279
  21.6 0.7 %copy-start.4 = (s32[16]{0:T(128)S(1)}, s32[16]{0:T(128)}, u32[]{:S(2)}) copy-start(s32[16]{0:T(128)} %param.14) | copy-start | bytes 196
  27.0 4.9 %collective-permute-start.2 = (bf16[272,1024]{1,0:T(8,128)(2,1)S(1)}, bf16[272,1024]{1,0:T(8,128)(2,1)S(1)}, u32[]{:S(2)}, u32[]{:S(2)}) collective-permute-start(bf16[272,1024]{1,0:T(8,128)(2,1)S(1)} %collective-permute-done.1.p2_ref), channel_id=1, source_target_pairs={{0,8},{8,0},{1,9},{9,1},{2,10},{10,2},{3,11},{11,3},{4,12},{12,4},... | collective-permute-start | bytes 1671176 | tf_op jit(solution)/shard_map/ppermute | solution.py:276
  37.4 9.7 %copy-start.3 = (bf16[2,128,1024]{2,1,0:T(8,128)(2,1)S(1)}, bf16[2,128,1024]{2,1,0:T(8,128)(2,1)}, u32[]{:S(2)}) copy-start(bf16[2,128,1024]{2,1,0:T(8,128)(2,1)} %get-tuple-element.17) | copy-start | bytes 1572868
  37.4 15.2 %copy-start.1 = (f32[128,1024]{1,0:T(8,128)S(1)}, f32[128,1024]{1,0:T(8,128)}, u32[]{:S(2)}) copy-start(f32[128,1024]{1,0:T(8,128)} %get-tuple-element.18.dq_ref) | copy-start | bytes 1572868
  37.4 26.3 %all-to-all-start.1 = ((bf16[8,256,128]{2,1,0:T(8,128)(2,1)}), bf16[8,256,128]{2,1,0:T(8,128)(2,1)S(1)}, u32[]{:S(2)}, u32[]{:S(2)}) async-start(bf16[8,256,128]{2,1,0:T(8,128)(2,1)} %bitcast.7), calls=%async_computation.1 | async-start | bytes 1048576 | tf_op jit(solution)/shard_map/all_to_all | solution.py:301
  47.1 5.5 %collective-permute-start.3 = (bf16[2,128,1024]{2,1,0:T(8,128)(2,1)S(1)}, bf16[2,128,1024]{2,1,0:T(8,128)(2,1)S(1)}, u32[]{:S(2)}, u32[]{:S(2)}) collective-permute-start(bf16[2,128,1024]{2,1,0:T(8,128)(2,1)S(1)} %copy-done.3), channel_id=1, source_target_pairs={{0,8},{8,0},{1,9},{9,1},{2,10},{10,2},{3,11},{11,3},{4,12},{12,4},... | collective-permute-start | bytes 1572872 | tf_op jit(solution)/shard_map/ppermute | solution.py:302
  52.6 11.1 %copy-start = (f32[128,1024]{1,0:T(8,128)S(1)}, f32[128,1024]{1,0:T(8,128)}, u32[]{:S(2)}) copy-start(f32[128,1024]{1,0:T(8,128)} %get-tuple-element.16.own_ref) | copy-start | bytes 1572868
  52.7 8.5 %collective-permute-start.4 = (bf16[128,1024]{1,0:T(8,128)(2,1)S(1)}, bf16[128,1024]{1,0:T(8,128)(2,1)S(1)}, u32[]{:S(2)}, u32[]{:S(2)}) collective-permute-start(bf16[128,1024]{1,0:T(8,128)(2,1)S(1)} %pass_on.1), channel_id=1, source_target_pairs={{0,16},{16,32},{32,48},{48,0},{24,8},{40,24},{56,40},{8,56},{1,17}... | collective-permute-start | bytes 786440 | tf_op jit(solution)/shard_map/ppermute | solution.py:304

commit v10 on v8

--- a/solution.py
+++ b/solution.py
@@ -79,7 +79,7 @@
         copy.start()
     for copy in reads[2:5]:
         copy.wait()
-    ones = jnp.ones((8, HEAD), jnp.float32)
+    ones = jnp.ones((8, HEAD), jnp.bfloat16)
     dots = []
     for b in range(2):
         at = slice(b * BLOCK, (b + 1) * BLOCK)
@@ -91,10 +91,11 @@
             ],
             0,
         )
+        high = prod.astype(jnp.bfloat16)
+        low = (prod - high.astype(jnp.float32)).astype(jnp.bfloat16)
         dots.append(
-            lax.dot_general(
-                ones, prod, NT, precision=lax.Precision.HIGHEST, preferred_element_type=jnp.float32
-            )[:1]
+            lax.dot_general(ones, high, NT, preferred_element_type=jnp.float32)[:1]
+            + lax.dot_general(ones, low, NT, preferred_element_type=jnp.float32)[:1]
         )
     norms = terms_of(norm_buf[...])
     norms = jnp.concatenate(norms + [jnp.zeros((8, WIDTH - 3 * HEAD), jnp.float32)], 1)
@@ -130,7 +131,7 @@
 def terms(
     work_ref, held_ref, place_ref, first_ref, own_ref, p0_ref, p1_ref, p2_ref, p3_ref, kv_ref,
     dq0_ref, dq2_ref, side_ref, dkv_ref,
-    acc_ref, half_ref, dqt_ref, keep_buf, side_buf, q_ref, do_ref, norm_ref, dot_ref, sem,
+    acc_ref, half_ref, dqt_ref, own_buf, dq2_buf, q_ref, do_ref, norm_ref, dot_ref, sem,
 ):
     acc_ref[...] = jnp.zeros_like(acc_ref)
     dqt_ref[...] = jnp.zeros_like(dqt_ref)
@@ -175,16 +176,18 @@
         half_ref[at, :] = acc_ref[at, :].astype(jnp.bfloat16)
         copies.append(pltpu.make_async_copy(half_ref.at[at], dkv_ref.at[at], sem.at[i]))
         copies[-1].start()
-    for g in (1, 3, 2, 0):
-        buf, to = (side_buf, side_ref) if g % 2 else (keep_buf, (dq0_ref, dq2_ref)[g // 2])
+    outs = (own_buf, side_ref.at[0], dq2_buf, side_ref.at[1])
+    for g in (0, 2, 1, 3):
+        out = outs[g]
         for i in range(2):
             b = 2 * g + i
-            dq = dqt_ref[b * HEAD : (b + 1) * HEAD, :].T.astype(buf.dtype)
+            dq = dqt_ref[b * HEAD : (b + 1) * HEAD, :].T.astype(out.dtype)
             for h in range(HEADS):
-                buf[g // 2, i * BLOCK : (i + 1) * BLOCK, head(h)] = dq[h * BLOCK : (h + 1) * BLOCK]
-        to = to.at[g // 2] if g % 2 else to
-        copies.append(pltpu.make_async_copy(buf.at[g // 2], to, sem.at[4 + g]))
-        copies[-1].start()
+                out[i * BLOCK : (i + 1) * BLOCK, head(h)] = dq[h * BLOCK : (h + 1) * BLOCK]
+        if g % 2 == 0:
+            to = dq2_ref if g else dq0_ref
+            copies.append(pltpu.make_async_copy(out, to, sem.at[4 + g]))
+            copies[-1].start()
     for copy in copies:
         copy.wait()
 
@@ -276,16 +279,16 @@
     dq0, dq2, side, dkv = call(
         terms,
         (pltpu.HBM((ROWS, WIDTH), f32),) * 2
-        + (pltpu.HBM((2, ROWS, WIDTH), bf16), pltpu.HBM((nkeys, HEAD), bf16)),
+        + (shape((2, ROWS, WIDTH), bf16), pltpu.HBM((nkeys, HEAD), bf16)),
         [SMEM] * 3 + [VMEM] * 7,
-        (HBM,) * 4,
+        (HBM, HBM, VMEM, HBM),
         work, held, at, first, own, p0, p1, p2, p3, kv.reshape(nkeys, HEAD),
         scratch=[
             pltpu.VMEM((nkeys, HEAD), f32),
             pltpu.VMEM((nkeys, HEAD), bf16),
             pltpu.VMEM((8 * HEAD, LANES), f32),
-            pltpu.VMEM((2, ROWS, WIDTH), f32),
-            pltpu.VMEM((2, ROWS, WIDTH), bf16),
+            pltpu.VMEM((ROWS, WIDTH), f32),
+            pltpu.VMEM((ROWS, WIDTH), f32),
             pltpu.VMEM((8 * LANES, HEAD), bf16),
             pltpu.VMEM((8 * LANES, HEAD), bf16),
             pltpu.VMEM((8, LANES), f32),

time: 63.3 us -> 63.3 us (level)
  Pallas kernels: 8.83 us -> 9.65 us
  starting transfers between devices: 35.5 us -> 34.8 us
    ppermute x1, starting transfers between devices: 5.96 us -> 4.96 us  [on_device(): far = lax.ppermute(far, NEXT, facing)]
    pallas_call x4, Pallas kernels: 8.83 us -> 9.65 us  [call(): pl.pallas_call(kernel, out_shape=out, in_specs=ins, out_specs=outs, scrat...]
    unnamed x10 -> x8, local copies, waits for them, and re-layouts: 1.3 us -> 1.29 us
  transfers between devices with their start and end apart: 7 -> 7, of which waited for: 4 -> 5; matrix products, arithmetic and copies ran while one was open for 4% -> 4% of each run, Pallas kernels for 0% -> 0%
where the time goes in v10:
time: 63.3 us; the launch traced here: 62.9 us
  starting transfers between devices  34.8 us (55%)
  waiting for transfers between devices  13.2 us (21%)
  Pallas kernels  9.65 us (15%)
  local copies, waits for them, and re-layouts  2.13 us (3%)
  other arithmetic  1.66 us (3%)
  between operations  1.47 us (2%)
    pallas_call x4, Pallas kernels, call(): pl.pallas_call(kernel, out_shape=out, in_specs=ins, out_specs=outs, scrat...  9.65 us
    all_to_all x1, starting transfers between devices, on_device(): kv = lax.all_to_all(sent, KEEPERS, 0, 0, tiled=True)  8.59 us
    all_to_all x1, starting transfers between devices, on_device(): lax.all_to_all(dkv.reshape(PEERS, 2 * ROWS, HEAD), KEEPERS, 0, 0, tiled=T...  6.73 us
    ppermute x1, waiting for transfers between devices, on_device(): far = lax.ppermute(far, NEXT, facing)  6.53 us
    ppermute x1, starting transfers between devices, on_device(): far = lax.ppermute(far, NEXT, facing)  4.96 us
    ppermute x1, starting transfers between devices, on_device(): p2 = lax.ppermute(p0, NEXT, facing)  4.62 us
    ppermute x1, starting transfers between devices, on_device(): p3 = lax.ppermute(p2, 'core', swap)  4.57 us
    ppermute x1, starting transfers between devices, on_device(): p1 = lax.ppermute(later, 'core', swap)  3.42 us
  transfers between devices with their start and end apart: 7, of which 5 were waited for; matrix products, arithmetic and copies ran while one was open for 4% of the time, Pallas kernels for 0%

profile of v10, /device:TPU:1, one launch (start us, length us, event | category | flops | bytes accessed | tf_op | source)
XLA Modules:
  0.0 62.9 jit_solution(1621614796012531156)
XLA Ops:
  0.6 1.7 %pack.1 = (bf16[8,256,128]{2,1,0:T(8,128)(2,1)}, bf16[272,1024]{1,0:T(8,128)(2,1)S(1)}) custom-call(bf16[128,128]{1,0:T(8,128)(2,1)} %k_ref.1, bf16[128,128]{1,0:T(8,128)(2,1)} %v_ref.1, bf16[128,1024]{1,0:T(8,128)(2,1)} %q_ref.1, bf16[128,1024]{1,0:T(8,128)(2,1)} %do_ref.1, bf16[128,1024]{1,0:T(8,128)(2,1)} %o_ref.1, f32[8,128]{1,0:T(8,128)} %norm_ref.1), custom_call_target="tpu_custom_call" | custom-call | tf_op jit(solution)/shard_map/pack/pallas_call | solution.py:41
  2.3 8.6 %all-to-all-start = ((bf16[8,256,128]{2,1,0:T(8,128)(2,1)}), bf16[8,256,128]{2,1,0:T(8,128)(2,1)S(1)}, u32[]{:S(2)}, u32[]{:S(2)}) async-start(bf16[8,256,128]{2,1,0:T(8,128)(2,1)} %get-tuple-element.14), calls=%async_computation | async-start | bytes 1048576 | tf_op jit(solution)/shard_map/all_to_all | solution.py:272
  10.9 4.6 %collective-permute-start.1 = (bf16[272,1024]{1,0:T(8,128)(2,1)S(1)}, bf16[272,1024]{1,0:T(8,128)(2,1)S(1)}, u32[]{:S(2)}, u32[]{:S(2)}) collective-permute-start(bf16[272,1024]{1,0:T(8,128)(2,1)S(1)} %get-tuple-element.13.p0_ref), channel_id=1, source_target_pairs={{0,48},{8,56},{16,32},{24,40},{32,16},{40,24},{48,0},{56,8},{1,49}... | collective-permute-start | bytes 1671176 | tf_op jit(solution)/shard_map/ppermute | solution.py:273
  15.6 0.0 copy-start.2
  15.6 0.6 %copy-done.2 = s32[64]{0:T(128)S(1)} copy-done((s32[64]{0:T(128)S(1)}, s32[64]{0:T(128)}, u32[]{:S(2)}) %copy-start.2) | copy-done | bytes 280
  16.2 0.2 convert_reduce_fusion
  16.4 0.1 select_reduce_fusion.1
  16.5 3.4 %collective-permute-start = (bf16[272,1024]{1,0:T(8,128)(2,1)S(1)}, bf16[272,1024]{1,0:T(8,128)(2,1)S(1)}, u32[]{:S(2)}, u32[]{:S(2)}) collective-permute-start(bf16[272,1024]{1,0:T(8,128)(2,1)S(1)} %get-tuple-element.13.p0_ref), channel_id=1, source_target_pairs={{0,8},{8,0},{1,9},{9,1},{2,10},{10,2},{3,11},{11,3},{4,12},{12,4},... | collective-permute-start | bytes 1671176 | tf_op jit(solution)/shard_map/ppermute | solution.py:277
  20.0 0.0 copy-start.3
  20.0 0.6 %copy-done.3 = s32[16]{0:T(128)S(1)} copy-done((s32[16]{0:T(128)S(1)}, s32[16]{0:T(128)}, u32[]{:S(2)}) %copy-start.3) | copy-done | bytes 88
  20.7 0.1 select_reduce_fusion.3
  20.8 0.1 fusion.10
  20.9 0.1 iota_add_fusion.1
  20.9 0.1 add.170
  21.0 0.2 select_reduce_fusion.6
  21.2 0.1 iota_add_fusion
  21.3 0.1 select_reduce_fusion
  21.4 0.1 shift-right-arithmetic_reduce_fusion
  21.5 0.2 convert_reduce_fusion.2
  21.7 0.1 select_reduce_fusion.5
  21.8 0.6 slice.7
  23.1 0.1 tile.9.first_ref
  23.2 0.1 tile.21.own_ref
  23.3 3.2 %collective-permute-done.1.p2_ref = bf16[272,1024]{1,0:T(8,128)(2,1)S(1)} collective-permute-done((bf16[272,1024]{1,0:T(8,128)(2,1)S(1)}, bf16[272,1024]{1,0:T(8,128)(2,1)S(1)}, u32[]{:S(2)}, u32[]{:S(2)}) %collective-permute-start.1) | collective-permute-done | bytes 557088 | tf_op jit(solution)/shard_map/ppermute | solution.py:273
  26.4 4.6 %collective-permute-start.2 = (bf16[272,1024]{1,0:T(8,128)(2,1)S(1)}, bf16[272,1024]{1,0:T(8,128)(2,1)S(1)}, u32[]{:S(2)}, u32[]{:S(2)}) collective-permute-start(bf16[272,1024]{1,0:T(8,128)(2,1)S(1)} %collective-permute-done.1.p2_ref), channel_id=1, source_target_pairs={{0,8},{8,0},{1,9},{9,1},{2,10},{10,2},{3,11},{11,3},{4,12},{12,4},... | collective-permute-start | bytes 1671176 | tf_op jit(solution)/shard_map/ppermute | solution.py:274
  31.0 0.1 convert_reduce_fusion.1
  31.1 0.1 select_reduce_fusion.4
  31.2 0.1 pad_add_fusion.work_ref
  31.3 0.0 collective-permute-done.p1_ref
  31.3 0.0 all-to-all-done
  31.3 1.3 %collective-permute-done.2.p3_ref = bf16[272,1024]{1,0:T(8,128)(2,1)S(1)} collective-permute-done((bf16[272,1024]{1,0:T(8,128)(2,1)S(1)}, bf16[272,1024]{1,0:T(8,128)(2,1)S(1)}, u32[]{:S(2)}, u32[]{:S(2)}) %collective-permute-start.2) | collective-permute-done | bytes 557088 | tf_op jit(solution)/shard_map/ppermute | solution.py:274
  32.6 7.0 %terms.1 = (f32[128,1024]{1,0:T(8,128)}, f32[128,1024]{1,0:T(8,128)}, bf16[2,128,1024]{2,1,0:T(8,128)(2,1)S(1)}, bf16[2048,128]{1,0:T(8,128)(2,1)}) custom-call(s32[145]{0:T(256)S(1)} %pad_add_fusion.work_ref, s32[24]{0:T(128)S(1)} %compare_select_fusion.7.held_ref, s32[24]{0:T(128)S(1)} %get-tuple-element.19.place_ref, s32[8,512]{1,0:T(8,128)S(1)} %tile.9.first_ref, ...), custom_call_target="tpu_custom_call" | custom-call | tf_op jit(solution)/shard_map/terms/pallas_call | solution.py:41
  39.6 0.0 copy-start.1
  39.6 6.7 %all-to-all-start.1 = ((bf16[8,256,128]{2,1,0:T(8,128)(2,1)}), bf16[8,256,128]{2,1,0:T(8,128)(2,1)S(1)}, u32[]{:S(2)}, u32[]{:S(2)}) async-start(bf16[8,256,128]{2,1,0:T(8,128)(2,1)} %bitcast.7), calls=%async_computation.1 | async-start | bytes 1048576 | tf_op jit(solution)/shard_map/all_to_all | solution.py:299
  46.4 1.9 %collective-permute-start.3 = (bf16[2,128,1024]{2,1,0:T(8,128)(2,1)S(1)}, bf16[2,128,1024]{2,1,0:T(8,128)(2,1)S(1)}, u32[]{:S(2)}, u32[]{:S(2)}) collective-permute-start(bf16[2,128,1024]{2,1,0:T(8,128)(2,1)S(1)} %get-tuple-element.17), channel_id=1, source_target_pairs={{0,8},{8,0},{1,9},{9,1},{2,10},{10,2},{3,11},{11,3},{4,12},{12,4},... | collective-permute-start | bytes 1572872 | tf_op jit(solution)/shard_map/ppermute | solution.py:300
  48.3 1.9 %collective-permute-done.3.side_ref = bf16[2,128,1024]{2,1,0:T(8,128)(2,1)S(1)} collective-permute-done((bf16[2,128,1024]{2,1,0:T(8,128)(2,1)S(1)}, bf16[2,128,1024]{2,1,0:T(8,128)(2,1)S(1)}, u32[]{:S(2)}, u32[]{:S(2)}) %collective-permute-start.3) | collective-permute-done | bytes 524320 | tf_op jit(solution)/shard_map/ppermute | solution.py:300
  50.2 0.0 copy-done.1
  50.2 0.0 copy-start
  50.2 0.1 pass_on.1
  50.2 5.0 %collective-permute-start.4 = (bf16[128,1024]{1,0:T(8,128)(2,1)S(1)}, bf16[128,1024]{1,0:T(8,128)(2,1)S(1)}, u32[]{:S(2)}, u32[]{:S(2)}) collective-permute-start(bf16[128,1024]{1,0:T(8,128)(2,1)S(1)} %pass_on.1), channel_id=1, source_target_pairs={{0,48},{8,56},{16,32},{24,40},{32,16},{40,24},{48,0},{56,8},{1,49}... | collective-permute-start | bytes 786440 | tf_op jit(solution)/shard_map/ppermute | solution.py:302
  55.2 6.5 %collective-permute-done.4.far_ref = bf16[128,1024]{1,0:T(8,128)(2,1)S(1)} collective-permute-done((bf16[128,1024]{1,0:T(8,128)(2,1)S(1)}, bf16[128,1024]{1,0:T(8,128)(2,1)S(1)}, u32[]{:S(2)}, u32[]{:S(2)}) %collective-permute-start.4) | collective-permute-done | bytes 262176 | tf_op jit(solution)/shard_map/ppermute | solution.py:302
  61.7 0.3 all-to-all-done.1.got_ref
  62.0 0.0 copy-done
  62.0 0.8 %finish.1 = (bf16[128,1024]{1,0:T(8,128)(2,1)}, bf16[128,128]{1,0:T(8,128)(2,1)}, bf16[128,128]{1,0:T(8,128)(2,1)}) custom-call(bf16[8,256,128]{2,1,0:T(8,128)(2,1)S(1)} %all-to-all-done.1.got_ref, f32[128,1024]{1,0:T(8,128)S(1)} %copy-done, bf16[2,128,1024]{2,1,0:T(8,128)(2,1)S(1)} %collective-permute-done.3.side_ref, ...), custom_call_target="tpu_custom_call" | custom-call | tf_op jit(solution)/shard_map/finish/pallas_call | solution.py:41
  (9 shorter events, 0.1 us)
Async XLA Ops:
  2.3 29.0 %all-to-all-start = ((bf16[8,256,128]{2,1,0:T(8,128)(2,1)}), bf16[8,256,128]{2,1,0:T(8,128)(2,1)S(1)}, u32[]{:S(2)}, u32[]{:S(2)}) async-start(bf16[8,256,128]{2,1,0:T(8,128)(2,1)} %get-tuple-element.14), calls=%async_computation | async-start | bytes 1048576 | tf_op jit(solution)/shard_map/all_to_all | solution.py:272
  10.9 15.5 %collective-permute-start.1 = (bf16[272,1024]{1,0:T(8,128)(2,1)S(1)}, bf16[272,1024]{1,0:T(8,128)(2,1)S(1)}, u32[]{:S(2)}, u32[]{:S(2)}) collective-permute-start(bf16[272,1024]{1,0:T(8,128)(2,1)S(1)} %get-tuple-element.13.p0_ref), channel_id=1, source_target_pairs={{0,48},{8,56},{16,32},{24,40},{32,16},{40,24},{48,0},{56,8},{1,49}... | collective-permute-start | bytes 1671176 | tf_op jit(solution)/shard_map/ppermute | solution.py:273
  15.6 0.7 %copy-start.2 = (s32[64]{0:T(128)S(1)}, s32[64]{0:T(128)}, u32[]{:S(2)}) copy-start(s32[64]{0:T(128)} %param.15) | copy-start | bytes 772
  16.5 14.7 %collective-permute-start = (bf16[272,1024]{1,0:T(8,128)(2,1)S(1)}, bf16[272,1024]{1,0:T(8,128)(2,1)S(1)}, u32[]{:S(2)}, u32[]{:S(2)}) collective-permute-start(bf16[272,1024]{1,0:T(8,128)(2,1)S(1)} %get-tuple-element.13.p0_ref), channel_id=1, source_target_pairs={{0,8},{8,0},{1,9},{9,1},{2,10},{10,2},{3,11},{11,3},{4,12},{12,4},... | collective-permute-start | bytes 1671176 | tf_op jit(solution)/shard_map/ppermute | solution.py:277
  20.0 0.7 %copy-start.3 = (s32[16]{0:T(128)S(1)}, s32[16]{0:T(128)}, u32[]{:S(2)}) copy-start(s32[16]{0:T(128)} %param.14) | copy-start | bytes 196
  26.4 6.1 %collective-permute-start.2 = (bf16[272,1024]{1,0:T(8,128)(2,1)S(1)}, bf16[272,1024]{1,0:T(8,128)(2,1)S(1)}, u32[]{:S(2)}, u32[]{:S(2)}) collective-permute-start(bf16[272,1024]{1,0:T(8,128)(2,1)S(1)} %collective-permute-done.1.p2_ref), channel_id=1, source_target_pairs={{0,8},{8,0},{1,9},{9,1},{2,10},{10,2},{3,11},{11,3},{4,12},{12,4},... | collective-permute-start | bytes 1671176 | tf_op jit(solution)/shard_map/ppermute | solution.py:274
  39.6 10.5 %copy-start.1 = (f32[128,1024]{1,0:T(8,128)S(1)}, f32[128,1024]{1,0:T(8,128)}, u32[]{:S(2)}) copy-start(f32[128,1024]{1,0:T(8,128)} %get-tuple-element.18.dq_ref) | copy-start | bytes 1572868
  39.6 22.4 %all-to-all-start.1 = ((bf16[8,256,128]{2,1,0:T(8,128)(2,1)}), bf16[8,256,128]{2,1,0:T(8,128)(2,1)S(1)}, u32[]{:S(2)}, u32[]{:S(2)}) async-start(bf16[8,256,128]{2,1,0:T(8,128)(2,1)} %bitcast.7), calls=%async_computation.1 | async-start | bytes 1048576 | tf_op jit(solution)/shard_map/all_to_all | solution.py:299
  46.4 3.8 %collective-permute-start.3 = (bf16[2,128,1024]{2,1,0:T(8,128)(2,1)S(1)}, bf16[2,128,1024]{2,1,0:T(8,128)(2,1)S(1)}, u32[]{:S(2)}, u32[]{:S(2)}) collective-permute-start(bf16[2,128,1024]{2,1,0:T(8,128)(2,1)S(1)} %get-tuple-element.17), channel_id=1, source_target_pairs={{0,8},{8,0},{1,9},{9,1},{2,10},{10,2},{3,11},{11,3},{4,12},{12,4},... | collective-permute-start | bytes 1572872 | tf_op jit(solution)/shard_map/ppermute | solution.py:300
  50.2 11.9 %copy-start = (f32[128,1024]{1,0:T(8,128)S(1)}, f32[128,1024]{1,0:T(8,128)}, u32[]{:S(2)}) copy-start(f32[128,1024]{1,0:T(8,128)} %get-tuple-element.16.own_ref) | copy-start | bytes 1572868
  50.2 11.5 %collective-permute-start.4 = (bf16[128,1024]{1,0:T(8,128)(2,1)S(1)}, bf16[128,1024]{1,0:T(8,128)(2,1)S(1)}, u32[]{:S(2)}, u32[]{:S(2)}) collective-permute-start(bf16[128,1024]{1,0:T(8,128)(2,1)S(1)} %pass_on.1), channel_id=1, source_target_pairs={{0,48},{8,56},{16,32},{24,40},{32,16},{40,24},{48,0},{56,8},{1,49}... | collective-permute-start | bytes 786440 | tf_op jit(solution)/shard_map/ppermute | solution.py:302

commit v11 on v10

--- a/solution.py
+++ b/solution.py
@@ -60,15 +60,15 @@
 
 def pack(
     k_ref, v_ref, q_ref, do_ref, o_ref, norm_ref,
-    kv_ref, out_ref, kv_buf, o_buf, norm_buf, sem, kv_sem,
+    kv_ref, qx_ref, do_out, kv_buf, o_buf, norm_buf, sem, kv_sem,
 ):
     reads = [
         pltpu.make_async_copy(k_ref, kv_buf.at[:ROWS], sem.at[0]),
         pltpu.make_async_copy(v_ref, kv_buf.at[ROWS:], sem.at[1]),
-        pltpu.make_async_copy(do_ref, out_ref.at[ROWS : 2 * ROWS], sem.at[2]),
+        pltpu.make_async_copy(do_ref, do_out, sem.at[2]),
         pltpu.make_async_copy(o_ref, o_buf, sem.at[3]),
         pltpu.make_async_copy(norm_ref, norm_buf, sem.at[4]),
-        pltpu.make_async_copy(q_ref, out_ref.at[:ROWS], sem.at[5]),
+        pltpu.make_async_copy(q_ref, qx_ref.at[:ROWS], sem.at[5]),
     ]
     for copy in reads:
         copy.start()
@@ -83,10 +83,9 @@
     dots = []
     for b in range(2):
         at = slice(b * BLOCK, (b + 1) * BLOCK)
-        at2 = slice(ROWS + b * BLOCK, ROWS + (b + 1) * BLOCK)
         prod = jnp.concatenate(
             [
-                out_ref[at2, head(h)].astype(jnp.float32) * o_buf[at, head(h)].astype(jnp.float32)
+                do_out[at, head(h)].astype(jnp.float32) * o_buf[at, head(h)].astype(jnp.float32)
                 for h in range(HEADS)
             ],
             0,
@@ -101,15 +100,15 @@
     norms = jnp.concatenate(norms + [jnp.zeros((8, WIDTH - 3 * HEAD), jnp.float32)], 1)
     dots = terms_of(jnp.concatenate(dots, 1))
     dots = dots + [jnp.zeros((5, WIDTH), jnp.float32)]
-    out_ref[2 * ROWS :] = jnp.concatenate([norms] + dots, 0).astype(jnp.bfloat16)
+    qx_ref[ROWS:] = jnp.concatenate([norms] + dots, 0).astype(jnp.bfloat16)
     reads[5].wait()
     for copy in writes:
         copy.wait()
 
 
-def stage(p_refs, q_ref, do_ref, norm_ref, dot_ref):
-    for g, p_ref in enumerate(p_refs):
-        more = p_ref[2 * ROWS :, :].astype(jnp.float32)
+def stage(qx_refs, grad_refs, q_ref, do_ref, norm_ref, dot_ref):
+    for g, (qx_ref, grad_ref) in enumerate(zip(qx_refs, grad_refs)):
+        more = qx_ref[ROWS:, :].astype(jnp.float32)
         norm = (more[:8, head(0)] + more[:8, head(1)] + more[:8, head(2)]) * LOG2E
         turned = pltpu.roll(norm, BLOCK, 1)
         left = lax.broadcasted_iota(jnp.int32, (1, HEAD), 1) < BLOCK
@@ -124,18 +123,20 @@
                 )
             for h in range(HEADS):
                 to = slice(b * LANES + h * BLOCK, b * LANES + (h + 1) * BLOCK)
-                q_ref[to, :] = p_ref[i * BLOCK : (i + 1) * BLOCK, head(h)]
-                do_ref[to, :] = p_ref[ROWS + i * BLOCK : ROWS + (i + 1) * BLOCK, head(h)]
+                q_ref[to, :] = qx_ref[i * BLOCK : (i + 1) * BLOCK, head(h)]
+                do_ref[to, :] = grad_ref[i * BLOCK : (i + 1) * BLOCK, head(h)]
 
 
 def terms(
-    work_ref, held_ref, place_ref, first_ref, own_ref, p0_ref, p1_ref, p2_ref, p3_ref, kv_ref,
+    work_ref, held_ref, place_ref, first_ref, own_ref,
+    p0_ref, p1_ref, p2_ref, p3_ref, g0_ref, g1_ref, g2_ref, g3_ref, kv_ref,
     dq0_ref, dq2_ref, side_ref, dkv_ref,
     acc_ref, half_ref, dqt_ref, own_buf, dq2_buf, q_ref, do_ref, norm_ref, dot_ref, sem,
 ):
     acc_ref[...] = jnp.zeros_like(acc_ref)
     dqt_ref[...] = jnp.zeros_like(dqt_ref)
-    stage((p0_ref, p1_ref, p2_ref, p3_ref), q_ref, do_ref, norm_ref, dot_ref)
+    rows = (p0_ref, p1_ref, p2_ref, p3_ref), (g0_ref, g1_ref, g2_ref, g3_ref)
+    stage(*rows, q_ref, do_ref, norm_ref, dot_ref)
 
     def one(t):
         b, j = work_ref[t], work_ref[SLOTS + t]
@@ -255,11 +256,11 @@
     swap = [(0, 1), (1, 0)]
     partner = [3, 2, 1, 0]
     facing = [(2 * i + c, 2 * partner[i] + c) for i in range(4) for c in range(2)]
-    sent, p0 = call(
+    sent, *p0 = call(
         pack,
-        (pltpu.HBM((PEERS, 2 * ROWS, HEAD), bf16), shape((2 * ROWS + EXTRA, WIDTH), bf16)),
+        (pltpu.HBM((PEERS, 2 * ROWS, HEAD), bf16), shape((ROWS + EXTRA, WIDTH), bf16), shape((ROWS, WIDTH), bf16)),
         [HBM] * 6,
-        (HBM, VMEM),
+        (HBM, VMEM, VMEM),
         *map(in_hbm, (keys, values, queries, grad_out, attn_out, log_norm)),
         scratch=[
             pltpu.VMEM((2 * ROWS, HEAD), bf16),
@@ -270,19 +271,20 @@
         ],
     )
     kv = lax.all_to_all(sent, KEEPERS, 0, 0, tiled=True)
-    p2 = lax.ppermute(p0, NEXT, facing)
-    p3 = lax.ppermute(p2, "core", swap)
+    p2 = [lax.ppermute(p, NEXT, facing) for p in p0]
+    p3 = [lax.ppermute(p, "core", swap) for p in p2]
     work, held, at, first, own = plan(doc_lengths, block_order, *place)
     later, held = lax.optimization_barrier((p0, held))
-    p1 = lax.ppermute(later, "core", swap)
+    p1 = [lax.ppermute(p, "core", swap) for p in later]
     nkeys = 2 * PEERS * ROWS
     dq0, dq2, side, dkv = call(
         terms,
         (pltpu.HBM((ROWS, WIDTH), f32),) * 2
         + (shape((2, ROWS, WIDTH), bf16), pltpu.HBM((nkeys, HEAD), bf16)),
-        [SMEM] * 3 + [VMEM] * 7,
+        [SMEM] * 3 + [VMEM] * 11,
         (HBM, HBM, VMEM, HBM),
-        work, held, at, first, own, p0, p1, p2, p3, kv.reshape(nkeys, HEAD),
+        work, held, at, first, own, *[p[i] for i in (0, 1) for p in (p0, p1, p2, p3)],
+        kv.reshape(nkeys, HEAD),
         scratch=[
             pltpu.VMEM((nkeys, HEAD), f32),
             pltpu.VMEM((nkeys, HEAD), bf16),

time: 63.3 us -> 64.9 us (1.025)
  starting transfers between devices: 34.8 us -> 38.3 us
  waiting for transfers between devices: 13.2 us -> 11.1 us
    ppermute x3 -> x6, starting transfers between devices: 12.6 us -> 17 us  [the longest x2 6.55 us: on_device(): p2 = [lax.ppermute(p, NEXT, facing) for p in p0]]
    ppermute x3 -> x6, waiting for transfers between devices: 4.47 us -> 1.46 us  [the longest x2 1.44 us: on_device(): p3 = [lax.ppermute(p, 'core', swap) for p in p2]]
    all_to_all x1, waiting for transfers between devices: 0.29 us -> 1.37 us  [on_device(): lax.all_to_all(dkv.reshape(PEERS, 2 * ROWS, HEAD), KEEPERS, 0, 0, tiled=T...]
    all_to_all x1, starting transfers between devices: 6.73 us -> 5.97 us  [on_device(): lax.all_to_all(dkv.reshape(PEERS, 2 * ROWS, HEAD), KEEPERS, 0, 0, tiled=T...]
  transfers between devices with their start and end apart: 7 -> 10, of which waited for: 5 -> 4; matrix products, arithmetic and copies ran while one was open for 4% -> 4% of each run, Pallas kernels for 0% -> 0%
where the time goes in v11:
time: 64.9 us; the launch traced here: 64.3 us
  starting transfers between devices  38.3 us (59%)
  waiting for transfers between devices  11.1 us (17%)
  Pallas kernels  9.65 us (15%)
  local copies, waits for them, and re-layouts  2.12 us (3%)
  other arithmetic  1.66 us (3%)
  between operations  1.52 us (2%)
    pallas_call x4, Pallas kernels, call(): pl.pallas_call(kernel, out_shape=out, in_specs=ins, out_specs=outs, scrat...  9.65 us
    all_to_all x1, starting transfers between devices, on_device(): kv = lax.all_to_all(sent, KEEPERS, 0, 0, tiled=True)  8.59 us
    ppermute x2, starting transfers between devices, on_device(): p2 = [lax.ppermute(p, NEXT, facing) for p in p0]  6.55 us
    ppermute x1, waiting for transfers between devices, on_device(): far = lax.ppermute(far, NEXT, facing)  6.36 us
    ppermute x2, starting transfers between devices, on_device(): p1 = [lax.ppermute(p, 'core', swap) for p in later]  6.14 us
    all_to_all x1, starting transfers between devices, on_device(): lax.all_to_all(dkv.reshape(PEERS, 2 * ROWS, HEAD), KEEPERS, 0, 0, tiled=T...  5.97 us
    ppermute x1, starting transfers between devices, on_device(): far = lax.ppermute(far, NEXT, facing)  4.84 us
    ppermute x2, starting transfers between devices, on_device(): p3 = [lax.ppermute(p, 'core', swap) for p in p2]  4.32 us
  transfers between devices with their start and end apart: 10, of which 4 were waited for; matrix products, arithmetic and copies ran while one was open for 4% of the time, Pallas kernels for 0%

profile of v11, /device:TPU:1, one launch (start us, length us, event | category | flops | bytes accessed | tf_op | source)
XLA Modules:
  0.0 64.3 jit_solution(2389920497696163152)
XLA Ops:
  0.6 1.7 %pack.1 = (bf16[8,256,128]{2,1,0:T(8,128)(2,1)}, bf16[144,1024]{1,0:T(8,128)(2,1)S(1)}, bf16[128,1024]{1,0:T(8,128)(2,1)S(1)}) custom-call(bf16[128,128]{1,0:T(8,128)(2,1)} %k_ref.1, bf16[128,128]{1,0:T(8,128)(2,1)} %v_ref.1, bf16[128,1024]{1,0:T(8,128)(2,1)} %q_ref.1, bf16[128,1024]{1,0:T(8,128)(2,1)} %do_ref.1, bf16[128,1024]{1,0:T(8,128)(2,1)} %o_ref.1, ...), custom_call_target="tpu_custom_call" | custom-call | tf_op jit(solution)/shard_map/pack/pallas_call | solution.py:41
  2.3 8.6 %all-to-all-start = ((bf16[8,256,128]{2,1,0:T(8,128)(2,1)}), bf16[8,256,128]{2,1,0:T(8,128)(2,1)S(1)}, u32[]{:S(2)}, u32[]{:S(2)}) async-start(bf16[8,256,128]{2,1,0:T(8,128)(2,1)} %get-tuple-element.18), calls=%async_computation | async-start | bytes 1048576 | tf_op jit(solution)/shard_map/all_to_all | solution.py:273
  10.9 4.6 %collective-permute-start.4 = (bf16[128,1024]{1,0:T(8,128)(2,1)S(1)}, bf16[128,1024]{1,0:T(8,128)(2,1)S(1)}, u32[]{:S(2)}, u32[]{:S(2)}) collective-permute-start(bf16[128,1024]{1,0:T(8,128)(2,1)S(1)} %get-tuple-element.17.g0_ref), channel_id=1, source_target_pairs={{0,48},{8,56},{16,32},{24,40},{32,16},{40,24},{48,0},{56,8},{1,49}... | collective-permute-start | bytes 786440 | tf_op jit(solution)/shard_map/ppermute | solution.py:274
  15.5 1.9 %collective-permute-start.1 = (bf16[144,1024]{1,0:T(8,128)(2,1)S(1)}, bf16[144,1024]{1,0:T(8,128)(2,1)S(1)}, u32[]{:S(2)}, u32[]{:S(2)}) collective-permute-start(bf16[144,1024]{1,0:T(8,128)(2,1)S(1)} %get-tuple-element.16.p0_ref), channel_id=1, source_target_pairs={{0,48},{8,56},{16,32},{24,40},{32,16},{40,24},{48,0},{56,8},{1,49}... | collective-permute-start | bytes 884744 | tf_op jit(solution)/shard_map/ppermute | solution.py:274
  17.5 0.0 copy-start.2
  17.5 0.6 copy-done.2
  18.2 0.2 convert_reduce_fusion
  18.3 0.1 select_reduce_fusion.1
  18.5 4.2 %collective-permute-start.3 = (bf16[128,1024]{1,0:T(8,128)(2,1)S(1)}, bf16[128,1024]{1,0:T(8,128)(2,1)S(1)}, u32[]{:S(2)}, u32[]{:S(2)}) collective-permute-start(bf16[128,1024]{1,0:T(8,128)(2,1)S(1)} %get-tuple-element.17.g0_ref), channel_id=1, source_target_pairs={{0,8},{8,0},{1,9},{9,1},{2,10},{10,2},{3,11},{11,3},{4,12},{12,4},... | collective-permute-start | bytes 786440 | tf_op jit(solution)/shard_map/ppermute | solution.py:278
  22.7 1.9 %collective-permute-start = (bf16[144,1024]{1,0:T(8,128)(2,1)S(1)}, bf16[144,1024]{1,0:T(8,128)(2,1)S(1)}, u32[]{:S(2)}, u32[]{:S(2)}) collective-permute-start(bf16[144,1024]{1,0:T(8,128)(2,1)S(1)} %get-tuple-element.16.p0_ref), channel_id=1, source_target_pairs={{0,8},{8,0},{1,9},{9,1},{2,10},{10,2},{3,11},{11,3},{4,12},{12,4},... | collective-permute-start | bytes 884744 | tf_op jit(solution)/shard_map/ppermute | solution.py:278
  24.7 0.0 copy-start.3
  24.7 0.6 %copy-done.3 = s32[16]{0:T(128)S(1)} copy-done((s32[16]{0:T(128)S(1)}, s32[16]{0:T(128)}, u32[]{:S(2)}) %copy-start.3) | copy-done | bytes 88
  25.3 0.1 select_reduce_fusion.3
  25.4 0.1 fusion.10
  25.5 0.1 iota_add_fusion.1
  25.6 0.1 add.170
  25.7 0.2 select_reduce_fusion.6
  25.9 0.1 iota_add_fusion
  25.9 0.1 select_reduce_fusion
  26.0 0.1 shift-right-arithmetic_reduce_fusion
  26.2 0.2 convert_reduce_fusion.2
  26.4 0.1 select_reduce_fusion.5
  26.5 0.6 slice.7
  27.8 0.1 tile.9.first_ref
  27.8 0.1 tile.21.own_ref
  27.9 0.1 convert_reduce_fusion.1
  28.0 0.1 select_reduce_fusion.4
  28.1 0.0 collective-permute-done.4.g2_ref
  28.1 2.4 %collective-permute-start.5 = (bf16[128,1024]{1,0:T(8,128)(2,1)S(1)}, bf16[128,1024]{1,0:T(8,128)(2,1)S(1)}, u32[]{:S(2)}, u32[]{:S(2)}) collective-permute-start(bf16[128,1024]{1,0:T(8,128)(2,1)S(1)} %collective-permute-done.4.g2_ref), channel_id=1, source_target_pairs={{0,8},{8,0},{1,9},{9,1},{2,10},{10,2},{3,11},{11,3},{4,12},{12,4},... | collective-permute-start | bytes 786440 | tf_op jit(solution)/shard_map/ppermute | solution.py:275
  30.5 0.0 collective-permute-done.1.p2_ref
  30.5 1.9 %collective-permute-start.2 = (bf16[144,1024]{1,0:T(8,128)(2,1)S(1)}, bf16[144,1024]{1,0:T(8,128)(2,1)S(1)}, u32[]{:S(2)}, u32[]{:S(2)}) collective-permute-start(bf16[144,1024]{1,0:T(8,128)(2,1)S(1)} %collective-permute-done.1.p2_ref), channel_id=1, source_target_pairs={{0,8},{8,0},{1,9},{9,1},{2,10},{10,2},{3,11},{11,3},{4,12},{12,4},... | collective-permute-start | bytes 884744 | tf_op jit(solution)/shard_map/ppermute | solution.py:275
  32.5 0.1 pad_add_fusion.work_ref
  32.5 0.0 collective-permute-done.3.g1_ref
  32.5 0.0 collective-permute-done.p1_ref
  32.5 0.0 collective-permute-done.5.g3_ref
  32.5 1.4 %collective-permute-done.2.p3_ref = bf16[144,1024]{1,0:T(8,128)(2,1)S(1)} collective-permute-done((bf16[144,1024]{1,0:T(8,128)(2,1)S(1)}, bf16[144,1024]{1,0:T(8,128)(2,1)S(1)}, u32[]{:S(2)}, u32[]{:S(2)}) %collective-permute-start.2) | collective-permute-done | bytes 294944 | tf_op jit(solution)/shard_map/ppermute | solution.py:275
  34.0 0.0 all-to-all-done
  34.0 7.1 %terms.1 = (f32[128,1024]{1,0:T(8,128)}, f32[128,1024]{1,0:T(8,128)}, bf16[2,128,1024]{2,1,0:T(8,128)(2,1)S(1)}, bf16[2048,128]{1,0:T(8,128)(2,1)}) custom-call(s32[145]{0:T(256)S(1)} %pad_add_fusion.work_ref, s32[24]{0:T(128)S(1)} %compare_select_fusion.7.held_ref, s32[24]{0:T(128)S(1)} %get-tuple-element.23.place_ref, s32[8,512]{1,0:T(8,128)S(1)} %tile.9.first_ref, ...), custom_call_target="tpu_custom_call" | custom-call | tf_op jit(solution)/shard_map/terms/pallas_call | solution.py:41
  41.1 0.0 copy-start.1
  41.1 6.0 %all-to-all-start.1 = ((bf16[8,256,128]{2,1,0:T(8,128)(2,1)}), bf16[8,256,128]{2,1,0:T(8,128)(2,1)S(1)}, u32[]{:S(2)}, u32[]{:S(2)}) async-start(bf16[8,256,128]{2,1,0:T(8,128)(2,1)} %bitcast.7), calls=%async_computation.1 | async-start | bytes 1048576 | tf_op jit(solution)/shard_map/all_to_all | solution.py:301
  47.0 1.9 %collective-permute-start.6 = (bf16[2,128,1024]{2,1,0:T(8,128)(2,1)S(1)}, bf16[2,128,1024]{2,1,0:T(8,128)(2,1)S(1)}, u32[]{:S(2)}, u32[]{:S(2)}) collective-permute-start(bf16[2,128,1024]{2,1,0:T(8,128)(2,1)S(1)} %get-tuple-element.21), channel_id=1, source_target_pairs={{0,8},{8,0},{1,9},{9,1},{2,10},{10,2},{3,11},{11,3},{4,12},{12,4},... | collective-permute-start | bytes 1572872 | tf_op jit(solution)/shard_map/ppermute | solution.py:302
  48.9 1.9 %collective-permute-done.6.side_ref = bf16[2,128,1024]{2,1,0:T(8,128)(2,1)S(1)} collective-permute-done((bf16[2,128,1024]{2,1,0:T(8,128)(2,1)S(1)}, bf16[2,128,1024]{2,1,0:T(8,128)(2,1)S(1)}, u32[]{:S(2)}, u32[]{:S(2)}) %collective-permute-start.6) | collective-permute-done | bytes 524320 | tf_op jit(solution)/shard_map/ppermute | solution.py:302
  50.8 0.0 copy-done.1
  50.8 0.0 copy-start
  50.8 0.1 pass_on.1
  50.9 4.8 %collective-permute-start.7 = (bf16[128,1024]{1,0:T(8,128)(2,1)S(1)}, bf16[128,1024]{1,0:T(8,128)(2,1)S(1)}, u32[]{:S(2)}, u32[]{:S(2)}) collective-permute-start(bf16[128,1024]{1,0:T(8,128)(2,1)S(1)} %pass_on.1), channel_id=1, source_target_pairs={{0,48},{8,56},{16,32},{24,40},{32,16},{40,24},{48,0},{56,8},{1,49}... | collective-permute-start | bytes 786440 | tf_op jit(solution)/shard_map/ppermute | solution.py:304
  55.7 6.4 %collective-permute-done.7.far_ref = bf16[128,1024]{1,0:T(8,128)(2,1)S(1)} collective-permute-done((bf16[128,1024]{1,0:T(8,128)(2,1)S(1)}, bf16[128,1024]{1,0:T(8,128)(2,1)S(1)}, u32[]{:S(2)}, u32[]{:S(2)}) %collective-permute-start.7) | collective-permute-done | bytes 262176 | tf_op jit(solution)/shard_map/ppermute | solution.py:304
  62.1 1.4 %all-to-all-done.1.got_ref = bf16[8,256,128]{2,1,0:T(8,128)(2,1)S(1)} async-done(((bf16[8,256,128]{2,1,0:T(8,128)(2,1)}), bf16[8,256,128]{2,1,0:T(8,128)(2,1)S(1)}, u32[]{:S(2)}, u32[]{:S(2)}) %all-to-all-start.1) | async-done | bytes 524320 | tf_op jit(solution)/shard_map/all_to_all | solution.py:301
  63.5 0.0 copy-done
  63.5 0.8 %finish.1 = (bf16[128,1024]{1,0:T(8,128)(2,1)}, bf16[128,128]{1,0:T(8,128)(2,1)}, bf16[128,128]{1,0:T(8,128)(2,1)}) custom-call(bf16[8,256,128]{2,1,0:T(8,128)(2,1)S(1)} %all-to-all-done.1.got_ref, f32[128,1024]{1,0:T(8,128)S(1)} %copy-done, bf16[2,128,1024]{2,1,0:T(8,128)(2,1)S(1)} %collective-permute-done.6.side_ref, ...), custom_call_target="tpu_custom_call" | custom-call | tf_op jit(solution)/shard_map/finish/pallas_call | solution.py:41
  (9 shorter events, 0.1 us)
Async XLA Ops:
  2.3 31.7 %all-to-all-start = ((bf16[8,256,128]{2,1,0:T(8,128)(2,1)}), bf16[8,256,128]{2,1,0:T(8,128)(2,1)S(1)}, u32[]{:S(2)}, u32[]{:S(2)}) async-start(bf16[8,256,128]{2,1,0:T(8,128)(2,1)} %get-tuple-element.18), calls=%async_computation | async-start | bytes 1048576 | tf_op jit(solution)/shard_map/all_to_all | solution.py:273
  10.9 17.2 %collective-permute-start.4 = (bf16[128,1024]{1,0:T(8,128)(2,1)S(1)}, bf16[128,1024]{1,0:T(8,128)(2,1)S(1)}, u32[]{:S(2)}, u32[]{:S(2)}) collective-permute-start(bf16[128,1024]{1,0:T(8,128)(2,1)S(1)} %get-tuple-element.17.g0_ref), channel_id=1, source_target_pairs={{0,48},{8,56},{16,32},{24,40},{32,16},{40,24},{48,0},{56,8},{1,49}... | collective-permute-start | bytes 786440 | tf_op jit(solution)/shard_map/ppermute | solution.py:274
  15.5 15.0 %collective-permute-start.1 = (bf16[144,1024]{1,0:T(8,128)(2,1)S(1)}, bf16[144,1024]{1,0:T(8,128)(2,1)S(1)}, u32[]{:S(2)}, u32[]{:S(2)}) collective-permute-start(bf16[144,1024]{1,0:T(8,128)(2,1)S(1)} %get-tuple-element.16.p0_ref), channel_id=1, source_target_pairs={{0,48},{8,56},{16,32},{24,40},{32,16},{40,24},{48,0},{56,8},{1,49}... | collective-permute-start | bytes 884744 | tf_op jit(solution)/shard_map/ppermute | solution.py:274
  17.5 0.7 %copy-start.2 = (s32[64]{0:T(128)S(1)}, s32[64]{0:T(128)}, u32[]{:S(2)}) copy-start(s32[64]{0:T(128)} %param.15) | copy-start | bytes 772
  18.5 14.1 %collective-permute-start.3 = (bf16[128,1024]{1,0:T(8,128)(2,1)S(1)}, bf16[128,1024]{1,0:T(8,128)(2,1)S(1)}, u32[]{:S(2)}, u32[]{:S(2)}) collective-permute-start(bf16[128,1024]{1,0:T(8,128)(2,1)S(1)} %get-tuple-element.17.g0_ref), channel_id=1, source_target_pairs={{0,8},{8,0},{1,9},{9,1},{2,10},{10,2},{3,11},{11,3},{4,12},{12,4},... | collective-permute-start | bytes 786440 | tf_op jit(solution)/shard_map/ppermute | solution.py:278
  22.7 9.8 %collective-permute-start = (bf16[144,1024]{1,0:T(8,128)(2,1)S(1)}, bf16[144,1024]{1,0:T(8,128)(2,1)S(1)}, u32[]{:S(2)}, u32[]{:S(2)}) collective-permute-start(bf16[144,1024]{1,0:T(8,128)(2,1)S(1)} %get-tuple-element.16.p0_ref), channel_id=1, source_target_pairs={{0,8},{8,0},{1,9},{9,1},{2,10},{10,2},{3,11},{11,3},{4,12},{12,4},... | collective-permute-start | bytes 884744 | tf_op jit(solution)/shard_map/ppermute | solution.py:278
  24.7 0.7 %copy-start.3 = (s32[16]{0:T(128)S(1)}, s32[16]{0:T(128)}, u32[]{:S(2)}) copy-start(s32[16]{0:T(128)} %param.14) | copy-start | bytes 196
  28.1 4.4 %collective-permute-start.5 = (bf16[128,1024]{1,0:T(8,128)(2,1)S(1)}, bf16[128,1024]{1,0:T(8,128)(2,1)S(1)}, u32[]{:S(2)}, u32[]{:S(2)}) collective-permute-start(bf16[128,1024]{1,0:T(8,128)(2,1)S(1)} %collective-permute-done.4.g2_ref), channel_id=1, source_target_pairs={{0,8},{8,0},{1,9},{9,1},{2,10},{10,2},{3,11},{11,3},{4,12},{12,4},... | collective-permute-start | bytes 786440 | tf_op jit(solution)/shard_map/ppermute | solution.py:275
  30.5 3.5 %collective-permute-start.2 = (bf16[144,1024]{1,0:T(8,128)(2,1)S(1)}, bf16[144,1024]{1,0:T(8,128)(2,1)S(1)}, u32[]{:S(2)}, u32[]{:S(2)}) collective-permute-start(bf16[144,1024]{1,0:T(8,128)(2,1)S(1)} %collective-permute-done.1.p2_ref), channel_id=1, source_target_pairs={{0,8},{8,0},{1,9},{9,1},{2,10},{10,2},{3,11},{11,3},{4,12},{12,4},... | collective-permute-start | bytes 884744 | tf_op jit(solution)/shard_map/ppermute | solution.py:275
  41.1 9.8 %copy-start.1 = (f32[128,1024]{1,0:T(8,128)S(1)}, f32[128,1024]{1,0:T(8,128)}, u32[]{:S(2)}) copy-start(f32[128,1024]{1,0:T(8,128)} %get-tuple-element.22.dq_ref) | copy-start | bytes 1572868
  41.1 22.4 %all-to-all-start.1 = ((bf16[8,256,128]{2,1,0:T(8,128)(2,1)}), bf16[8,256,128]{2,1,0:T(8,128)(2,1)S(1)}, u32[]{:S(2)}, u32[]{:S(2)}) async-start(bf16[8,256,128]{2,1,0:T(8,128)(2,1)} %bitcast.7), calls=%async_computation.1 | async-start | bytes 1048576 | tf_op jit(solution)/shard_map/all_to_all | solution.py:301
  47.0 3.8 %collective-permute-start.6 = (bf16[2,128,1024]{2,1,0:T(8,128)(2,1)S(1)}, bf16[2,128,1024]{2,1,0:T(8,128)(2,1)S(1)}, u32[]{:S(2)}, u32[]{:S(2)}) collective-permute-start(bf16[2,128,1024]{2,1,0:T(8,128)(2,1)S(1)} %get-tuple-element.21), channel_id=1, source_target_pairs={{0,8},{8,0},{1,9},{9,1},{2,10},{10,2},{3,11},{11,3},{4,12},{12,4},... | collective-permute-start | bytes 1572872 | tf_op jit(solution)/shard_map/ppermute | solution.py:302
  50.8 12.6 %copy-start = (f32[128,1024]{1,0:T(8,128)S(1)}, f32[128,1024]{1,0:T(8,128)}, u32[]{:S(2)}) copy-start(f32[128,1024]{1,0:T(8,128)} %get-tuple-element.20.own_ref) | copy-start | bytes 1572868
  50.9 11.2 %collective-permute-start.7 = (bf16[128,1024]{1,0:T(8,128)(2,1)S(1)}, bf16[128,1024]{1,0:T(8,128)(2,1)S(1)}, u32[]{:S(2)}, u32[]{:S(2)}) collective-permute-start(bf16[128,1024]{1,0:T(8,128)(2,1)S(1)} %pass_on.1), channel_id=1, source_target_pairs={{0,48},{8,56},{16,32},{24,40},{32,16},{40,24},{48,0},{56,8},{1,49}... | collective-permute-start | bytes 786440 | tf_op jit(solution)/shard_map/ppermute | solution.py:304

commit v12 on v10

--- a/solution.py
+++ b/solution.py
@@ -273,8 +273,7 @@
     p2 = lax.ppermute(p0, NEXT, facing)
     p3 = lax.ppermute(p2, "core", swap)
     work, held, at, first, own = plan(doc_lengths, block_order, *place)
-    later, held = lax.optimization_barrier((p0, held))
-    p1 = lax.ppermute(later, "core", swap)
+    p1 = lax.ppermute(p0, "core", swap)
     nkeys = 2 * PEERS * ROWS
     dq0, dq2, side, dkv = call(
         terms,

time: 63.3 us -> 61.2 us (0.967)
  starting transfers between devices: 34.8 us -> 30.6 us
  waiting for transfers between devices: 13.2 us -> 16.8 us
  Pallas kernels: 9.65 us -> 8.2 us
    all_to_all x1, waiting for transfers between devices: 0.01 us -> 8.43 us  [on_device(): kv = lax.all_to_all(sent, KEEPERS, 0, 0, tiled=True)]
    all_to_all x1, starting transfers between devices: 8.59 us -> 4.21 us  [on_device(): kv = lax.all_to_all(sent, KEEPERS, 0, 0, tiled=True)]
    ppermute x1, waiting for transfers between devices: 3.17 us -> 0.01 us  [on_device(): p2 = lax.ppermute(p0, NEXT, facing)]
    ppermute x1, starting transfers between devices: 4.57 us -> 2.33 us  [on_device(): p3 = lax.ppermute(p2, 'core', swap)]
    ppermute x1, starting transfers between devices: 3.42 us -> 5.49 us  [on_device(): p1 = lax.ppermute(p0, 'core', swap)]
    pallas_call x4, Pallas kernels: 9.65 us -> 8.2 us  [call(): pl.pallas_call(kernel, out_shape=out, in_specs=ins, out_specs=outs, scrat...]
    ppermute x1, waiting for transfers between devices: 1.3 us -> 0.01 us  [on_device(): p3 = lax.ppermute(p2, 'core', swap)]
  transfers between devices with their start and end apart: 7 -> 7, of which waited for: 5 -> 3; matrix products, arithmetic and copies ran while one was open for 4% -> 4% of each run, Pallas kernels for 0% -> 0%
where the time goes in v12:
time: 61.2 us; the launch traced here: 60.7 us
  starting transfers between devices  30.6 us (50%)
  waiting for transfers between devices  16.8 us (27%)
  Pallas kernels  8.2 us (13%)
  local copies, waits for them, and re-layouts  2.03 us (3%)
  other arithmetic  1.66 us (3%)
  between operations  1.43 us (2%)
    all_to_all x1, waiting for transfers between devices, on_device(): kv = lax.all_to_all(sent, KEEPERS, 0, 0, tiled=True)  8.43 us
    pallas_call x4, Pallas kernels, call(): pl.pallas_call(kernel, out_shape=out, in_specs=ins, out_specs=outs, scrat...  8.2 us
    all_to_all x1, starting transfers between devices, on_device(): lax.all_to_all(dkv.reshape(PEERS, 2 * ROWS, HEAD), KEEPERS, 0, 0, tiled=T...  6.93 us
    ppermute x1, waiting for transfers between devices, on_device(): far = lax.ppermute(far, NEXT, facing)  6.44 us
    ppermute x1, starting transfers between devices, on_device(): p1 = lax.ppermute(p0, 'core', swap)  5.49 us
    ppermute x1, starting transfers between devices, on_device(): p2 = lax.ppermute(p0, NEXT, facing)  5.22 us
    ppermute x1, starting transfers between devices, on_device(): far = lax.ppermute(far, NEXT, facing)  4.55 us
    all_to_all x1, starting transfers between devices, on_device(): kv = lax.all_to_all(sent, KEEPERS, 0, 0, tiled=True)  4.21 us
  transfers between devices with their start and end apart: 7, of which 3 were waited for; matrix products, arithmetic and copies ran while one was open for 4% of the time, Pallas kernels for 0%

profile of v12, /device:TPU:1, one launch (start us, length us, event | category | flops | bytes accessed | tf_op | source)
XLA Modules:
  0.0 60.7 jit_solution(13082323409190167463)
XLA Ops:
  0.6 1.7 %pack.1 = (bf16[8,256,128]{2,1,0:T(8,128)(2,1)}, bf16[272,1024]{1,0:T(8,128)(2,1)S(1)}) custom-call(bf16[128,128]{1,0:T(8,128)(2,1)} %k_ref.1, bf16[128,128]{1,0:T(8,128)(2,1)} %v_ref.1, bf16[128,1024]{1,0:T(8,128)(2,1)} %q_ref.1, bf16[128,1024]{1,0:T(8,128)(2,1)} %do_ref.1, bf16[128,1024]{1,0:T(8,128)(2,1)} %o_ref.1, f32[8,128]{1,0:T(8,128)} %norm_ref.1), custom_call_target="tpu_custom_call" | custom-call | tf_op jit(solution)/shard_map/pack/pallas_call | solution.py:41
  2.3 5.2 %collective-permute-start.1 = (bf16[272,1024]{1,0:T(8,128)(2,1)S(1)}, bf16[272,1024]{1,0:T(8,128)(2,1)S(1)}, u32[]{:S(2)}, u32[]{:S(2)}) collective-permute-start(bf16[272,1024]{1,0:T(8,128)(2,1)S(1)} %get-tuple-element.9.p0_ref), channel_id=1, source_target_pairs={{0,48},{8,56},{16,32},{24,40},{32,16},{40,24},{48,0},{56,8},{1,49}... | collective-permute-start | bytes 1671176 | tf_op jit(solution)/shard_map/ppermute | solution.py:273
  7.5 5.5 %collective-permute-start = (bf16[272,1024]{1,0:T(8,128)(2,1)S(1)}, bf16[272,1024]{1,0:T(8,128)(2,1)S(1)}, u32[]{:S(2)}, u32[]{:S(2)}) collective-permute-start(bf16[272,1024]{1,0:T(8,128)(2,1)S(1)} %get-tuple-element.9.p0_ref), channel_id=1, source_target_pairs={{0,8},{8,0},{1,9},{9,1},{2,10},{10,2},{3,11},{11,3},{4,12},{12,4},... | collective-permute-start | bytes 1671176 | tf_op jit(solution)/shard_map/ppermute | solution.py:276
  13.0 4.2 %all-to-all-start = ((bf16[8,256,128]{2,1,0:T(8,128)(2,1)}), bf16[8,256,128]{2,1,0:T(8,128)(2,1)S(1)}, u32[]{:S(2)}, u32[]{:S(2)}) async-start(bf16[8,256,128]{2,1,0:T(8,128)(2,1)} %get-tuple-element.10), calls=%async_computation | async-start | bytes 1048576 | tf_op jit(solution)/shard_map/all_to_all | solution.py:272
  17.3 0.0 copy-start.3
  17.3 0.6 %copy-done.3 = s32[16]{0:T(128)S(1)} copy-done((s32[16]{0:T(128)S(1)}, s32[16]{0:T(128)}, u32[]{:S(2)}) %copy-start.3) | copy-done | bytes 88
  17.9 0.0 copy-start.2
  17.9 0.1 select_reduce_fusion.3
  18.1 0.5 copy-done.2
  18.6 0.2 convert_reduce_fusion
  18.8 0.1 select_reduce_fusion.1
  18.9 0.1 fusion.10
  19.0 0.1 iota_add_fusion.1
  19.1 0.1 add.170
  19.2 0.2 select_reduce_fusion.6
  19.3 0.1 iota_add_fusion
  19.4 0.1 select_reduce_fusion
  19.5 0.1 shift-right-arithmetic_reduce_fusion
  19.6 0.2 convert_reduce_fusion.2
  19.9 0.1 select_reduce_fusion.5
  20.0 0.6 slice.7
  21.2 0.1 tile.9.first_ref
  21.3 0.1 tile.21.own_ref
  21.4 0.0 collective-permute-done.1.p2_ref
  21.4 2.3 %collective-permute-start.2 = (bf16[272,1024]{1,0:T(8,128)(2,1)S(1)}, bf16[272,1024]{1,0:T(8,128)(2,1)S(1)}, u32[]{:S(2)}, u32[]{:S(2)}) collective-permute-start(bf16[272,1024]{1,0:T(8,128)(2,1)S(1)} %collective-permute-done.1.p2_ref), channel_id=1, source_target_pairs={{0,8},{8,0},{1,9},{9,1},{2,10},{10,2},{3,11},{11,3},{4,12},{12,4},... | collective-permute-start | bytes 1671176 | tf_op jit(solution)/shard_map/ppermute | solution.py:274
  23.7 0.1 convert_reduce_fusion.1
  23.8 0.1 select_reduce_fusion.4
  23.9 0.1 pad_add_fusion.work_ref
  24.0 0.0 collective-permute-done.p1_ref
  24.0 8.4 %all-to-all-done = bf16[8,256,128]{2,1,0:T(8,128)(2,1)S(1)} async-done(((bf16[8,256,128]{2,1,0:T(8,128)(2,1)}), bf16[8,256,128]{2,1,0:T(8,128)(2,1)S(1)}, u32[]{:S(2)}, u32[]{:S(2)}) %all-to-all-start) | async-done | bytes 524320 | tf_op jit(solution)/shard_map/all_to_all | solution.py:272
  32.4 0.0 collective-permute-done.2.p3_ref
  32.4 5.6 %terms.1 = (f32[128,1024]{1,0:T(8,128)}, f32[128,1024]{1,0:T(8,128)}, bf16[2,128,1024]{2,1,0:T(8,128)(2,1)S(1)}, bf16[2048,128]{1,0:T(8,128)(2,1)}) custom-call(s32[145]{0:T(256)S(1)} %pad_add_fusion.work_ref, s32[24]{0:T(128)S(1)} %compare_select_fusion.7.held_ref, s32[24]{0:T(128)S(1)} %get-tuple-element.15.place_ref, s32[8,512]{1,0:T(8,128)S(1)} %tile.9.first_ref, ...), custom_call_target="tpu_custom_call" | custom-call | tf_op jit(solution)/shard_map/terms/pallas_call | solution.py:41
  38.1 0.0 copy-start.1
  38.1 6.9 %all-to-all-start.1 = ((bf16[8,256,128]{2,1,0:T(8,128)(2,1)}), bf16[8,256,128]{2,1,0:T(8,128)(2,1)S(1)}, u32[]{:S(2)}, u32[]{:S(2)}) async-start(bf16[8,256,128]{2,1,0:T(8,128)(2,1)} %bitcast.7), calls=%async_computation.1 | async-start | bytes 1048576 | tf_op jit(solution)/shard_map/all_to_all | solution.py:298
  45.0 1.9 %collective-permute-start.3 = (bf16[2,128,1024]{2,1,0:T(8,128)(2,1)S(1)}, bf16[2,128,1024]{2,1,0:T(8,128)(2,1)S(1)}, u32[]{:S(2)}, u32[]{:S(2)}) collective-permute-start(bf16[2,128,1024]{2,1,0:T(8,128)(2,1)S(1)} %get-tuple-element.13), channel_id=1, source_target_pairs={{0,8},{8,0},{1,9},{9,1},{2,10},{10,2},{3,11},{11,3},{4,12},{12,4},... | collective-permute-start | bytes 1572872 | tf_op jit(solution)/shard_map/ppermute | solution.py:299
  46.9 1.9 %collective-permute-done.3.side_ref = bf16[2,128,1024]{2,1,0:T(8,128)(2,1)S(1)} collective-permute-done((bf16[2,128,1024]{2,1,0:T(8,128)(2,1)S(1)}, bf16[2,128,1024]{2,1,0:T(8,128)(2,1)S(1)}, u32[]{:S(2)}, u32[]{:S(2)}) %collective-permute-start.3) | collective-permute-done | bytes 524320 | tf_op jit(solution)/shard_map/ppermute | solution.py:299
  48.8 0.0 copy-done.1
  48.8 0.0 copy-start
  48.8 4.6 %collective-permute-start.4 = (bf16[128,1024]{1,0:T(8,128)(2,1)S(1)}, bf16[128,1024]{1,0:T(8,128)(2,1)S(1)}, u32[]{:S(2)}, u32[]{:S(2)}) collective-permute-start(bf16[128,1024]{1,0:T(8,128)(2,1)S(1)} %pass_on.1), channel_id=1, source_target_pairs={{0,48},{8,56},{16,32},{24,40},{32,16},{40,24},{48,0},{56,8},{1,49}... | collective-permute-start | bytes 786440 | tf_op jit(solution)/shard_map/ppermute | solution.py:301
  53.4 6.4 %collective-permute-done.4.far_ref = bf16[128,1024]{1,0:T(8,128)(2,1)S(1)} collective-permute-done((bf16[128,1024]{1,0:T(8,128)(2,1)S(1)}, bf16[128,1024]{1,0:T(8,128)(2,1)S(1)}, u32[]{:S(2)}, u32[]{:S(2)}) %collective-permute-start.4) | collective-permute-done | bytes 262176 | tf_op jit(solution)/shard_map/ppermute | solution.py:301
  59.8 0.0 all-to-all-done.1.got_ref
  59.9 0.0 copy-done
  59.9 0.9 %finish.1 = (bf16[128,1024]{1,0:T(8,128)(2,1)}, bf16[128,128]{1,0:T(8,128)(2,1)}, bf16[128,128]{1,0:T(8,128)(2,1)}) custom-call(bf16[8,256,128]{2,1,0:T(8,128)(2,1)S(1)} %all-to-all-done.1.got_ref, f32[128,1024]{1,0:T(8,128)S(1)} %copy-done, bf16[2,128,1024]{2,1,0:T(8,128)(2,1)S(1)} %collective-permute-done.3.side_ref, ...), custom_call_target="tpu_custom_call" | custom-call | tf_op jit(solution)/shard_map/finish/pallas_call | solution.py:41
  (10 shorter events, 0.1 us)
Async XLA Ops:
  2.3 19.1 %collective-permute-start.1 = (bf16[272,1024]{1,0:T(8,128)(2,1)S(1)}, bf16[272,1024]{1,0:T(8,128)(2,1)S(1)}, u32[]{:S(2)}, u32[]{:S(2)}) collective-permute-start(bf16[272,1024]{1,0:T(8,128)(2,1)S(1)} %get-tuple-element.9.p0_ref), channel_id=1, source_target_pairs={{0,48},{8,56},{16,32},{24,40},{32,16},{40,24},{48,0},{56,8},{1,49}... | collective-permute-start | bytes 1671176 | tf_op jit(solution)/shard_map/ppermute | solution.py:273
  7.5 16.5 %collective-permute-start = (bf16[272,1024]{1,0:T(8,128)(2,1)S(1)}, bf16[272,1024]{1,0:T(8,128)(2,1)S(1)}, u32[]{:S(2)}, u32[]{:S(2)}) collective-permute-start(bf16[272,1024]{1,0:T(8,128)(2,1)S(1)} %get-tuple-element.9.p0_ref), channel_id=1, source_target_pairs={{0,8},{8,0},{1,9},{9,1},{2,10},{10,2},{3,11},{11,3},{4,12},{12,4},... | collective-permute-start | bytes 1671176 | tf_op jit(solution)/shard_map/ppermute | solution.py:276
  13.0 19.4 %all-to-all-start = ((bf16[8,256,128]{2,1,0:T(8,128)(2,1)}), bf16[8,256,128]{2,1,0:T(8,128)(2,1)S(1)}, u32[]{:S(2)}, u32[]{:S(2)}) async-start(bf16[8,256,128]{2,1,0:T(8,128)(2,1)} %get-tuple-element.10), calls=%async_computation | async-start | bytes 1048576 | tf_op jit(solution)/shard_map/all_to_all | solution.py:272
  17.3 0.7 %copy-start.3 = (s32[16]{0:T(128)S(1)}, s32[16]{0:T(128)}, u32[]{:S(2)}) copy-start(s32[16]{0:T(128)} %param.14) | copy-start | bytes 196
  17.9 0.7 %copy-start.2 = (s32[64]{0:T(128)S(1)}, s32[64]{0:T(128)}, u32[]{:S(2)}) copy-start(s32[64]{0:T(128)} %param.15) | copy-start | bytes 772
  21.4 11.0 %collective-permute-start.2 = (bf16[272,1024]{1,0:T(8,128)(2,1)S(1)}, bf16[272,1024]{1,0:T(8,128)(2,1)S(1)}, u32[]{:S(2)}, u32[]{:S(2)}) collective-permute-start(bf16[272,1024]{1,0:T(8,128)(2,1)S(1)} %collective-permute-done.1.p2_ref), channel_id=1, source_target_pairs={{0,8},{8,0},{1,9},{9,1},{2,10},{10,2},{3,11},{11,3},{4,12},{12,4},... | collective-permute-start | bytes 1671176 | tf_op jit(solution)/shard_map/ppermute | solution.py:274
  38.1 10.7 %copy-start.1 = (f32[128,1024]{1,0:T(8,128)S(1)}, f32[128,1024]{1,0:T(8,128)}, u32[]{:S(2)}) copy-start(f32[128,1024]{1,0:T(8,128)} %get-tuple-element.14.dq_ref) | copy-start | bytes 1572868
  38.1 21.8 %all-to-all-start.1 = ((bf16[8,256,128]{2,1,0:T(8,128)(2,1)}), bf16[8,256,128]{2,1,0:T(8,128)(2,1)S(1)}, u32[]{:S(2)}, u32[]{:S(2)}) async-start(bf16[8,256,128]{2,1,0:T(8,128)(2,1)} %bitcast.7), calls=%async_computation.1 | async-start | bytes 1048576 | tf_op jit(solution)/shard_map/all_to_all | solution.py:298
  45.0 3.8 %collective-permute-start.3 = (bf16[2,128,1024]{2,1,0:T(8,128)(2,1)S(1)}, bf16[2,128,1024]{2,1,0:T(8,128)(2,1)S(1)}, u32[]{:S(2)}, u32[]{:S(2)}) collective-permute-start(bf16[2,128,1024]{2,1,0:T(8,128)(2,1)S(1)} %get-tuple-element.13), channel_id=1, source_target_pairs={{0,8},{8,0},{1,9},{9,1},{2,10},{10,2},{3,11},{11,3},{4,12},{12,4},... | collective-permute-start | bytes 1572872 | tf_op jit(solution)/shard_map/ppermute | solution.py:299
  48.8 11.1 %copy-start = (f32[128,1024]{1,0:T(8,128)S(1)}, f32[128,1024]{1,0:T(8,128)}, u32[]{:S(2)}) copy-start(f32[128,1024]{1,0:T(8,128)} %get-tuple-element.12.own_ref) | copy-start | bytes 1572868
  48.8 11.0 %collective-permute-start.4 = (bf16[128,1024]{1,0:T(8,128)(2,1)S(1)}, bf16[128,1024]{1,0:T(8,128)(2,1)S(1)}, u32[]{:S(2)}, u32[]{:S(2)}) collective-permute-start(bf16[128,1024]{1,0:T(8,128)(2,1)S(1)} %pass_on.1), channel_id=1, source_target_pairs={{0,48},{8,56},{16,32},{24,40},{32,16},{40,24},{48,0},{56,8},{1,49}... | collective-permute-start | bytes 786440 | tf_op jit(solution)/shard_map/ppermute | solution.py:301
